TPU v7x, 32 devices: a whole 2x2x4 slice. The times are simulated.
32 devices in a mesh: seq: 2 (over y), wt: 4 (over x, core), grp: 4 (over z).
Axes of the slice: x: 2, y: 2, z: 4, core: 2. Of those that a mesh axis runs over, the one named last changes fastest.
Arguments:
- tokens: bfloat16 [4, 2048, 2048], P('grp', ('seq', 'wt')), may hold values from -6 to 6
- lengths: int32 [4, 4], P('grp'), may hold values from 1 to 1025, 2048 in all within a row
- order: int32 [4, 2048], P('grp'), may hold values from 0 to 2047, as said below
- mixer_gain: float32 [2048], replicated, may hold values from 0.1 to 1.9
- feed_gain: float32 [2048], replicated, may hold values from 0.1 to 1.9
- in_weight: bfloat16 [2048, 3, 2048], P(('seq', 'grp'), None, 'wt'), may hold values from -0.125 to 0.125
- conv_taps: bfloat16 [3, 2048], P(None, 'wt'), may hold values from -3.5 to 3.5
- out_weight: bfloat16 [2048, 2048], P('wt', ('seq', 'grp')), may hold values from -0.125 to 0.125
- gate_up: bfloat16 [2048, 2, 8192], P(('seq', 'grp'), None, 'wt'), may hold values from -0.125 to 0.125
- down_weight: bfloat16 [8192, 2048], P('wt', ('seq', 'grp')), may hold values from -0.0625 to 0.0625
- cotangent: bfloat16 [4, 2048, 2048], P('grp', ('seq', 'wt')), may hold values from -6 to 6
Outputs:
- block_out: bfloat16 [4, 2048, 2048], P('grp', ('seq', 'wt'))
- tokens_grad: float32 [4, 2048, 2048], P('grp', ('seq', 'wt'))
- mixer_grad: float32 [2048], replicated
- feed_grad: float32 [2048], replicated
- in_grad: float32 [2048, 3, 2048], P(('seq', 'grp'), None, 'wt')
- taps_grad: float32 [3, 2048], P(None, 'wt')
- out_grad: float32 [2048, 2048], P('wt', ('seq', 'grp'))
- gating_grad: float32 [2048, 2, 8192], P(('seq', 'grp'), None, 'wt')
- down_grad: float32 [8192, 2048], P('wt', ('seq', 'grp'))
Inputs may be any that keep to these rules, and one draw needn't show every extreme that they name: The 4 lengths of each sequence sum to 2048, and the longest is exactly 1025. Each row of order is a permutation of the 2048 positions. Split the slots and the positions alike into aligned blocks of 256; every block of slots holds exactly 32 positions of every block of positions.
All inputs are finite; a program needn't handle non-finite values.
Results may differ from a plain program's by a relative error of at most 0.015.
Values may be sent and summed in bfloat16 or wider, within the bound.
No kernel may reach another device: no remote copies, remote signals or barrier semaphores. Data moves between devices by JAX's collectives and lax.ppermute only.
A program may use at most 256 MiB of HBM per device.

v0:
```python
import jax
import jax.numpy as jnp
from jax import lax
from jax.sharding import PartitionSpec as P

epsilon = 1e-05


def passed_along(array, axis, by):
    count = lax.axis_size(axis)
    pairs = [(i, i + by) for i in range(count) if 0 <= i + by < count]
    return lax.ppermute(array, axis, pairs)


def rms_scale(values):
    return lax.rsqrt(jnp.mean(values * values, axis=-1, keepdims=True) + epsilon)


def conv_masks(lengths_row, first, count):
    positions = first + jnp.arange(count, dtype=jnp.int32)
    starts = jnp.cumsum(lengths_row) - lengths_row
    opening = jnp.max(jnp.where(starts[None, :] <= positions[:, None], starts[None, :], 0), axis=1)
    mask_one = (positions - 1 >= opening).astype(jnp.float32)[:, None]
    mask_two = (positions - 2 >= opening).astype(jnp.float32)[:, None]
    return (mask_one, mask_two)


def gather_rows(values):
    return lax.all_gather(values, "wt", axis=0, tiled=True)


def scatter_rows(values):
    return lax.psum_scatter(values, "wt", scatter_dimension=0, tiled=True)


def widen(values):
    return lax.optimization_barrier(values).astype(jnp.float32)


def shards(
    tokens,
    lengths,
    order,
    mixer_gain,
    feed_gain,
    in_weight,
    conv_taps,
    out_weight,
    gate_up,
    down_weight,
    cotangent,
):
    local_rows = tokens.shape[1]
    width = tokens.shape[2]
    peers = lax.axis_size("seq") * lax.axis_size("wt")
    per_peer = local_rows // peers
    block_index = lax.axis_index("seq") * lax.axis_size("wt") + lax.axis_index("wt")
    order_row = order[0]
    here_positions = lax.dynamic_slice_in_dim(order_row, block_index * local_rows, local_rows)
    targets = here_positions // local_rows
    send_index = jnp.argsort(targets, stable=True)
    undo_send = jnp.argsort(send_index)
    sent_tokens = tokens[0][send_index].reshape(peers, per_peer, width)
    sent_cot = cotangent[0][send_index].reshape(peers, per_peer, width)
    got_tokens, got_cot = (
        lax.all_to_all(sent_tokens, ("seq", "wt"), split_axis=0, concat_axis=0, tiled=True),
        lax.all_to_all(sent_cot, ("seq", "wt"), split_axis=0, concat_axis=0, tiled=True),
    )
    mine = order_row // local_rows == block_index
    arrivals = jnp.nonzero(mine, size=local_rows)[0].astype(jnp.int32)
    local_pos = order_row[arrivals] - block_index * local_rows
    placing = jnp.argsort(local_pos)
    home_tokens = got_tokens.reshape(local_rows, width)[placing]
    cot_rows = got_cot.reshape(local_rows, width)[placing]
    token_rows = home_tokens.astype(jnp.float32)
    scale_mix = rms_scale(token_rows)
    normed = (token_rows * scale_mix * mixer_gain).astype(jnp.bfloat16)
    normed_all = gather_rows(normed)
    span_rows = normed_all.shape[0]
    full_in, full_out, full_gate, full_down = (
        lax.all_gather(in_weight, ("seq", "grp"), axis=0, tiled=True),
        lax.all_gather(out_weight, ("seq", "grp"), axis=1, tiled=True),
        lax.all_gather(gate_up, ("seq", "grp"), axis=0, tiled=True),
        lax.all_gather(down_weight, ("seq", "grp"), axis=1, tiled=True),
    )
    projected = jnp.einsum("td,dkc->tkc", normed_all, full_in, preferred_element_type=jnp.float32)
    in_gate = projected[:, 0]
    out_gate = projected[:, 1]
    values = projected[:, 2]
    gated = (in_gate * values).astype(jnp.bfloat16)
    carried = passed_along(gated[-2:], "seq", 1)
    extended = widen(jnp.concatenate([carried, gated], axis=0))
    first = lax.axis_index("seq") * span_rows
    mask_one, mask_two = conv_masks(lengths[0], first, span_rows + 2)
    taps = conv_taps.astype(jnp.float32)
    mixed = (
        taps[2] * extended[2:]
        + mask_one[:span_rows] * taps[1] * extended[1:-1]
        + mask_two[:span_rows] * taps[0] * extended[:-2]
    )
    mixed_out = (out_gate * mixed).astype(jnp.bfloat16)
    branch = scatter_rows(jnp.dot(mixed_out, full_out, preferred_element_type=jnp.float32))
    hidden_state = token_rows + branch
    scale_feed = rms_scale(hidden_state)
    feed_in = (hidden_state * scale_feed * feed_gain).astype(jnp.bfloat16)
    feed_all = gather_rows(feed_in)
    gates = jnp.einsum("td,dkf->tkf", feed_all, full_gate, preferred_element_type=jnp.float32)
    gate_part = gates[:, 0]
    up_part = gates[:, 1]
    sigmoid_gate = jax.nn.sigmoid(gate_part)
    silu_gate = gate_part * sigmoid_gate
    activated = (silu_gate * up_part).astype(jnp.bfloat16)
    feed_out = scatter_rows(jnp.dot(activated, full_down, preferred_element_type=jnp.float32))
    block_home = (hidden_state + feed_out).astype(jnp.bfloat16)
    out_back = lax.all_to_all(
        block_home[local_pos].reshape(peers, per_peer, width),
        ("seq", "wt"),
        split_axis=0,
        concat_axis=0,
        tiled=True,
    )
    block_out = out_back.reshape(local_rows, width)[undo_send][None]
    full_in, full_out, full_gate, full_down = (
        lax.all_gather(in_weight, ("seq", "grp"), axis=0, tiled=True),
        lax.all_gather(out_weight, ("seq", "grp"), axis=1, tiled=True),
        lax.all_gather(gate_up, ("seq", "grp"), axis=0, tiled=True),
        lax.all_gather(down_weight, ("seq", "grp"), axis=1, tiled=True),
    )
    contract_rows = (((0,), (0,)), ((), ()))
    contract_cols = (((1,), (1,)), ((), ()))
    cot_all = gather_rows(cot_rows)
    down_term = lax.dot_general(
        activated, cot_all, contract_rows, preferred_element_type=jnp.float32
    )
    act_grad = lax.dot_general(
        cot_all, full_down, contract_cols, preferred_element_type=jnp.float32
    )
    gate_grad = act_grad * up_part * sigmoid_gate * (1.0 + gate_part * (1.0 - sigmoid_gate))
    up_grad = act_grad * silu_gate
    gates_grad = jnp.stack([gate_grad, up_grad], axis=1).astype(jnp.bfloat16)
    gating_term = jnp.einsum(
        "td,tkf->dkf", feed_all, gates_grad, preferred_element_type=jnp.float32
    )
    feed_norm_grad = scatter_rows(
        jnp.einsum("tkf,dkf->td", gates_grad, full_gate, preferred_element_type=jnp.float32)
    )
    feed_hat = hidden_state * scale_feed
    feed_term = jnp.sum(feed_norm_grad * feed_hat, axis=0)
    feed_scaled = feed_norm_grad * feed_gain
    hidden_grad = cot_rows.astype(jnp.float32) + scale_feed * (
        feed_scaled - feed_hat * jnp.mean(feed_scaled * feed_hat, axis=-1, keepdims=True)
    )
    branch_grad = gather_rows(hidden_grad.astype(jnp.bfloat16))
    out_term = lax.dot_general(
        mixed_out, branch_grad, contract_rows, preferred_element_type=jnp.float32
    )
    mixed_out_grad = lax.dot_general(
        branch_grad, full_out, contract_cols, preferred_element_type=jnp.float32
    )
    out_gate_grad = mixed_out_grad * mixed
    mixed_grad = (mixed_out_grad * out_gate).astype(jnp.bfloat16)
    incoming = passed_along(mixed_grad[:2], "seq", -1)
    grad_ext = widen(jnp.concatenate([mixed_grad, incoming], axis=0))
    mixed_low = grad_ext[:span_rows]
    gated_grad = (
        taps[2] * mixed_low
        + taps[1] * mask_one[1 : span_rows + 1] * grad_ext[1 : span_rows + 1]
        + taps[0] * mask_two[2:] * grad_ext[2:]
    )
    taps_term = jnp.stack(
        [
            jnp.sum(mixed_low * mask_two[:span_rows] * extended[:-2], axis=0),
            jnp.sum(mixed_low * mask_one[:span_rows] * extended[1:-1], axis=0),
            jnp.sum(mixed_low * extended[2:], axis=0),
        ]
    )
    gated_low = widen(gated_grad.astype(jnp.bfloat16))
    projected_grad = jnp.stack(
        [gated_low * values, out_gate_grad, gated_low * in_gate], axis=1
    ).astype(jnp.bfloat16)
    in_term = jnp.einsum(
        "td,tkc->dkc", normed_all, projected_grad, preferred_element_type=jnp.float32
    )
    mix_norm_grad = scatter_rows(
        jnp.einsum("tkc,dkc->td", projected_grad, full_in, preferred_element_type=jnp.float32)
    )
    mix_hat = token_rows * scale_mix
    mixer_term = jnp.sum(mix_norm_grad * mix_hat, axis=0)
    mix_scaled = mix_norm_grad * mixer_gain
    grad_home = hidden_grad + scale_mix * (
        mix_scaled - mix_hat * jnp.mean(mix_scaled * mix_hat, axis=-1, keepdims=True)
    )
    grad_back = lax.all_to_all(
        grad_home[local_pos].reshape(peers, per_peer, width).astype(jnp.bfloat16),
        ("seq", "wt"),
        split_axis=0,
        concat_axis=0,
        tiled=True,
    ).astype(jnp.float32)
    tokens_grad = grad_back.reshape(local_rows, width)[undo_send][None]
    mixer_grad, feed_grad = lax.psum((mixer_term, feed_term), ("seq", "wt", "grp"))
    taps_grad = lax.psum(taps_term, ("seq", "grp"))
    in_grad, out_grad, gating_grad, down_grad = (
        lax.psum_scatter(
            in_term.astype(jnp.bfloat16), ("seq", "grp"), scatter_dimension=0, tiled=True
        ).astype(jnp.float32),
        lax.psum_scatter(
            out_term.astype(jnp.bfloat16), ("seq", "grp"), scatter_dimension=1, tiled=True
        ).astype(jnp.float32),
        lax.psum_scatter(
            gating_term.astype(jnp.bfloat16), ("seq", "grp"), scatter_dimension=0, tiled=True
        ).astype(jnp.float32),
        lax.psum_scatter(
            down_term.astype(jnp.bfloat16), ("seq", "grp"), scatter_dimension=1, tiled=True
        ).astype(jnp.float32),
    )
    return (
        block_out,
        tokens_grad,
        mixer_grad,
        feed_grad,
        in_grad,
        taps_grad,
        out_grad,
        gating_grad,
        down_grad,
    )


def solution(mesh):
    in_specs = (
        P("grp", ("seq", "wt"), None),
        P("grp", None),
        P("grp", None),
        P(),
        P(),
        P(("seq", "grp"), None, "wt"),
        P(None, "wt"),
        P("wt", ("seq", "grp")),
        P(("seq", "grp"), None, "wt"),
        P("wt", ("seq", "grp")),
        P("grp", ("seq", "wt"), None),
    )
    out_specs = (
        P("grp", ("seq", "wt"), None),
        P("grp", ("seq", "wt"), None),
        P(),
        P(),
        P(("seq", "grp"), None, "wt"),
        P(None, "wt"),
        P("wt", ("seq", "grp")),
        P(("seq", "grp"), None, "wt"),
        P("wt", ("seq", "grp")),
    )
    return jax.shard_map(shards, mesh=mesh, in_specs=in_specs, out_specs=out_specs, check_vma=False)
```

profile of v0, /device:TPU:0, one launch (start us, length us, event | category | flops | bytes accessed | tf_op | source)
XLA Modules:
  0.0 1756.2 jit_solution(3104021879700820598)
XLA Ops:
  14.1 5.3 all-to-all-start
  20.1 14.7 scatter_custom_fusion
  47.2 33.8 %all-gather.10.cloned.1.call-done = bf16[1024,2048]{1,0:T(8,128)(2,1)} async-done(((bf16[256,2048]{1,0:T(8,128)(2,1)}), bf16[1024,2048]{1,0:T(8,128)(2,1)}) %all-gather.10.cloned.1.call-update) | async-done | bytes 4194320 | tf_op jit(solution)/shard_map/all_gather | solution.py:29
  81.0 101.2 %all-gather.12.cloned.1.call-done = bf16[2048,3,512]{2,0,1:T(8,128)(2,1)} async-done(((bf16[256,3,512]{2,0,1:T(8,128)(2,1)}), bf16[2048,3,512]{2,0,1:T(8,128)(2,1)}) %all-gather.12.cloned.1.call-update) | async-done | bytes 6291472 | tf_op jit(solution)/shard_map/all_gather | solution.py:81
  182.2 10.2 fusion.8
  200.6 33.0 %all-gather.14.cloned.1.call-done = bf16[512,2048]{1,0:T(8,128)(2,1)} async-done(((bf16[512,256]{1,0:T(8,128)(2,1)}), bf16[512,2048]{1,0:T(8,128)(2,1)}) %all-gather.14.cloned.1.call-update) | async-done | bytes 2097168 | tf_op jit(solution)/shard_map/all_gather | solution.py:82
  233.5 7.2 fusion.50
  244.6 66.2 %reduce-scatter.9.cloned.1.call-done = f32[256,2048]{1,0:T(8,128)} async-done(((f32[1024,2048]{1,0:T(8,128)}), f32[256,2048]{1,0:T(8,128)}) %reduce-scatter.9.cloned.1.call-update) | async-done | bytes 2097168 | tf_op jit(solution)/shard_map/reduce_scatter | solution.py:33
  317.1 22.1 %all_to_all.20 = bf16[8,32,2048]{2,1,0:T(8,128)(2,1)S(1)} all-to-all(bf16[8,32,2048]{2,1,0:T(8,128)(2,1)} %bitcast.126), channel_id=1, replica_groups=mesh['seq'=2,'wt'=4,'grp'=4] {'seq','wt'}, dimensions={0} | all-to-all | bytes 2097152 | tf_op jit(solution)/shard_map/all_to_all | solution.py:67
  342.4 198.8 %all-gather.18.cloned.1.call-done = bf16[2048,2,2048]{2,0,1:T(8,128)(2,1)} async-done(((bf16[256,2,2048]{2,0,1:T(8,128)(2,1)}), bf16[2048,2,2048]{2,0,1:T(8,128)(2,1)}) %all-gather.18.cloned.1.call-update) | async-done | bytes 16777232 | tf_op jit(solution)/shard_map/all_gather | solution.py:83
  541.2 34.8 %all-gather.16.cloned.1.call-done = bf16[1024,2048]{1,0:T(8,128)(2,1)} async-done(((bf16[256,2048]{1,0:T(8,128)(2,1)}), bf16[1024,2048]{1,0:T(8,128)(2,1)}) %all-gather.16.cloned.1.call-update) | async-done | bytes 4194320 | tf_op jit(solution)/shard_map/all_gather | solution.py:29
  576.0 23.5 %fusion.5 = f32[1024,2,2048]{2,0,1:T(8,128)} fusion(bf16[2048,2,2048]{2,0,1:T(8,128)(2,1)} %all-gather.18.cloned.1.call-done, bf16[1024,2048]{1,0:T(8,128)(2,1)} %all-gather.16.cloned.1.call-done), kind=kOutput, calls=%fused_computation.26 | convolution fusion | flops 17179869184 | bytes 37748736 | tf_op jit(solution)/shard_map/td,dkf->tkf/dot_general | solution.py:107
  599.4 12.7 all-gather.24.cloned.1.call-done
  612.1 127.6 %all-gather.20.cloned.1.call-done = bf16[2048,2048]{1,0:T(8,128)(2,1)} async-done(((bf16[2048,256]{1,0:T(8,128)(2,1)}), bf16[2048,2048]{1,0:T(8,128)(2,1)}) %all-gather.20.cloned.1.call-update) | async-done | bytes 8388624 | tf_op jit(solution)/shard_map/all_gather | solution.py:84
  739.7 21.7 %fusion.10 = (bf16[1024,1,2048]{2,0,1:T(8,128)(2,1)}, bf16[1024,1,2048]{2,0,1:T(8,128)(2,1)}, bf16[1024,2048]{1,0:T(8,128)(2,1)}) fusion(f32[1024,2,2048]{2,0,1:T(8,128)} %fusion.5, bf16[1024,2048]{1,0:T(8,128)(2,1)} %all-gather.24.cloned.1.call-done, bf16[2048,2048]{1,0:T(8,128)(2,1)} %all-gather.20.cloned.1.call-done), kind=kOutput, calls=%fused_computation.31 | convolution fusion | flops 8621391872 | bytes 41943040 | tf_op jit(solution)/shard_map/dot_general | solution.py:135
  761.4 24.2 %fusion.2 = f32[1024,2048]{1,0:T(8,128)} fusion(bf16[2048,2,2048]{2,0,1:T(8,128)(2,1)} %all-gather.18.cloned.1.call-done, bf16[1024,1,2048]{2,0,1:T(8,128)(2,1)} %get-tuple-element.56, bf16[1024,1,2048]{2,0,1:T(8,128)(2,1)} %get-tuple-element.55), kind=kOutput, calls=%fused_computation.22 | convolution fusion | flops 17184063488 | bytes 33554432 | tf_op jit(solution)/shard_map/tkf,dkf->td/dot_general | solution.py:145
  786.0 14.4 fusion.51
  800.5 55.3 %reduce-scatter.13.cloned.1.call-done = f32[256,2048]{1,0:T(8,128)} async-done(((f32[1024,2048]{1,0:T(8,128)}), f32[256,2048]{1,0:T(8,128)}) %reduce-scatter.13.cloned.1.call-update) | async-done | bytes 2097168 | tf_op jit(solution)/shard_map/reduce_scatter | solution.py:33
  857.9 72.0 %reduce-scatter.11.cloned.1.call-done = f32[256,2048]{1,0:T(8,128)} async-done(((f32[1024,2048]{1,0:T(8,128)}), f32[256,2048]{1,0:T(8,128)}) %reduce-scatter.11.cloned.1.call-update) | async-done | bytes 2097168 | tf_op jit(solution)/shard_map/reduce_scatter | solution.py:33
  934.3 34.6 %all-gather.22.cloned.1.call-done = bf16[1024,2048]{1,0:T(8,128)(2,1)} async-done(((bf16[256,2048]{1,0:T(8,128)(2,1)}), bf16[1024,2048]{1,0:T(8,128)(2,1)}) %all-gather.22.cloned.1.call-update) | async-done | bytes 4194320 | tf_op jit(solution)/shard_map/all_gather | solution.py:29
  987.6 10.7 convolution_bitcast_fusion
  998.8 14.1 convolution_convert_fusion.1
  1014.2 5.9 convolution_convert_fusion.3
  1020.4 25.2 %convolution_convert_fusion = bf16[2048,2,2048]{2,0,1:T(8,128)(2,1)} fusion(bf16[1024,1,2048]{2,0,1:T(8,128)(2,1)} %get-tuple-element.56, bf16[1024,1,2048]{2,0,1:T(8,128)(2,1)} %get-tuple-element.55, bf16[1024,2048]{1,0:T(8,128)(2,1)} %all-gather.16.cloned.1.call-done), kind=kOutput, calls=%fused_computation.10 | convolution fusion | flops 17205035008 | bytes 29360128 | tf_op jit(solution)/shard_map/td,tkf->dkf/dot_general | solution.py:141
  1046.7 11.2 convolution_convert_fusion.2
  1087.5 137.8 %reduce-scatter.23.cloned.1.call-done = bf16[2048,256]{1,0:T(8,128)(2,1)} async-done(((bf16[2048,2048]{1,0:T(8,128)(2,1)}), bf16[2048,256]{1,0:T(8,128)(2,1)}) %reduce-scatter.23.cloned.1.call-update) | async-done | bytes 1048592 | tf_op jit(solution)/shard_map/reduce_scatter | solution.py:213
  1230.3 20.7 %psum.23 = f32[3,512]{1,0:T(4,128)} all-reduce(f32[3,512]{1,0:T(4,128)S(1)} %pad_maximum_fusion.10), channel_id=1, replica_groups=mesh['seq'=2,'wt'=4,'grp'=4] {'seq','grp'}, use_global_device_ids=true, to_apply=%region_27.28 | all-reduce | flops 1536 | bytes 12288 | tf_op jit(solution)/shard_map/psum | solution.py:202
  1251.0 46.2 %reduce-scatter.19.cloned.1.call-done = bf16[512,256]{1,0:T(8,128)(2,1)} async-done(((bf16[512,2048]{1,0:T(8,128)(2,1)}), bf16[512,256]{1,0:T(8,128)(2,1)}) %reduce-scatter.19.cloned.1.call-update) | async-done | bytes 262160 | tf_op jit(solution)/shard_map/reduce_scatter | solution.py:207
  1299.0 283.4 %reduce-scatter.21.cloned.1.call-done = bf16[256,2,2048]{2,0,1:T(8,128)(2,1)} async-done(((bf16[2048,2,2048]{2,0,1:T(8,128)(2,1)}), bf16[256,2,2048]{2,0,1:T(8,128)(2,1)}) %reduce-scatter.21.cloned.1.call-update) | async-done | bytes 2097168 | tf_op jit(solution)/shard_map/reduce_scatter | solution.py:210
  1582.4 5.8 copy.31
  1588.3 115.0 %reduce-scatter.17.cloned.1.call-done = bf16[256,3,512]{2,0,1:T(8,128)(2,1)} async-done(((bf16[2048,3,512]{2,0,1:T(8,128)(2,1)}), bf16[256,3,512]{2,0,1:T(8,128)(2,1)}) %reduce-scatter.17.cloned.1.call-update) | async-done | bytes 786448 | tf_op jit(solution)/shard_map/reduce_scatter | solution.py:204
  1705.8 39.5 %all-reduce = (f32[2048]{0:T(1024)}, f32[2048]{0:T(1024)}) all-reduce(f32[2048]{0:T(1024)S(1)} %get-tuple-element.47, f32[2048]{0:T(1024)S(1)} %get-tuple-element.45), channel_id=1, replica_groups=mesh['seq'=2,'wt'=4,'grp'=4] {'seq','wt','grp'}, use_global_device_ids=true, to_apply=%region_20.21 | all-reduce | flops 4096 | bytes 32768 | tf_op jit(solution)/shard_map/psum | solution.py:201
  (212 shorter events, 112.5 us)
Async XLA Ops:
  14.1 27.5 %all-to-all-start = ((bf16[8,32,2048]{2,1,0:T(8,128)(2,1)}), bf16[8,32,2048]{2,1,0:T(8,128)(2,1)S(1)}, u32[]{:S(2)}, u32[]{:S(2)}) async-start(bf16[8,32,2048]{2,1,0:T(8,128)(2,1)} %bitcast.2), calls=%async_computation | async-start | bytes 2097152 | tf_op jit(solution)/shard_map/all_to_all | solution.py:66
  19.4 61.6 %all-gather.10.cloned.1.call-start = ((), (), s32[]{:S(2)}) async-start(), calls=%async_computation.12 | async-start | bytes 5242880 | tf_op jit(solution)/shard_map/all_gather | solution.py:29
  44.6 137.5 %all-gather.12.cloned.1.call-start = ((), (), s32[]{:S(2)}) async-start(), calls=%async_computation.13 | async-start | bytes 7077888 | tf_op jit(solution)/shard_map/all_gather | solution.py:81
  45.4 188.1 %all-gather.14.cloned.1.call-start = ((), (), s32[]{:S(2)}) async-start(), calls=%async_computation.14 | async-start | bytes 2359296 | tf_op jit(solution)/shard_map/all_gather | solution.py:82
  46.1 264.6 %reduce-scatter.9.cloned.1.call-start = ((), (), s32[]{:S(2)}) async-start(), calls=%async_computation.15 | async-start | bytes 10485760 | tf_op jit(solution)/shard_map/reduce_scatter | solution.py:33
  47.2 149.9 %copy-start.23 = (f32[1024]{0:T(1024)}, f32[1024]{0:T(1024)S(1)}, u32[]{:S(2)}) copy-start(f32[1024]{0:T(1024)S(1)} %get-tuple-element.66) | copy-start | bytes 12292
  47.2 149.9 %copy-start.25 = (f32[1024]{0:T(1024)}, f32[1024]{0:T(1024)S(1)}, u32[]{:S(2)}) copy-start(f32[1024]{0:T(1024)S(1)} %get-tuple-element.74) | copy-start | bytes 12292
  192.8 3.8 collective-permute-start
  200.6 40.1 %copy-start.15 = (bf16[1024,512]{1,0:T(8,128)(2,1)}, bf16[1024,512]{1,0:T(8,128)(2,1)S(1)}, u32[]{:S(2)}) copy-start(bf16[1024,512]{1,0:T(8,128)(2,1)S(1)} %get-tuple-element.53) | copy-start | bytes 3145732
  240.7 300.5 %all-gather.18.cloned.1.call-start = ((), (), s32[]{:S(2)}) async-start(), calls=%async_computation.17 | async-start | bytes 18874368 | tf_op jit(solution)/shard_map/all_gather | solution.py:83
  244.5 66.3 %copy-start.9 = (bf16[256,2048]{1,0:T(8,128)(2,1)S(1)}, bf16[256,2048]{1,0:T(8,128)(2,1)}, u32[]{:S(2)}) copy-start(bf16[256,2048]{1,0:T(8,128)(2,1)} %copy-done.8) | copy-start | bytes 3145732
  244.5 68.2 %copy-start.20 = (f32[2048]{0:T(1024)S(1)}, f32[2048]{0:T(1024)}, u32[]{:S(2)}) copy-start(f32[2048]{0:T(1024)} %param.15) | copy-start | bytes 24580
  244.5 331.4 %all-gather.16.cloned.1.call-start = ((), (), s32[]{:S(2)}) async-start(), calls=%async_computation.16 | async-start | bytes 5242880 | tf_op jit(solution)/shard_map/all_gather | solution.py:29
  312.7 617.2 %copy-start.6 = (f32[256,2048]{1,0:T(8,128)}, f32[256,2048]{1,0:T(8,128)S(1)}, u32[]{:S(2)}) copy-start(f32[256,2048]{1,0:T(8,128)S(1)} %get-tuple-element.52) | copy-start | bytes 6291460
  314.0 298.1 %all-gather.24.cloned.1.call-start = ((), (), s32[]{:S(2)}) async-start(), calls=%async_computation.27 | async-start | bytes 5242880 | tf_op jit(solution)/shard_map/all_gather | solution.py:29
  341.6 398.2 %all-gather.20.cloned.1.call-start = ((), (), s32[]{:S(2)}) async-start(), calls=%async_computation.18 | async-start | bytes 9437184 | tf_op jit(solution)/shard_map/all_gather | solution.py:84
  342.3 513.5 %reduce-scatter.13.cloned.1.call-start = ((), (), s32[]{:S(2)}) async-start(), calls=%async_computation.20 | async-start | bytes 10485760 | tf_op jit(solution)/shard_map/reduce_scatter | solution.py:33
  785.7 144.2 %reduce-scatter.11.cloned.1.call-start = ((), (), s32[]{:S(2)}) async-start(), calls=%async_computation.19 | async-start | bytes 10485760 | tf_op jit(solution)/shard_map/reduce_scatter | solution.py:33
  800.4 168.4 %all-gather.22.cloned.1.call-start = ((), (), s32[]{:S(2)}) async-start(), calls=%async_computation.21 | async-start | bytes 5242880 | tf_op jit(solution)/shard_map/all_gather | solution.py:29
  934.2 39.9 %copy-start.13 = (f32[1024,512]{1,0:T(8,128)S(1)}, f32[1024,512]{1,0:T(8,128)}, u32[]{:S(2)}) copy-start(f32[1024,512]{1,0:T(8,128)} %get-tuple-element.54) | copy-start | bytes 6291460
  934.2 135.2 %reduce-scatter.15.cloned.1.call-start = ((), (), s32[]{:S(2)}) async-start(), calls=%async_computation.22 | async-start | bytes 10485760 | tf_op jit(solution)/shard_map/reduce_scatter | solution.py:33
  974.1 8.6 copy-start.24
  974.1 8.6 copy-start.26
  974.2 11.8 slice-start
  976.8 9.8 copy-start.19
  976.8 5.5 collective-permute-start.1
  998.4 226.9 %reduce-scatter.23.cloned.1.call-start = ((), (), s32[]{:S(2)}) async-start(), calls=%async_computation.26 | async-start | bytes 9437184 | tf_op jit(solution)/shard_map/reduce_scatter | solution.py:213
  1013.0 284.3 %reduce-scatter.19.cloned.1.call-start = ((), (), s32[]{:S(2)}) async-start(), calls=%async_computation.24 | async-start | bytes 2359296 | tf_op jit(solution)/shard_map/reduce_scatter | solution.py:207
  1020.1 562.3 %reduce-scatter.21.cloned.1.call-start = ((), (), s32[]{:S(2)}) async-start(), calls=%async_computation.25 | async-start | bytes 18874368 | tf_op jit(solution)/shard_map/reduce_scatter | solution.py:210
  1045.5 657.8 %reduce-scatter.17.cloned.1.call-start = ((), (), s32[]{:S(2)}) async-start(), calls=%async_computation.23 | async-start | bytes 7077888 | tf_op jit(solution)/shard_map/reduce_scatter | solution.py:204
  1061.0 19.1 %all-to-all-start.1 = ((bf16[8,32,2048]{2,1,0:T(8,128)(2,1)}), bf16[8,32,2048]{2,1,0:T(8,128)(2,1)S(1)}, u32[]{:S(2)}, u32[]{:S(2)}) async-start(bf16[8,32,2048]{2,1,0:T(8,128)(2,1)} %bitcast.24), calls=%async_computation.3 | async-start | bytes 2097152 | tf_op jit(solution)/shard_map/all_to_all | solution.py:115
  1080.1 665.2 %all-to-all-start.3 = ((bf16[8,32,2048]{2,1,0:T(8,128)(2,1)}), bf16[8,32,2048]{2,1,0:T(8,128)(2,1)}, u32[]{:S(2)}, u32[]{:S(2)}) async-start(bf16[8,32,2048]{2,1,0:T(8,128)(2,1)} %bitcast.37), calls=%async_computation.7 | async-start | bytes 2097152 | tf_op jit(solution)/shard_map/all_to_all | solution.py:193
  (34 other events, 132.2 us)
Sparse Core Ops, SparseCore 0:
  44.8 36.1 all-gather.9
  83.1 99.0 all-gather.11
  184.2 49.3 all-gather.13
  240.8 69.8 reduce-scatter.8
  313.5 227.6 all-gather.17
  543.3 32.6 all-gather.15
  577.6 34.4 all-gather.23
  614.3 125.4 all-gather.19
  785.8 69.9 reduce-scatter.12
  858.2 71.6 reduce-scatter.10
  934.3 34.4 all-gather.21
  998.5 70.9 reduce-scatter.14
  1073.1 152.1 reduce-scatter.22
  1229.7 67.4 reduce-scatter.18
  1301.3 281.0 reduce-scatter.20
  1585.9 117.3 reduce-scatter.16
where the time goes:
time: 1770 us; the launch traced here: 1760 us
  waiting for transfers between devices  1370 us (77%)
  matrix products  174 us (10%)
  blocking collectives  82.3 us (5%)
  other arithmetic  60.7 us (3%)
  local copies, waits for them, and re-layouts  38.6 us (2%)
  starting transfers between devices  18.8 us (1%)
    reduce_scatter x1, waiting for transfers between devices, shards(): lax.psum_scatter(gating_term.astype(jnp.bfloat16), ('seq', 'grp'), scatte...  283 us
    all_gather x1, waiting for transfers between devices, shards(): lax.all_gather(gate_up, ('seq', 'grp'), axis=0, tiled=True)  199 us
    reduce_scatter x4, waiting for transfers between devices, scatter_rows(): return lax.psum_scatter(values, 'wt', scatter_dimension=0, tiled=True)  198 us
    reduce_scatter x1, waiting for transfers between devices, shards(): lax.psum_scatter(down_term.astype(jnp.bfloat16), ('seq', 'grp'), scatter_...  138 us
    all_gather x1, waiting for transfers between devices, shards(): lax.all_gather(down_weight, ('seq', 'grp'), axis=1, tiled=True)  128 us
    all_gather x4, waiting for transfers between devices, gather_rows(): return lax.all_gather(values, 'wt', axis=0, tiled=True)  116 us
    reduce_scatter x1, waiting for transfers between devices, shards(): lax.psum_scatter(in_term.astype(jnp.bfloat16), ('seq', 'grp'), scatter_di...  115 us
    all_gather x1, waiting for transfers between devices, shards(): lax.all_gather(in_weight, ('seq', 'grp'), axis=0, tiled=True)  101 us
  transfers between devices with their start and end apart: 21, of which 19 were waited for; matrix products, arithmetic and copies ran while one was open for 10% of the time, Pallas kernels for 0%

commit v1 on v0

v1 whole, which is shorter than its diff:
```python
import jax
import jax.numpy as jnp
from jax import lax
from jax.sharding import PartitionSpec as P

epsilon = 1e-05
bf16 = jnp.bfloat16
f32 = jnp.float32
contract_rows = (((0,), (0,)), ((), ()))
contract_cols = (((1,), (1,)), ((), ()))


def rotated(array, axis, by):
    count = lax.axis_size(axis)
    return lax.ppermute(array, axis, [(i, (i + by) % count) for i in range(count)])


def crossed(array, axis, by):
    count = lax.axis_size(axis)
    return lax.ppermute(array, axis, [(i, i ^ by) for i in range(count)])


def passed_along(array, axis, by):
    count = lax.axis_size(axis)
    pairs = [(i, i + by) for i in range(count) if 0 <= i + by < count]
    return lax.ppermute(array, axis, pairs)


class Chain:
    def __init__(self, depth):
        self.depth = depth
        self.arrived = []

    def send(self, array, move):
        if len(self.arrived) >= self.depth:
            array, _ = lax.optimization_barrier((array, self.arrived[-self.depth]))
        result = move(array)
        self.arrived.append(result)
        return result


def rms_scale(values):
    return lax.rsqrt(jnp.mean(values * values, axis=-1, keepdims=True) + epsilon)


def relative_columns(array, seq_at, grp_at, seq_count, grp_count):
    width = array.shape[1] // (seq_count * grp_count)
    blocks = {
        (a, b): array[:, (a * grp_count + b) * width : (a * grp_count + b + 1) * width]
        for a in range(seq_count)
        for b in range(grp_count)
    }
    blocks = {(a, b): blocks[(-a % seq_count, -b % grp_count)] for a, b in blocks}
    step = 1
    while step < seq_count:
        chosen = (seq_at // step) % 2 == 1
        blocks = {
            (a, b): jnp.where(chosen, blocks[((a - step) % seq_count, b)], blocks[(a, b)])
            for a, b in blocks
        }
        step *= 2
    step = 1
    while step < grp_count:
        chosen = (grp_at // step) % 2 == 1
        blocks = {
            (a, b): jnp.where(chosen, blocks[(a, (b - step) % grp_count)], blocks[(a, b)])
            for a, b in blocks
        }
        step *= 2
    return jnp.concatenate(
        [blocks[(a, b)] for a in range(seq_count) for b in range(grp_count)], axis=1
    )


def gather_rows(values):
    count = lax.axis_size("wt")
    blocks = {0: values}
    step = count // 2
    while step:
        for j in list(blocks):
            blocks[j ^ step] = crossed(blocks[j], "wt", step)
        step //= 2
    return jnp.concatenate([blocks[j] for j in range(count)], axis=0)


def scatter_rows(product):
    count = lax.axis_size("wt")
    blocks = {j: product(j) for j in sorted(range(count), key=lambda j: -(j % 2))}
    step = 1
    while step < count:
        for j in [j for j in blocks if j & step]:
            sent = blocks.pop(j).astype(bf16)
            blocks[j ^ step] = blocks[j ^ step] + crossed(sent, "wt", step).astype(f32)
        step *= 2
    return blocks[0]


def exchange(rows, peers):
    size = rows.shape[0] // peers
    parts = [rows[k * size : (k + 1) * size] for k in range(peers)]
    return jnp.concatenate(
        [parts[0]] + [crossed_both(parts[k], k, peers) for k in range(1, peers)], axis=0
    )


def crossed_both(array, by, peers):
    return lax.ppermute(array, ("seq", "wt"), [(i, i ^ by) for i in range(peers)])


def summed(array, axes):
    for axis in axes:
        step = 1
        while step < lax.axis_size(axis):
            array = array + crossed(array, axis, step)
            step *= 2
    return array


def select_rows(matrix, rows, dims):
    return lax.dot_general(matrix, rows, dims, preferred_element_type=f32).astype(bf16)


def matmul(left, right, dims=(((1,), (0,)), ((), ()))):
    return lax.dot_general(left, right, dims, preferred_element_type=f32)


def shards(
    tokens,
    lengths,
    order,
    mixer_gain,
    feed_gain,
    in_weight,
    conv_taps,
    out_weight,
    gate_up,
    down_weight,
    cotangent,
):
    local_rows = tokens.shape[1]
    seq_count, wt_count, grp_count = (lax.axis_size(a) for a in ("seq", "wt", "grp"))
    seq_at, wt_at, grp_at = (lax.axis_index(a) for a in ("seq", "wt", "grp"))
    peers = seq_count * wt_count
    per_peer = local_rows // peers
    block_index = seq_at * wt_count + wt_at
    places = [(a, b) for a in range(seq_count) for b in range(grp_count)]
    ring = list(range(1, grp_count)) + [0]

    def relative(array):
        return relative_columns(array, seq_at, grp_at, seq_count, grp_count)

    chain_seq, chain_grp = Chain(2), Chain(2)

    def gathered(pieces):
        held = [{(0, 0): piece} for piece in pieces]
        for b in range(grp_count):
            for i in range(len(pieces)):
                if b:
                    held[i][(0, b)] = chain_grp.send(
                        held[i][(0, b - 1)], lambda v: rotated(v, "grp", 1)
                    )
            for i in range(len(pieces)):
                for a in range(1, seq_count):
                    held[i][(a, b)] = chain_seq.send(
                        held[i][(0, b)], lambda v, a=a: rotated(v, "seq", a)
                    )
        return held

    down_half = down_weight.shape[0] // 2
    in_planes = [in_weight[:, k] for k in range(3)]
    in_held = gathered([jnp.stack(in_planes)])[0]
    out_held = gathered([out_weight])[0]
    gate_held = gathered([gate_up[:, k] for k in range(2)])
    down_held = gathered([down_weight[:down_half], down_weight[down_half:]])
    full_in = jnp.concatenate([in_held[p] for p in places], axis=1)
    full_out = jnp.concatenate([out_held[p] for p in places], axis=1)
    full_gate = [jnp.concatenate([h[p] for p in places], axis=0) for h in gate_held]
    full_down = [jnp.concatenate([h[p] for p in places], axis=1) for h in down_held]

    order_row = order[0]
    slot_blocks = order_row.reshape(peers, local_rows)
    here_positions = lax.dynamic_index_in_dim(slot_blocks, block_index, 0, keepdims=False)
    targets = here_positions // local_rows
    slots = jnp.arange(local_rows, dtype=jnp.int32)
    earlier = slots[:, None] < slots[None, :]
    same = (targets[:, None] == targets[None, :]) & earlier
    rank = jnp.sum(same.astype(jnp.int32), axis=0)
    send_place = (targets ^ block_index) * per_peer + rank
    send_matrix = (slots[:, None] == send_place[None, :]).astype(bf16)
    mine = slot_blocks // local_rows == block_index
    mine_rank = matmul(mine.astype(bf16), earlier.astype(bf16)).astype(jnp.int32)
    sources = jnp.arange(peers, dtype=jnp.int32) ^ block_index
    arrival = jnp.where(mine, sources[:, None] * per_peer + mine_rank, -1).reshape(-1)
    home_place = order_row - block_index * local_rows
    home_hot = (home_place[:, None] == slots[None, :]).astype(bf16)
    arrival_hot = (arrival[:, None] == slots[None, :]).astype(bf16)
    home_matrix = matmul(home_hot, arrival_hot, contract_rows).astype(bf16)
    plain = (((1,), (0,)), ((), ()))

    def to_home(rows):
        got = exchange(select_rows(send_matrix, rows, plain), peers)
        return relative(select_rows(home_matrix, got, plain))

    def to_arrival(rows):
        back = exchange(select_rows(home_matrix, relative(rows), contract_rows), peers)
        return select_rows(send_matrix, back, contract_rows)

    token_rows = to_home(tokens[0]).astype(f32)
    cot_rows = to_home(cotangent[0])
    mixer_row = relative(mixer_gain[None])
    feed_row = relative(feed_gain[None])

    scale_mix = rms_scale(token_rows)
    normed_all = gather_rows((token_rows * scale_mix * mixer_row).astype(bf16))
    span_rows = normed_all.shape[0]
    channels = out_weight.shape[0]
    in_gate, out_gate, values = (matmul(normed_all, full_in[k]) for k in range(3))
    gated = (in_gate * values).astype(bf16)

    block_at = [wt_at ^ j for j in range(wt_count)]
    tails = gated.reshape(wt_count, local_rows, channels)[:, -2:]
    carried = passed_along(
        lax.dynamic_index_in_dim(tails, wt_at ^ (wt_count - 1), 0, keepdims=False), "seq", 1
    )
    tails = jnp.concatenate([tails, carried[None]], axis=0)
    before = jnp.stack(
        [
            lax.dynamic_index_in_dim(
                tails, jnp.where(at == 0, wt_count, wt_at ^ (at - 1)), 0, keepdims=False
            )
            for at in block_at
        ]
    )
    extended = jnp.concatenate(
        [before, gated.reshape(wt_count, local_rows, channels)], axis=1
    ).astype(f32)
    positions = (
        (seq_at * wt_count + jnp.stack(block_at))[:, None] * local_rows + slots[None, :]
    )[:, :, None]
    docs = lengths.shape[1]
    starts = [sum([lengths[0, i] for i in range(d)], jnp.int32(0)) for d in range(docs)]

    def mask(at, back):
        opening = jnp.zeros_like(at)
        for start in starts:
            opening = jnp.where(start <= at, jnp.maximum(opening, start), opening)
        return (at - back >= opening).astype(f32)

    mask_one, mask_two = mask(positions, 1), mask(positions, 2)
    taps = conv_taps.astype(f32)
    now, one_back, two_back = extended[:, 2:], extended[:, 1:-1], extended[:, :-2]
    mixed = (taps[2] * now + mask_one * taps[1] * one_back + mask_two * taps[0] * two_back).reshape(
        span_rows, channels
    )
    mixed_out = (out_gate * mixed).astype(bf16)

    def rows_of(array, j):
        return array[j * local_rows : (j + 1) * local_rows]

    branch = scatter_rows(lambda j: matmul(rows_of(mixed_out, j), full_out))
    hidden_state = token_rows + branch
    scale_feed = rms_scale(hidden_state)
    feed_all = gather_rows((hidden_state * scale_feed * feed_row).astype(bf16))
    gate_part, up_part = (matmul(feed_all, full_gate[k]) for k in range(2))
    sigmoid_gate = jax.nn.sigmoid(gate_part)
    silu_gate = gate_part * sigmoid_gate
    activated = (silu_gate * up_part).astype(bf16)
    act_halves = [activated[:, :down_half], activated[:, down_half:]]
    feed_out = scatter_rows(
        lambda j: sum(matmul(rows_of(act_halves[h], j), full_down[h]) for h in range(2))
    )
    block_out = to_arrival((hidden_state + feed_out).astype(bf16))

    def reduced(terms):
        sums = [{} for _ in terms]
        for b in ring:
            for i, term in enumerate(terms):
                got = [
                    chain_seq.send(term((a, b)), lambda v, a=a: rotated(v, "seq", -a))
                    for a in range(1, seq_count)
                ]
                total = term((0, b)).astype(f32)
                for other in got:
                    total = total + other.astype(f32)
                sums[i][b] = total
        results = [s[ring[0]] for s in sums]
        for b in ring[1:]:
            for i in range(len(terms)):
                results[i] = sums[i][b] + chain_grp.send(
                    results[i].astype(bf16), lambda v: rotated(v, "grp", 1)
                ).astype(f32)
        return results

    cot_all = gather_rows(cot_rows)
    width = cot_all.shape[1] // len(places)

    def columns(array, place):
        at = (place[0] * grp_count + place[1]) * width
        return array[:, at : at + width]

    down_grad = jnp.concatenate(
        reduced(
            [
                lambda p, h=h: matmul(act_halves[h], columns(cot_all, p), contract_rows).astype(bf16)
                for h in range(2)
            ]
        ),
        axis=0,
    )
    act_grad = jnp.concatenate(
        [matmul(cot_all, full_down[h], contract_cols) for h in range(2)], axis=1
    )
    gates_grad = [
        (act_grad * up_part * sigmoid_gate * (1.0 + gate_part * (1.0 - sigmoid_gate))).astype(bf16),
        (act_grad * silu_gate).astype(bf16),
    ]
    feed_norm_grad = scatter_rows(
        lambda j: sum(
            matmul(rows_of(gates_grad[k], j), full_gate[k], contract_cols) for k in range(2)
        )
    )
    gating_grad = jnp.stack(
        reduced(
            [
                lambda p, k=k: matmul(columns(feed_all, p), gates_grad[k], contract_rows).astype(bf16)
                for k in range(2)
            ]
        ),
        axis=1,
    )
    feed_hat = hidden_state * scale_feed
    feed_term = jnp.sum(feed_norm_grad * feed_hat, axis=0)
    feed_scaled = feed_norm_grad * feed_row
    hidden_grad = cot_rows.astype(f32) + scale_feed * (
        feed_scaled - feed_hat * jnp.mean(feed_scaled * feed_hat, axis=-1, keepdims=True)
    )
    branch_grad = gather_rows(hidden_grad.astype(bf16))
    [out_grad] = reduced(
        [lambda p: matmul(mixed_out, columns(branch_grad, p), contract_rows).astype(bf16)]
    )
    mixed_out_grad = matmul(branch_grad, full_out, contract_cols)
    out_gate_grad = (mixed_out_grad * mixed).astype(bf16)
    mixed_grad = (mixed_out_grad * out_gate).astype(bf16)
    heads = mixed_grad.reshape(wt_count, local_rows, channels)[:, :2]
    incoming = passed_along(
        lax.dynamic_index_in_dim(heads, wt_at, 0, keepdims=False), "seq", -1
    )
    heads = jnp.concatenate([heads, incoming[None]], axis=0)
    after = jnp.stack(
        [
            lax.dynamic_index_in_dim(
                heads,
                jnp.where(at == wt_count - 1, wt_count, wt_at ^ (at + 1)),
                0,
                keepdims=False,
            )
            for at in block_at
        ]
    )
    grad_ext = jnp.concatenate(
        [mixed_grad.reshape(wt_count, local_rows, channels), after], axis=1
    ).astype(f32)
    mixed_low = grad_ext[:, :-2]
    gated_grad = (
        taps[2] * mixed_low
        + taps[1] * mask(positions + 1, 1) * grad_ext[:, 1:-1]
        + taps[0] * mask(positions + 2, 2) * grad_ext[:, 2:]
    )
    taps_term = jnp.stack(
        [
            jnp.sum(mixed_low * mask_two * two_back, axis=(0, 1)),
            jnp.sum(mixed_low * mask_one * one_back, axis=(0, 1)),
            jnp.sum(mixed_low * now, axis=(0, 1)),
        ]
    )
    gated_low = gated_grad.astype(bf16).astype(f32).reshape(span_rows, channels)
    projected_grad = [
        (gated_low * values).astype(bf16),
        out_gate_grad,
        (gated_low * in_gate).astype(bf16),
    ]
    [in_planes_grad] = reduced(
        [
            lambda p: jnp.stack(
                [matmul(columns(normed_all, p), g, contract_rows).astype(bf16) for g in projected_grad]
            )
        ]
    )
    in_grad = jnp.stack([in_planes_grad[k] for k in range(3)], axis=1)
    mix_norm_grad = scatter_rows(
        lambda j: sum(
            matmul(rows_of(projected_grad[k], j), full_in[k], contract_cols) for k in range(3)
        )
    )
    mix_hat = token_rows * scale_mix
    mixer_term = jnp.sum(mix_norm_grad * mix_hat, axis=0)
    mix_scaled = mix_norm_grad * mixer_row
    grad_home = hidden_grad + scale_mix * (
        mix_scaled - mix_hat * jnp.mean(mix_scaled * mix_hat, axis=-1, keepdims=True)
    )
    tokens_grad = to_arrival(grad_home.astype(bf16)).astype(f32)
    gains = summed(relative(jnp.stack([mixer_term, feed_term])), ("wt", "seq", "grp"))
    taps_grad = summed(taps_term, ("seq", "grp"))
    return (
        block_out[None],
        tokens_grad[None],
        gains[0],
        gains[1],
        in_grad,
        taps_grad,
        out_grad,
        gating_grad,
        down_grad,
    )


def solution(mesh):
    in_specs = (
        P("grp", ("seq", "wt"), None),
        P("grp", None),
        P("grp", None),
        P(),
        P(),
        P(("seq", "grp"), None, "wt"),
        P(None, "wt"),
        P("wt", ("seq", "grp")),
        P(("seq", "grp"), None, "wt"),
        P("wt", ("seq", "grp")),
        P("grp", ("seq", "wt"), None),
    )
    out_specs = (
        P("grp", ("seq", "wt"), None),
        P("grp", ("seq", "wt"), None),
        P(),
        P(),
        P(("seq", "grp"), None, "wt"),
        P(None, "wt"),
        P("wt", ("seq", "grp")),
        P(("seq", "grp"), None, "wt"),
        P("wt", ("seq", "grp")),
    )
    return jax.shard_map(shards, mesh=mesh, in_specs=in_specs, out_specs=out_specs, check_vma=False)
```

time: 1770 us -> 1040 us (0.59)
  waiting for transfers between devices: 1370 us -> 517 us
  starting transfers between devices: 18.8 us -> 134 us
  matrix products: 174 us -> 266 us
  blocking collectives: 82.3 us -> 0 us
    reduce_scatter x8 -> x0, waiting for transfers between devices: 781 us -> none  [the longest x1 283 us: shards(): lax.psum_scatter(gating_term.astype(jnp.bfloat16), ('seq', 'grp'), scatte...]
    all_gather x8 -> x0, waiting for transfers between devices: 576 us -> none  [the longest x1 199 us: shards(): lax.all_gather(gate_up, ('seq', 'grp'), axis=0, tiled=True)]
    ppermute x0 -> x144, waiting for transfers between devices: none -> 505 us  [the longest x84 431 us: rotated(): lax.ppermute(array, axis, [(i, (i + by) % count) for i in range(count)])]
    ppermute x0 -> x144, starting transfers between devices: none -> 131 us  [the longest x84 95.6 us: rotated(): lax.ppermute(array, axis, [(i, (i + by) % count) for i in range(count)])]
    dot_general x12 -> x114, matrix products: 174 us -> 266 us  [the longest x106 260 us: matmul(): return lax.dot_general(left, right, dims, preferred_element_type=f32)]
    psum x2 -> x0, blocking collectives: 60.2 us -> none  [the longest x1 39.5 us: shards(): lax.psum((mixer_term, feed_term), ('seq', 'wt', 'grp'))]
    unnamed x92 -> x358, local copies, waits for them, and re-layouts: 17.1 us -> 42.6 us
    all_to_all x1 -> x0, blocking collectives: 22.1 us -> none  [shards(): lax.all_to_all(sent_cot, ('seq', 'wt'), split_axis=0, concat_axis=0, tile...]
  transfers between devices with their start and end apart: 21 -> 146, of which waited for: 19 -> 67; matrix products, arithmetic and copies ran while one was open for 10% -> 26% of each run, Pallas kernels for 0% -> 0%
where the time goes in v1:
time: 1040 us; the launch traced here: 1030 us
  waiting for transfers between devices  517 us (50%)
  matrix products  266 us (26%)
  starting transfers between devices  134 us (13%)
  local copies, waits for them, and re-layouts  54.9 us (5%)
  other arithmetic  46.7 us (4%)
    ppermute x84, waiting for transfers between devices, rotated(): lax.ppermute(array, axis, [(i, (i + by) % count) for i in range(count)])  431 us
    dot_general x106, matrix products, matmul(): return lax.dot_general(left, right, dims, preferred_element_type=f32)  260 us
    ppermute x84, starting transfers between devices, rotated(): lax.ppermute(array, axis, [(i, (i + by) % count) for i in range(count)])  95.6 us
    ppermute x28, waiting for transfers between devices, crossed_both(): lax.ppermute(array, ('seq', 'wt'), [(i, i ^ by) for i in range(peers)])  46.4 us
    unnamed x358, local copies, waits for them, and re-layouts  42.6 us
    ppermute x32, waiting for transfers between devices, crossed(): return lax.ppermute(array, axis, [(i, i ^ by) for i in range(count)])  27.1 us
  transfers between devices with their start and end apart: 146, of which 67 were waited for; matrix products, arithmetic and copies ran while one was open for 26% of the time, Pallas kernels for 0%

profile of v1, /device:TPU:0, one launch (start us, length us, event | category | flops | bytes accessed | tf_op | source)
XLA Modules:
  0.0 1026.2 jit_solution(2636318946602893409)
XLA Ops:
  71.9 16.7 %collective-permute-done.11 = bf16[3,256,512]{2,1,0:T(8,128)(2,1)S(1)} collective-permute-done((bf16[3,256,512]{2,1,0:T(8,128)(2,1)}, bf16[3,256,512]{2,1,0:T(8,128)(2,1)S(1)}, u32[]{:S(2)}, u32[]{:S(2)}) %collective-permute-start.11) | collective-permute-done | bytes 786464 | tf_op jit(solution)/shard_map/ppermute | solution.py:15
  94.6 16.2 %collective-permute-done.12 = bf16[3,256,512]{2,1,0:T(8,128)(2,1)S(1)} collective-permute-done((bf16[3,256,512]{2,1,0:T(8,128)(2,1)S(1)}, bf16[3,256,512]{2,1,0:T(8,128)(2,1)S(1)}, u32[]{:S(2)}, u32[]{:S(2)}) %collective-permute-start.12) | collective-permute-done | bytes 786464 | tf_op jit(solution)/shard_map/ppermute | solution.py:15
  122.6 10.3 %collective-permute-done.21 = bf16[512,256]{1,0:T(8,128)(2,1)S(1)} collective-permute-done((bf16[512,256]{1,0:T(8,128)(2,1)S(1)}, bf16[512,256]{1,0:T(8,128)(2,1)S(1)}, u32[]{:S(2)}, u32[]{:S(2)}) %collective-permute-start.21) | collective-permute-done | bytes 262176 | tf_op jit(solution)/shard_map/ppermute | solution.py:15
  151.0 12.5 %collective-permute-done.17 = bf16[2,512]{1,0:T(2,128)(2,1)S(1)} collective-permute-done((bf16[2,512]{1,0:T(2,128)(2,1)S(1)}, bf16[2,512]{1,0:T(2,128)(2,1)S(1)}, u32[]{:S(2)}, u32[]{:S(2)}) %collective-permute-start.17) | collective-permute-done | bytes 2080 | tf_op jit(solution)/shard_map/ppermute | solution.py:26
  189.4 17.8 %collective-permute-done.41 = bf16[256,2048]{1,0:T(8,128)(2,1)} collective-permute-done((bf16[256,2048]{1,0:T(8,128)(2,1)}, bf16[256,2048]{1,0:T(8,128)(2,1)}, u32[]{:S(2)}, u32[]{:S(2)}) %collective-permute-start.41) | collective-permute-done | bytes 1048608 | tf_op jit(solution)/shard_map/ppermute | solution.py:15
  224.0 10.8 %collective-permute-done.39 = bf16[256,2048]{1,0:T(8,128)(2,1)S(1)} collective-permute-done((bf16[256,2048]{1,0:T(8,128)(2,1)}, bf16[256,2048]{1,0:T(8,128)(2,1)S(1)}, u32[]{:S(2)}, u32[]{:S(2)}) %collective-permute-start.39) | collective-permute-done | bytes 1048608 | tf_op jit(solution)/shard_map/ppermute | solution.py:15
  237.5 20.0 %collective-permute-done.42 = bf16[256,2048]{1,0:T(8,128)(2,1)S(1)} collective-permute-done((bf16[256,2048]{1,0:T(8,128)(2,1)}, bf16[256,2048]{1,0:T(8,128)(2,1)S(1)}, u32[]{:S(2)}, u32[]{:S(2)}) %collective-permute-start.42) | collective-permute-done | bytes 1048608 | tf_op jit(solution)/shard_map/ppermute | solution.py:15
  267.0 16.8 %collective-permute-done.36 = bf16[256,2048]{1,0:T(8,128)(2,1)S(1)} collective-permute-done((bf16[256,2048]{1,0:T(8,128)(2,1)}, bf16[256,2048]{1,0:T(8,128)(2,1)S(1)}, u32[]{:S(2)}, u32[]{:S(2)}) %collective-permute-start.36) | collective-permute-done | bytes 1048608 | tf_op jit(solution)/shard_map/ppermute | solution.py:15
  296.7 11.1 %collective-permute-done.52 = bf16[1024,256]{1,0:T(8,128)(2,1)S(1)} collective-permute-done((bf16[1024,256]{1,0:T(8,128)(2,1)S(1)}, bf16[1024,256]{1,0:T(8,128)(2,1)S(1)}, u32[]{:S(2)}, u32[]{:S(2)}) %collective-permute-start.52) | collective-permute-done | bytes 524320 | tf_op jit(solution)/shard_map/ppermute | solution.py:15
  310.6 18.2 %collective-permute-done.37 = bf16[256,2048]{1,0:T(8,128)(2,1)S(1)} collective-permute-done((bf16[256,2048]{1,0:T(8,128)(2,1)S(1)}, bf16[256,2048]{1,0:T(8,128)(2,1)S(1)}, u32[]{:S(2)}, u32[]{:S(2)}) %collective-permute-start.37) | collective-permute-done | bytes 1048608 | tf_op jit(solution)/shard_map/ppermute | solution.py:15
  333.7 27.2 %collective-permute-done.48 = bf16[1024,256]{1,0:T(8,128)(2,1)S(1)} collective-permute-done((bf16[1024,256]{1,0:T(8,128)(2,1)S(1)}, bf16[1024,256]{1,0:T(8,128)(2,1)S(1)}, u32[]{:S(2)}, u32[]{:S(2)}) %collective-permute-start.48) | collective-permute-done | bytes 524320 | tf_op jit(solution)/shard_map/ppermute | solution.py:15
  366.6 8.4 collective-permute-done.54
  380.9 9.6 collective-permute-done.55
  392.2 14.1 %fusion.345 = f32[1024,2048]{1,0:T(8,128)} fusion(bf16[2048,2048]{1,0:T(8,128)(2,1)S(1)} %constant_dynamic-update-slice_fusion.56, bf16[256,2048]{1,0:T(8,128)(2,1)S(1)} %collective-permute-done.30, bf16[256,2048]{1,0:T(8,128)(2,1)S(1)} %collective-permute-done.29, bf16[256,2048]{1,0:T(8,128)(2,1)S(1)} %collective-permute-done.28, ...), kind=kOutput, calls=%fused_computation.820 | convolution fusion | flops 8606711808 | bytes 20971520 | tf_op jit(solution)/shard_map/dot_general | solution.py:124
  416.5 7.7 collective-permute-done.51
  424.3 8.4 collective-permute-done.57
  434.3 8.9 fusion.344
  446.0 8.8 fusion.343
  454.7 23.3 %multiply_convert_fusion.1 = (bf16[1024,2048]{1,0:T(8,128)(2,1)}, bf16[1024,2048]{1,0:T(8,128)(2,1)}, bf16[1024,2048]{1,0:T(8,128)(2,1)}) fusion(f32[1024,2048]{1,0:T(8,128)} %fusion.345, f32[1024,1024]{1,0:T(8,128)} %fusion.343, f32[1024,1024]{1,0:T(8,128)} %fusion.344, bf16[2048,2048]{1,0:T(8,128)(2,1)} %constant_dynamic-update-slice_fusion.48, ...), kind=kOutput, calls=%fused_computation.2 | convolution fusion | flops 8640266240 | bytes 41943040 | tf_op jit(solution)/shard_map/dot_general | solution.py:124
  558.1 9.2 collective-permute-done.113
  570.3 8.2 collective-permute-done.101
  592.9 8.0 collective-permute-done.102
  638.5 11.9 %collective-permute-done.81 = bf16[256,2048]{1,0:T(8,128)(2,1)} collective-permute-done((bf16[256,2048]{1,0:T(8,128)(2,1)S(1)}, bf16[256,2048]{1,0:T(8,128)(2,1)}, u32[]{:S(2)}, u32[]{:S(2)}) %collective-permute-start.81) | collective-permute-done | bytes 1048608 | tf_op jit(solution)/shard_map/ppermute | solution.py:20
  671.0 18.9 %collective-permute-done.63 = bf16[32,2048]{1,0:T(8,128)(2,1)S(1)} collective-permute-done((bf16[32,2048]{1,0:T(8,128)(2,1)S(1)}, bf16[32,2048]{1,0:T(8,128)(2,1)S(1)}, u32[]{:S(2)}, u32[]{:S(2)}) %collective-permute-start.63) | collective-permute-done | bytes 131104 | tf_op jit(solution)/shard_map/ppermute | solution.py:107
  706.5 17.4 %collective-permute-done.117 = bf16[256,2048]{1,0:T(8,128)(2,1)S(1)} collective-permute-done((bf16[256,2048]{1,0:T(8,128)(2,1)S(1)}, bf16[256,2048]{1,0:T(8,128)(2,1)S(1)}, u32[]{:S(2)}, u32[]{:S(2)}) %collective-permute-start.117) | collective-permute-done | bytes 1048608 | tf_op jit(solution)/shard_map/ppermute | solution.py:15
  728.8 17.5 %collective-permute-done.105 = bf16[256,2048]{1,0:T(8,128)(2,1)S(1)} collective-permute-done((bf16[256,2048]{1,0:T(8,128)(2,1)S(1)}, bf16[256,2048]{1,0:T(8,128)(2,1)S(1)}, u32[]{:S(2)}, u32[]{:S(2)}) %collective-permute-start.105) | collective-permute-done | bytes 1048608 | tf_op jit(solution)/shard_map/ppermute | solution.py:15
  855.8 12.6 %collective-permute-done.120 = bf16[256,2048]{1,0:T(8,128)(2,1)S(1)} collective-permute-done((bf16[256,2048]{1,0:T(8,128)(2,1)S(1)}, bf16[256,2048]{1,0:T(8,128)(2,1)S(1)}, u32[]{:S(2)}, u32[]{:S(2)}) %collective-permute-start.120) | collective-permute-done | bytes 1048608 | tf_op jit(solution)/shard_map/ppermute | solution.py:15
  868.9 21.2 %collective-permute-done.108 = bf16[256,2048]{1,0:T(8,128)(2,1)S(1)} collective-permute-done((bf16[256,2048]{1,0:T(8,128)(2,1)S(1)}, bf16[256,2048]{1,0:T(8,128)(2,1)S(1)}, u32[]{:S(2)}, u32[]{:S(2)}) %collective-permute-start.108) | collective-permute-done | bytes 1048608 | tf_op jit(solution)/shard_map/ppermute | solution.py:15
  939.7 8.5 collective-permute-done.110
  967.7 8.4 collective-permute-done.139
  976.7 10.3 %collective-permute-done.140 = bf16[512,256]{1,0:T(8,128)(2,1)S(1)} collective-permute-done((bf16[512,256]{1,0:T(8,128)(2,1)S(1)}, bf16[512,256]{1,0:T(8,128)(2,1)S(1)}, u32[]{:S(2)}, u32[]{:S(2)}) %collective-permute-start.140) | collective-permute-done | bytes 262176 | tf_op jit(solution)/shard_map/ppermute | solution.py:15
  989.4 20.7 %collective-permute-done.124 = bf16[3,256,512]{2,1,0:T(8,128)(2,1)S(1)} collective-permute-done((bf16[3,256,512]{2,1,0:T(8,128)(2,1)S(1)}, bf16[3,256,512]{2,1,0:T(8,128)(2,1)S(1)}, u32[]{:S(2)}, u32[]{:S(2)}) %collective-permute-start.124) | collective-permute-done | bytes 786464 | tf_op jit(solution)/shard_map/ppermute | solution.py:15
  (867 shorter events, 579.9 us)
Async XLA Ops:
  3.3 63.9 %collective-permute-start.10 = (bf16[3,256,512]{2,1,0:T(8,128)(2,1)}, bf16[3,256,512]{2,1,0:T(8,128)(2,1)}, u32[]{:S(2)}, u32[]{:S(2)}) collective-permute-start(bf16[3,256,512]{2,1,0:T(8,128)(2,1)} %get-tuple-element.337), channel_id=1, source_target_pairs={{0,1},{1,2},{2,3},{3,0},{4,5},{5,6},{6,7},{7,4},{8,9},{9,10},{10,1... | collective-permute-start | bytes 2359304 | tf_op jit(solution)/shard_map/ppermute | solution.py:15
  6.3 83.0 %collective-permute-start.13 = (bf16[3,256,512]{2,1,0:T(8,128)(2,1)}, bf16[3,256,512]{2,1,0:T(8,128)(2,1)}, u32[]{:S(2)}, u32[]{:S(2)}) collective-permute-start(bf16[3,256,512]{2,1,0:T(8,128)(2,1)} %get-tuple-element.337), channel_id=1, source_target_pairs={{0,16},{16,0},{1,17},{17,1},{2,18},{18,2},{3,19},{19,3},{4,20},{20... | collective-permute-start | bytes 2359304 | tf_op jit(solution)/shard_map/ppermute | solution.py:15
  94.0 46.9 %collective-permute-start.7 = (bf16[256,2048]{1,0:T(8,128)(2,1)S(1)}, bf16[256,2048]{1,0:T(8,128)(2,1)S(1)}, u32[]{:S(2)}, u32[]{:S(2)}) collective-permute-start(bf16[256,2048]{1,0:T(8,128)(2,1)S(1)} %fusion.66), channel_id=1, source_target_pairs={{0,4},{4,0},{8,12},{12,8},{1,5},{5,1},{9,13},{13,9},{2,6},{6,2},{1... | collective-permute-start | bytes 3145736 | tf_op jit(solution)/shard_map/ppermute | solution.py:20
  94.1 48.6 %collective-permute-start.9 = (bf16[256,2048]{1,0:T(8,128)(2,1)S(1)}, bf16[256,2048]{1,0:T(8,128)(2,1)S(1)}, u32[]{:S(2)}, u32[]{:S(2)}) collective-permute-start(bf16[256,2048]{1,0:T(8,128)(2,1)S(1)} %collective-permute-done.8), channel_id=1, source_target_pairs={{0,4},{4,0},{8,12},{12,8},{1,5},{5,1},{9,13},{13,9},{2,6},{6,2},{1... | collective-permute-start | bytes 3145736 | tf_op jit(solution)/shard_map/ppermute | solution.py:20
  134.9 48.1 %collective-permute-start.77 = (bf16[256,2048]{1,0:T(8,128)(2,1)}, bf16[256,2048]{1,0:T(8,128)(2,1)}, u32[]{:S(2)}, u32[]{:S(2)}) collective-permute-start(bf16[256,2048]{1,0:T(8,128)(2,1)} %constant_dynamic-update-slice_fusion.104), channel_id=1, source_target_pairs={{0,8},{4,12},{8,0},{12,4},{1,9},{5,13},{9,1},{13,5},{2,10},{6,14},... | collective-permute-start | bytes 3145736 | tf_op jit(solution)/shard_map/ppermute | solution.py:20
  140.7 44.0 %collective-permute-start.38 = (bf16[256,2048]{1,0:T(8,128)(2,1)}, bf16[256,2048]{1,0:T(8,128)(2,1)}, u32[]{:S(2)}, u32[]{:S(2)}) collective-permute-start(bf16[256,2048]{1,0:T(8,128)(2,1)} %get-tuple-element.109), channel_id=1, source_target_pairs={{0,1},{1,2},{2,3},{3,0},{4,5},{5,6},{6,7},{7,4},{8,9},{9,10},{10,1... | collective-permute-start | bytes 3145736 | tf_op jit(solution)/shard_map/ppermute | solution.py:15
  207.2 52.0 %collective-permute-start.25 = (bf16[256,2048]{1,0:T(8,128)(2,1)S(1)}, bf16[256,2048]{1,0:T(8,128)(2,1)S(1)}, u32[]{:S(2)}, u32[]{:S(2)}) collective-permute-start(bf16[256,2048]{1,0:T(8,128)(2,1)S(1)} %convolution_convert_fusion.1), channel_id=1, source_target_pairs={{0,4},{4,0},{8,12},{12,8},{1,5},{5,1},{9,13},{13,9},{2,6},{6,2},{1... | collective-permute-start | bytes 3145736 | tf_op jit(solution)/shard_map/ppermute | solution.py:20
  211.2 48.4 %collective-permute-start.27 = (bf16[256,2048]{1,0:T(8,128)(2,1)S(1)}, bf16[256,2048]{1,0:T(8,128)(2,1)S(1)}, u32[]{:S(2)}, u32[]{:S(2)}) collective-permute-start(bf16[256,2048]{1,0:T(8,128)(2,1)S(1)} %fusion.22), channel_id=1, source_target_pairs={{0,8},{4,12},{8,0},{12,4},{1,9},{5,13},{9,1},{13,5},{2,10},{6,14},... | collective-permute-start | bytes 3145736 | tf_op jit(solution)/shard_map/ppermute | solution.py:20
  212.4 45.1 %collective-permute-start.42 = (bf16[256,2048]{1,0:T(8,128)(2,1)}, bf16[256,2048]{1,0:T(8,128)(2,1)S(1)}, u32[]{:S(2)}, u32[]{:S(2)}) collective-permute-start(bf16[256,2048]{1,0:T(8,128)(2,1)} %collective-permute-done.38), channel_id=1, source_target_pairs={{0,16},{16,0},{1,17},{17,1},{2,18},{18,2},{3,19},{19,3},{4,20},{20... | collective-permute-start | bytes 3145736 | tf_op jit(solution)/shard_map/ppermute | solution.py:15
  235.8 50.8 %collective-permute-start.40 = (bf16[256,2048]{1,0:T(8,128)(2,1)S(1)}, bf16[256,2048]{1,0:T(8,128)(2,1)S(1)}, u32[]{:S(2)}, u32[]{:S(2)}) collective-permute-start(bf16[256,2048]{1,0:T(8,128)(2,1)S(1)} %collective-permute-done.39), channel_id=1, source_target_pairs={{0,1},{1,2},{2,3},{3,0},{4,5},{5,6},{6,7},{7,4},{8,9},{9,10},{10,1... | collective-permute-start | bytes 3145736 | tf_op jit(solution)/shard_map/ppermute | solution.py:15
  259.2 48.6 %collective-permute-start.43 = (bf16[256,2048]{1,0:T(8,128)(2,1)S(1)}, bf16[256,2048]{1,0:T(8,128)(2,1)S(1)}, u32[]{:S(2)}, u32[]{:S(2)}) collective-permute-start(bf16[256,2048]{1,0:T(8,128)(2,1)S(1)} %collective-permute-done.39), channel_id=1, source_target_pairs={{0,16},{16,0},{1,17},{17,1},{2,18},{18,2},{3,19},{19,3},{4,20},{20... | collective-permute-start | bytes 3145736 | tf_op jit(solution)/shard_map/ppermute | solution.py:15
  261.0 72.0 %collective-permute-start.29 = (bf16[256,2048]{1,0:T(8,128)(2,1)S(1)}, bf16[256,2048]{1,0:T(8,128)(2,1)S(1)}, u32[]{:S(2)}, u32[]{:S(2)}) collective-permute-start(bf16[256,2048]{1,0:T(8,128)(2,1)S(1)} %multiply_convert_fusion.4), channel_id=1, source_target_pairs={{0,8},{4,12},{8,0},{12,4},{1,9},{5,13},{9,1},{13,5},{2,10},{6,14},... | collective-permute-start | bytes 3145736 | tf_op jit(solution)/shard_map/ppermute | solution.py:20
  283.9 44.9 %collective-permute-start.37 = (bf16[256,2048]{1,0:T(8,128)(2,1)S(1)}, bf16[256,2048]{1,0:T(8,128)(2,1)S(1)}, u32[]{:S(2)}, u32[]{:S(2)}) collective-permute-start(bf16[256,2048]{1,0:T(8,128)(2,1)S(1)} %collective-permute-done.33), channel_id=1, source_target_pairs={{0,16},{16,0},{1,17},{17,1},{2,18},{18,2},{3,19},{19,3},{4,20},{20... | collective-permute-start | bytes 3145736 | tf_op jit(solution)/shard_map/ppermute | solution.py:15
  307.8 56.6 %collective-permute-start.44 = (bf16[256,2048]{1,0:T(8,128)(2,1)S(1)}, bf16[256,2048]{1,0:T(8,128)(2,1)S(1)}, u32[]{:S(2)}, u32[]{:S(2)}) collective-permute-start(bf16[256,2048]{1,0:T(8,128)(2,1)S(1)} %collective-permute-done.40), channel_id=1, source_target_pairs={{0,16},{16,0},{1,17},{17,1},{2,18},{18,2},{3,19},{19,3},{4,20},{20... | collective-permute-start | bytes 3145736 | tf_op jit(solution)/shard_map/ppermute | solution.py:15
  333.1 59.1 %collective-permute-start.28 = (bf16[256,2048]{1,0:T(8,128)(2,1)S(1)}, bf16[256,2048]{1,0:T(8,128)(2,1)S(1)}, u32[]{:S(2)}, u32[]{:S(2)}) collective-permute-start(bf16[256,2048]{1,0:T(8,128)(2,1)S(1)} %multiply_convert_fusion.4), channel_id=1, source_target_pairs={{0,4},{4,0},{8,12},{12,8},{1,5},{5,1},{9,13},{13,9},{2,6},{6,2},{1... | collective-permute-start | bytes 3145736 | tf_op jit(solution)/shard_map/ppermute | solution.py:20
  333.1 59.0 %collective-permute-start.30 = (bf16[256,2048]{1,0:T(8,128)(2,1)S(1)}, bf16[256,2048]{1,0:T(8,128)(2,1)S(1)}, u32[]{:S(2)}, u32[]{:S(2)}) collective-permute-start(bf16[256,2048]{1,0:T(8,128)(2,1)S(1)} %collective-permute-done.29), channel_id=1, source_target_pairs={{0,4},{4,0},{8,12},{12,8},{1,5},{5,1},{9,13},{13,9},{2,6},{6,2},{1... | collective-permute-start | bytes 3145736 | tf_op jit(solution)/shard_map/ppermute | solution.py:20
  536.3 44.6 %collective-permute-start.60 = (bf16[256,2048]{1,0:T(8,128)(2,1)S(1)}, bf16[256,2048]{1,0:T(8,128)(2,1)S(1)}, u32[]{:S(2)}, u32[]{:S(2)}) collective-permute-start(bf16[256,2048]{1,0:T(8,128)(2,1)S(1)} %fusion.28), channel_id=1, source_target_pairs={{0,4},{4,0},{8,12},{12,8},{1,5},{5,1},{9,13},{13,9},{2,6},{6,2},{1... | collective-permute-start | bytes 3145736 | tf_op jit(solution)/shard_map/ppermute | solution.py:20
  557.2 46.5 %collective-permute-start.80 = (bf16[256,2048]{1,0:T(8,128)(2,1)S(1)}, bf16[256,2048]{1,0:T(8,128)(2,1)S(1)}, u32[]{:S(2)}, u32[]{:S(2)}) collective-permute-start(bf16[256,2048]{1,0:T(8,128)(2,1)S(1)} %fusion.21), channel_id=1, source_target_pairs={{0,4},{4,0},{8,12},{12,8},{1,5},{5,1},{9,13},{13,9},{2,6},{6,2},{1... | collective-permute-start | bytes 3145736 | tf_op jit(solution)/shard_map/ppermute | solution.py:20
  661.5 87.3 %collective-permute-start.82 = (bf16[256,2048]{1,0:T(8,128)(2,1)S(1)}, bf16[256,2048]{1,0:T(8,128)(2,1)S(1)}, u32[]{:S(2)}, u32[]{:S(2)}) collective-permute-start(bf16[256,2048]{1,0:T(8,128)(2,1)S(1)} %fusion.342), channel_id=1, source_target_pairs={{0,4},{4,0},{8,12},{12,8},{1,5},{5,1},{9,13},{13,9},{2,6},{6,2},{1... | collective-permute-start | bytes 3145736 | tf_op jit(solution)/shard_map/ppermute | solution.py:20
  698.3 48.1 %collective-permute-start.105 = (bf16[256,2048]{1,0:T(8,128)(2,1)S(1)}, bf16[256,2048]{1,0:T(8,128)(2,1)S(1)}, u32[]{:S(2)}, u32[]{:S(2)}) collective-permute-start(bf16[256,2048]{1,0:T(8,128)(2,1)S(1)} %copy-done.126), channel_id=1, source_target_pairs={{0,16},{16,0},{1,17},{17,1},{2,18},{18,2},{3,19},{19,3},{4,20},{20... | collective-permute-start | bytes 3145736 | tf_op jit(solution)/shard_map/ppermute | solution.py:15
  704.8 46.7 %collective-permute-start.84 = (bf16[256,2048]{1,0:T(8,128)(2,1)S(1)}, bf16[256,2048]{1,0:T(8,128)(2,1)S(1)}, u32[]{:S(2)}, u32[]{:S(2)}) collective-permute-start(bf16[256,2048]{1,0:T(8,128)(2,1)S(1)} %collective-permute-done.83), channel_id=1, source_target_pairs={{0,4},{4,0},{8,12},{12,8},{1,5},{5,1},{9,13},{13,9},{2,6},{6,2},{1... | collective-permute-start | bytes 3145736 | tf_op jit(solution)/shard_map/ppermute | solution.py:20
  723.9 56.1 %collective-permute-start.118 = (bf16[256,2048]{1,0:T(8,128)(2,1)}, bf16[256,2048]{1,0:T(8,128)(2,1)}, u32[]{:S(2)}, u32[]{:S(2)}) collective-permute-start(bf16[256,2048]{1,0:T(8,128)(2,1)} %convolution_convert_fusion.11), channel_id=1, source_target_pairs={{0,16},{16,0},{1,17},{17,1},{2,18},{18,2},{3,19},{19,3},{4,20},{20... | collective-permute-start | bytes 3145736 | tf_op jit(solution)/shard_map/ppermute | solution.py:15
  726.4 56.3 %collective-permute-start.128 = (bf16[256,2048]{1,0:T(8,128)(2,1)}, bf16[256,2048]{1,0:T(8,128)(2,1)}, u32[]{:S(2)}, u32[]{:S(2)}) collective-permute-start(bf16[256,2048]{1,0:T(8,128)(2,1)} %fusion.51), channel_id=1, source_target_pairs={{0,1},{1,2},{2,3},{3,0},{4,5},{5,6},{6,7},{7,4},{8,9},{9,10},{10,1... | collective-permute-start | bytes 3145736 | tf_op jit(solution)/shard_map/ppermute | solution.py:15
  746.4 45.0 %collective-permute-start.106 = (bf16[256,2048]{1,0:T(8,128)(2,1)}, bf16[256,2048]{1,0:T(8,128)(2,1)}, u32[]{:S(2)}, u32[]{:S(2)}) collective-permute-start(bf16[256,2048]{1,0:T(8,128)(2,1)} %convolution_convert_fusion.15), channel_id=1, source_target_pairs={{0,16},{16,0},{1,17},{17,1},{2,18},{18,2},{3,19},{19,3},{4,20},{20... | collective-permute-start | bytes 3145736 | tf_op jit(solution)/shard_map/ppermute | solution.py:15
  780.0 60.5 %collective-permute-start.119 = (bf16[256,2048]{1,0:T(8,128)(2,1)}, bf16[256,2048]{1,0:T(8,128)(2,1)}, u32[]{:S(2)}, u32[]{:S(2)}) collective-permute-start(bf16[256,2048]{1,0:T(8,128)(2,1)} %convolution_convert_fusion.12), channel_id=1, source_target_pairs={{0,16},{16,0},{1,17},{17,1},{2,18},{18,2},{3,19},{19,3},{4,20},{20... | collective-permute-start | bytes 3145736 | tf_op jit(solution)/shard_map/ppermute | solution.py:15
  786.7 60.7 %collective-permute-start.129 = (bf16[256,2048]{1,0:T(8,128)(2,1)}, bf16[256,2048]{1,0:T(8,128)(2,1)}, u32[]{:S(2)}, u32[]{:S(2)}) collective-permute-start(bf16[256,2048]{1,0:T(8,128)(2,1)} %fusion.55), channel_id=1, source_target_pairs={{0,1},{1,2},{2,3},{3,0},{4,5},{5,6},{6,7},{7,4},{8,9},{9,10},{10,1... | collective-permute-start | bytes 3145736 | tf_op jit(solution)/shard_map/ppermute | solution.py:15
  791.4 50.9 %collective-permute-start.107 = (bf16[256,2048]{1,0:T(8,128)(2,1)}, bf16[256,2048]{1,0:T(8,128)(2,1)}, u32[]{:S(2)}, u32[]{:S(2)}) collective-permute-start(bf16[256,2048]{1,0:T(8,128)(2,1)} %convolution_convert_fusion.16), channel_id=1, source_target_pairs={{0,16},{16,0},{1,17},{17,1},{2,18},{18,2},{3,19},{19,3},{4,20},{20... | collective-permute-start | bytes 3145736 | tf_op jit(solution)/shard_map/ppermute | solution.py:15
  795.6 47.1 %collective-permute-start.136 = (bf16[256,2048]{1,0:T(8,128)(2,1)}, bf16[256,2048]{1,0:T(8,128)(2,1)}, u32[]{:S(2)}, u32[]{:S(2)}) collective-permute-start(bf16[256,2048]{1,0:T(8,128)(2,1)} %fusion.44), channel_id=1, source_target_pairs={{0,1},{1,2},{2,3},{3,0},{4,5},{5,6},{6,7},{7,4},{8,9},{9,10},{10,1... | collective-permute-start | bytes 3145736 | tf_op jit(solution)/shard_map/ppermute | solution.py:15
  842.7 47.4 %collective-permute-start.108 = (bf16[256,2048]{1,0:T(8,128)(2,1)S(1)}, bf16[256,2048]{1,0:T(8,128)(2,1)S(1)}, u32[]{:S(2)}, u32[]{:S(2)}) collective-permute-start(bf16[256,2048]{1,0:T(8,128)(2,1)S(1)} %copy-done.125), channel_id=1, source_target_pairs={{0,16},{16,0},{1,17},{17,1},{2,18},{18,2},{3,19},{19,3},{4,20},{20... | collective-permute-start | bytes 3145736 | tf_op jit(solution)/shard_map/ppermute | solution.py:15
  852.2 44.4 %collective-permute-start.130 = (bf16[256,2048]{1,0:T(8,128)(2,1)S(1)}, bf16[256,2048]{1,0:T(8,128)(2,1)S(1)}, u32[]{:S(2)}, u32[]{:S(2)}) collective-permute-start(bf16[256,2048]{1,0:T(8,128)(2,1)S(1)} %fusion.59), channel_id=1, source_target_pairs={{0,1},{1,2},{2,3},{3,0},{4,5},{5,6},{6,7},{7,4},{8,9},{9,10},{10,1... | collective-permute-start | bytes 3145736 | tf_op jit(solution)/shard_map/ppermute | solution.py:15
  853.9 49.8 %collective-permute-start.86 = (bf16[256,2048]{1,0:T(8,128)(2,1)}, bf16[256,2048]{1,0:T(8,128)(2,1)}, u32[]{:S(2)}, u32[]{:S(2)}) collective-permute-start(bf16[256,2048]{1,0:T(8,128)(2,1)} %fusion.23), channel_id=1, source_target_pairs={{0,4},{4,0},{8,12},{12,8},{1,5},{5,1},{9,13},{13,9},{2,6},{6,2},{1... | collective-permute-start | bytes 3145736 | tf_op jit(solution)/shard_map/ppermute | solution.py:20
  931.6 55.6 %collective-permute-start.91 = (bf16[32,2048]{1,0:T(8,128)(2,1)S(1)}, bf16[32,2048]{1,0:T(8,128)(2,1)S(1)}, u32[]{:S(2)}, u32[]{:S(2)}) collective-permute-start(bf16[32,2048]{1,0:T(8,128)(2,1)S(1)} %get-tuple-element.302), channel_id=1, source_target_pairs={{0,12},{4,8},{8,4},{12,0},{16,28},{20,24},{24,20},{28,16},{1,13},{... | collective-permute-start | bytes 393224 | tf_op jit(solution)/shard_map/ppermute | solution.py:107
  (260 other events, 4957.6 us)

commit v2 on v1

v2 whole, which is shorter than its diff:
```python
import jax
import jax.numpy as jnp
from jax import lax
from jax.sharding import PartitionSpec as P

epsilon = 1e-05
bf16 = jnp.bfloat16
f32 = jnp.float32
plain = (((1,), (0,)), ((), ()))
contract_rows = (((0,), (0,)), ((), ()))
contract_cols = (((1,), (1,)), ((), ()))


def rotated(array, axis, by):
    count = lax.axis_size(axis)
    return lax.ppermute(array, axis, [(i, (i + by) % count) for i in range(count)])


def crossed(array, axis, by):
    count = lax.axis_size(axis)
    return lax.ppermute(array, axis, [(i, i ^ by) for i in range(count)])


def passed_along(array, axis, by):
    count = lax.axis_size(axis)
    pairs = [(i, i + by) for i in range(count) if 0 <= i + by < count]
    return lax.ppermute(array, axis, pairs)


def after(array, *others):
    return lax.optimization_barrier((array, *others))[0]


class Sequence:
    def __init__(self):
        self.last = ()

    def tie(self, array, *others):
        return after(array, *self.last, *others) if self.last or others else array

    def mark(self, array):
        self.last = (array,)
        return array

    def send(self, array, move, *others):
        return move(self.mark(self.tie(array, *others)))


class Chain:
    def __init__(self, stages, axis, depth):
        self.stages, self.axis, self.depth = stages, axis, depth
        self.arrived = []

    def send(self, array, by):
        behind = self.arrived[-self.depth : len(self.arrived) - self.depth + 1]
        result = self.stages.send(array, lambda v: rotated(v, self.axis, by), *behind)
        self.arrived.append(result)
        return result


def go(steps, count=1):
    for _ in range(count):
        next(steps, None)


def rest(*all_steps):
    for steps in all_steps:
        for _ in steps:
            pass


def rms_scale(values):
    return lax.rsqrt(jnp.mean(values * values, axis=-1, keepdims=True) + epsilon)


def relative_columns(array, seq_at, grp_at, seq_count, grp_count):
    width = array.shape[1] // (seq_count * grp_count)
    blocks = {
        (a, b): array[:, (a * grp_count + b) * width : (a * grp_count + b + 1) * width]
        for a in range(seq_count)
        for b in range(grp_count)
    }
    blocks = {(a, b): blocks[(-a % seq_count, -b % grp_count)] for a, b in blocks}
    step = 1
    while step < seq_count:
        chosen = (seq_at // step) % 2 == 1
        blocks = {
            (a, b): jnp.where(chosen, blocks[((a - step) % seq_count, b)], blocks[(a, b)])
            for a, b in blocks
        }
        step *= 2
    step = 1
    while step < grp_count:
        chosen = (grp_at // step) % 2 == 1
        blocks = {
            (a, b): jnp.where(chosen, blocks[(a, (b - step) % grp_count)], blocks[(a, b)])
            for a, b in blocks
        }
        step *= 2
    return jnp.concatenate(
        [blocks[(a, b)] for a in range(seq_count) for b in range(grp_count)], axis=1
    )


def peer_order(count):
    order, step = [0], count // 2
    while step:
        order = order + [j ^ step for j in order]
        step //= 2
    return order


def summed(array, axes):
    for axis in axes:
        step = 1
        while step < lax.axis_size(axis):
            array = array + crossed(array, axis, step)
            step *= 2
    return array


def select_rows(matrix, rows, dims):
    return lax.dot_general(matrix, rows, dims, preferred_element_type=f32).astype(bf16)


def matmul(left, right, dims=plain):
    return lax.dot_general(left, right, dims, preferred_element_type=f32)


def shards(
    tokens,
    lengths,
    order,
    mixer_gain,
    feed_gain,
    in_weight,
    conv_taps,
    out_weight,
    gate_up,
    down_weight,
    cotangent,
):
    local_rows = tokens.shape[1]
    seq_count, wt_count, grp_count = (lax.axis_size(a) for a in ("seq", "wt", "grp"))
    seq_at, wt_at, grp_at = (lax.axis_index(a) for a in ("seq", "wt", "grp"))
    peers = seq_count * wt_count
    per_peer = local_rows // peers
    block_index = seq_at * wt_count + wt_at
    places = [(a, b) for a in range(seq_count) for b in range(grp_count)]
    others = range(1, seq_count)
    steps = range(1, grp_count)
    ring = list(steps) + [0]
    shard_width = in_weight.shape[0]
    channels = out_weight.shape[0]
    half = gate_up.shape[2] // 2

    def relative(array):
        return relative_columns(array, seq_at, grp_at, seq_count, grp_count)

    stages = Sequence()
    by_seq, by_grp = Chain(stages, "seq", 2), Chain(stages, "grp", 2)
    backwards = [*others, 0]

    def grp_steps(held, sides=(0,)):
        for b in steps:
            for a in sides:
                held[(a, b)] = by_grp.send(held[(a, b - 1)], 1)
                yield

    def seq_steps(held, at=None):
        for b in [0, *steps] if at is None else at:
            for a in others:
                held[(a, b)] = by_seq.send(held[(0, b)], a)
            yield

    def gathering(values):
        step = wt_count // 2
        while step:
            got = stages.send(values, lambda v, step=step: crossed(v, "wt", step))
            yield
            values = jnp.concatenate([values, got], axis=0)
            step //= 2
        yield stages.tie(values)

    def scattering(product):
        rows, step, total = span_rows, 1, None
        while step < wt_count:
            half_rows = rows // 2
            if total is None:
                got = stages.send(
                    product(half_rows, rows).astype(bf16), lambda v, step=step: crossed(v, "wt", step)
                )
                kept = stages.mark(product(0, half_rows))
            else:
                got = stages.send(
                    total[half_rows:].astype(bf16), lambda v, step=step: crossed(v, "wt", step)
                )
                kept = total[:half_rows]
            yield
            total = kept + stages.tie(got).astype(f32)
            rows, step = half_rows, step * 2
        yield total

    def side(array, a):
        return array[:, a * grp_count * shard_width : (a + 1) * grp_count * shard_width]

    def block(array, b, axis):
        return lax.slice_in_dim(array, b * shard_width, (b + 1) * shard_width, axis=axis)

    def whole(held, axis):
        return jnp.concatenate([held[p] for p in places], axis=axis)

    class Reduction:
        def __init__(self, axis):
            self.axis, self.sums = axis, {}

        def part(self, a, b):
            return block(self.products[a], b, self.axis)

        def seq(self):
            for b in ring:
                got = [by_seq.send(self.part(a, b), -a) for a in others]
                self.sums[b] = sum([g.astype(f32) for g in got], self.part(0, b).astype(f32))
                yield

        def grp(self):
            self.total = self.sums[ring[0]]
            for b in ring[1:]:
                got = by_grp.send(self.total.astype(bf16), 1)
                yield
                self.total = self.sums[b] + got.astype(f32)

        def grp_first(self):
            self.totals = {a: self.part(a, ring[0]) for a in backwards}
            for b in ring[1:]:
                for a in backwards:
                    got = by_grp.send(self.totals[a].astype(bf16), 1).astype(f32)
                    self.totals[a] = self.part(a, b).astype(f32) + got
                    yield

        def seq_last(self):
            self.total = self.totals[0]
            for a in others:
                got = by_seq.send(self.totals[a].astype(bf16), -a)
                self.total = self.total + got.astype(f32)

    def products(left, right, axis):
        result = {}
        for a in backwards:
            pair = (side(left, a), right) if axis == 0 else (left, side(right, a))
            result[a] = stages.mark(
                matmul(stages.tie(pair[0]), pair[1], contract_rows).astype(bf16)
            )
        return result

    def hidden_part(array, h):
        return array[..., h * half : (h + 1) * half]

    in_held = {(0, 0): in_weight.reshape(shard_width, 3 * channels)}
    out_held = {(0, 0): out_weight}
    gate_held = [
        {(0, 0): hidden_part(gate_up, h).reshape(shard_width, 2 * half)} for h in range(2)
    ]
    down_held = [{(0, 0): down_weight[h * half : (h + 1) * half]} for h in range(2)]
    in_grp, out_grp = grp_steps(in_held), grp_steps(out_held)
    gate_grp = [grp_steps(held) for held in gate_held]
    down_grp = [grp_steps(held, [0, *others]) for held in down_held]
    in_seq, out_seq = seq_steps(in_held), seq_steps(out_held)
    gate_seq = [seq_steps(held) for held in gate_held]
    down_seq = [seq_steps(held, [0]) for held in down_held]

    go(in_grp)
    go(in_seq)

    order_row = order[0]
    slot_blocks = order_row.reshape(peers, local_rows)
    here_positions = lax.dynamic_index_in_dim(slot_blocks, block_index, 0, keepdims=False)
    targets = here_positions // local_rows
    slots = jnp.arange(local_rows, dtype=jnp.int32)
    earlier = slots[:, None] < slots[None, :]
    same = (targets[:, None] == targets[None, :]) & earlier
    send_place = targets * per_peer + jnp.sum(same.astype(jnp.int32), axis=0)
    send_matrix = (slots[:, None] == send_place[None, :]).astype(bf16)
    mine = slot_blocks // local_rows == block_index
    mine_rank = matmul(mine.astype(bf16), earlier.astype(bf16)).astype(jnp.int32)
    sources = jnp.arange(peers, dtype=jnp.int32)
    arrival = jnp.where(mine, sources[:, None] * per_peer + mine_rank, -1).reshape(-1)
    home_place = order_row - block_index * local_rows
    home_hot = (home_place[:, None] == slots[None, :]).astype(bf16)
    arrival_hot = (arrival[:, None] == slots[None, :]).astype(bf16)

    def exchange(rows):
        return lax.all_to_all(rows, ("seq", "wt"), split_axis=0, concat_axis=0, tiled=True)

    tokens_got = stages.send(select_rows(send_matrix, tokens[0], plain), exchange)
    home_matrix = stages.mark(matmul(stages.tie(home_hot), arrival_hot, contract_rows).astype(bf16))
    cot_sent = stages.mark(select_rows(send_matrix, stages.tie(cotangent[0]), plain))

    def home_of(got):
        return relative(select_rows(home_matrix, stages.tie(got), plain))

    def to_arrival(rows):
        return stages.send(select_rows(home_matrix, relative(rows), contract_rows), exchange)

    def arrived(got):
        return select_rows(send_matrix, got, contract_rows)

    go(in_grp)
    go(in_seq)
    token_rows = home_of(tokens_got).astype(f32)
    mixer_row = relative(mixer_gain[None])
    feed_row = relative(feed_gain[None])
    scale_mix = rms_scale(token_rows)
    normed = gathering((token_rows * scale_mix * mixer_row).astype(bf16))
    next(normed)
    rest(in_grp)
    go(in_seq)
    go(out_grp)
    go(in_seq)
    next(normed)
    go(out_grp)
    go(out_seq)
    normed_all = next(normed)
    span_rows = normed_all.shape[0]
    rest(out_grp)
    go(gate_grp[0])
    go(out_seq)
    go(gate_grp[1])

    full_in = whole(in_held, 0)
    projected = matmul(stages.tie(normed_all), full_in)
    in_gate, out_gate, values = (
        projected[:, k * channels : (k + 1) * channels] for k in range(3)
    )
    gated = stages.mark((in_gate * values).astype(bf16))

    rel = peer_order(wt_count)
    place_of = jnp.array([rel.index(j) for j in range(wt_count)] + [wt_count], dtype=jnp.int32)
    block_at = [wt_at ^ j for j in rel]

    def taken(array, at):
        return lax.dynamic_index_in_dim(array, at, 0, keepdims=False)

    def row_of(block):
        return place_of[wt_at ^ block]

    tails = gated.reshape(wt_count, local_rows, channels)[:, -2:]
    carried = stages.send(
        taken(tails, row_of(wt_count - 1)), lambda v: passed_along(v, "seq", 1)
    )
    rest(out_seq)
    tails = jnp.concatenate([tails, stages.tie(carried)[None]], axis=0)
    before = jnp.stack(
        [
            taken(tails, jnp.where(at == 0, wt_count, row_of(jnp.maximum(at - 1, 0))))
            for at in block_at
        ]
    )
    extended = jnp.concatenate(
        [before, gated.reshape(wt_count, local_rows, channels)], axis=1
    ).astype(f32)
    positions = (
        (seq_at * wt_count + jnp.stack(block_at))[:, None] * local_rows + slots[None, :]
    )[:, :, None]
    docs = lengths.shape[1]
    starts = [sum([lengths[0, i] for i in range(d)], jnp.int32(0)) for d in range(docs)]

    def mask(at, back):
        opening = jnp.zeros_like(at)
        for start in starts:
            opening = jnp.where(start <= at, jnp.maximum(opening, start), opening)
        return (at - back >= opening).astype(f32)

    mask_one, mask_two = mask(positions, 1), mask(positions, 2)
    taps = conv_taps.astype(f32)
    now, one_back, two_back = extended[:, 2:], extended[:, 1:-1], extended[:, :-2]
    mixed = (taps[2] * now + mask_one * taps[1] * one_back + mask_two * taps[0] * two_back).reshape(
        span_rows, channels
    )
    mixed_out = stages.mark((out_gate * mixed).astype(bf16))
    go(gate_grp[0])
    go(gate_seq[0])
    full_out = whole(out_held, 1)
    branch = scattering(lambda i, j: matmul(stages.tie(mixed_out)[i:j], full_out))
    next(branch)
    go(gate_seq[0])
    next(branch)
    go(gate_grp[1])
    go(gate_grp[0])
    go(gate_seq[0])
    hidden_state = token_rows + next(branch)
    scale_feed = rms_scale(hidden_state)
    feed = gathering((hidden_state * scale_feed * feed_row).astype(bf16))
    next(feed)
    go(down_seq[0])
    cot_got = stages.send(cot_sent, exchange)
    go(gate_grp[1])
    next(feed)
    feed_all = next(feed)
    go(gate_seq[0])
    go(down_seq[1])
    go(down_grp[0])
    cot_rows = home_of(cot_got)
    cot = gathering(cot_rows)
    next(cot)
    go(down_grp[0])
    go(gate_seq[1])
    go(down_grp[0])

    full_gate, gate_part, up_part, activated = ({} for _ in range(4))
    full_down, gates_grad = {}, {}

    def forward_half(h):
        full_gate[h] = whole(gate_held[h], 0)
        source = stages.tie(feed_all)
        gate_part[h] = matmul(source, full_gate[h][:, :half])
        up_part[h] = matmul(source, full_gate[h][:, half:])
        activated[h] = stages.mark(
            (gate_part[h] * jax.nn.sigmoid(gate_part[h]) * up_part[h]).astype(bf16)
        )

    def backward_half(h):
        full_down[h] = whole(down_held[h], 1)
        act_grad = matmul(stages.tie(cot_all), full_down[h], contract_cols)
        gate, sigmoid_gate = gate_part[h], jax.nn.sigmoid(gate_part[h])
        gates_grad[h] = stages.mark(
            jnp.concatenate(
                [
                    (act_grad * up_part[h] * sigmoid_gate * (1.0 + gate * (1.0 - sigmoid_gate))).astype(
                        bf16
                    ),
                    (act_grad * gate * sigmoid_gate).astype(bf16),
                ],
                axis=1,
            )
        )

    gating, down = [Reduction(0), Reduction(0)], [Reduction(1), Reduction(1)]
    gating_seq, gating_grp = [g.seq() for g in gating], [g.grp() for g in gating]
    down_first, down_then = down[0].grp_first(), down[1].grp()
    down_swap = down[1].seq()
    forward_half(0)
    go(down_grp[0])
    go(gate_seq[1])
    next(cot)
    cot_all = next(cot)
    down[0].products = products(activated[0], cot_all, 1)
    go(down_grp[0])
    rest(down_grp[0])
    go(gate_seq[1])
    go(down_grp[1])
    rest(gate_seq[1])
    go(down_grp[1])
    backward_half(0)
    gating[0].products = products(feed_all, gates_grad[0], 0)
    go(down_grp[1], 2)
    go(gating_seq[0])
    rest(down_grp[1])
    go(gating_seq[0])
    forward_half(1)
    go(down_first)
    down[1].products = products(activated[1], cot_all, 1)
    go(down_first)
    go(gating_seq[0])
    backward_half(1)
    go(down_first)
    rest(gating_seq[0])
    gating[1].products = products(feed_all, gates_grad[1], 0)
    go(down_first)

    feed_norm = scattering(
        lambda i, j: sum(
            matmul(stages.tie(gates_grad[h])[i:j], full_gate[h], contract_cols) for h in range(2)
        )
    )
    next(feed_norm)
    go(down_swap)
    rest(down_first)
    next(feed_norm)
    go(down_swap)
    go(gating_grp[0])
    go(down_swap)
    go(gating_grp[0])
    go(down_swap)
    feed_norm_grad = next(feed_norm)
    feed_hat = hidden_state * scale_feed
    feed_term = jnp.sum(feed_norm_grad * feed_hat, axis=0)
    feed_scaled = feed_norm_grad * feed_row
    hidden_grad = cot_rows.astype(f32) + scale_feed * (
        feed_scaled - feed_hat * jnp.mean(feed_scaled * feed_hat, axis=-1, keepdims=True)
    )
    branch_back = gathering(hidden_grad.astype(bf16))
    next(branch_back)
    feed_out = scattering(
        lambda i, j: sum(matmul(stages.tie(activated[h])[i:j], full_down[h]) for h in range(2))
    )
    next(feed_out)
    go(gating_seq[1])
    rest(gating_grp[0])
    next(branch_back)
    branch_grad = next(branch_back)
    go(gating_seq[1])
    go(down_then)

    mixed_out_grad = matmul(stages.tie(branch_grad), full_out, contract_cols)
    out_gate_grad = (mixed_out_grad * mixed).astype(bf16)
    mixed_grad = stages.mark((mixed_out_grad * out_gate).astype(bf16))
    heads = mixed_grad.reshape(wt_count, local_rows, channels)[:, :2]
    incoming = stages.send(taken(heads, row_of(0)), lambda v: passed_along(v, "seq", -1))
    out_sum, in_sum = Reduction(1), Reduction(0)
    out_swap, out_ring = out_sum.seq(), out_sum.grp()
    in_swap, in_ring = in_sum.seq(), in_sum.grp()
    out_sum.products = products(mixed_out, branch_grad, 1)
    next(feed_out)
    go(gating_seq[1])
    go(down_then)
    rest(gating_seq[1], down_then)
    go(gating_grp[1])
    heads = jnp.concatenate([heads, stages.tie(incoming)[None]], axis=0)
    last = wt_count - 1
    behind = jnp.stack(
        [
            taken(heads, jnp.where(at == last, wt_count, row_of(jnp.minimum(at + 1, last))))
            for at in block_at
        ]
    )
    grad_ext = jnp.concatenate(
        [mixed_grad.reshape(wt_count, local_rows, channels), behind], axis=1
    ).astype(f32)
    mixed_low = grad_ext[:, :-2]
    gated_grad = (
        taps[2] * mixed_low
        + taps[1] * mask(positions + 1, 1) * grad_ext[:, 1:-1]
        + taps[0] * mask(positions + 2, 2) * grad_ext[:, 2:]
    )
    taps_term = jnp.stack(
        [
            jnp.sum(mixed_low * mask_two * two_back, axis=(0, 1)),
            jnp.sum(mixed_low * mask_one * one_back, axis=(0, 1)),
            jnp.sum(mixed_low * now, axis=(0, 1)),
        ]
    )
    gated_low = gated_grad.astype(bf16).astype(f32).reshape(span_rows, channels)
    projected_grad = stages.mark(
        jnp.concatenate(
            [(gated_low * values).astype(bf16), out_gate_grad, (gated_low * in_gate).astype(bf16)],
            axis=1,
        )
    )
    mix_norm = scattering(
        lambda i, j: matmul(stages.tie(projected_grad)[i:j], full_in, contract_cols)
    )
    next(mix_norm)
    go(out_swap)
    next(mix_norm)
    in_sum.products = products(normed_all, projected_grad, 0)
    go(gating_grp[1])
    go(out_swap)
    block_got = to_arrival((hidden_state + next(feed_out)).astype(bf16))
    rest(out_swap)
    rest(gating_grp[1])
    mix_norm_grad = next(mix_norm)
    mix_hat = token_rows * scale_mix
    mixer_term = jnp.sum(mix_norm_grad * mix_hat, axis=0)
    mix_scaled = mix_norm_grad * mixer_row
    grad_home = hidden_grad + scale_mix * (
        mix_scaled - mix_hat * jnp.mean(mix_scaled * mix_hat, axis=-1, keepdims=True)
    )
    grad_got = to_arrival(grad_home.astype(bf16))
    down[0].seq_last()
    go(in_swap, 2)
    rest(out_ring)
    go(in_swap)
    block_out = arrived(block_got)
    gains = summed(relative(jnp.stack([mixer_term, feed_term])), ("wt", "seq", "grp"))
    taps_grad = summed(taps_term, ("seq", "grp"))
    go(in_ring)
    rest(in_swap)
    tokens_grad = arrived(grad_got).astype(f32)
    rest(in_ring)
    out_grad = out_sum.total
    in_grad = in_sum.total.reshape(shard_width, 3, channels)
    down_grad = jnp.concatenate([d.total for d in down], axis=0)
    gating_grad = jnp.concatenate(
        [g.total.reshape(shard_width, 2, half) for g in gating], axis=2
    )
    return (
        block_out[None],
        tokens_grad[None],
        gains[0],
        gains[1],
        in_grad,
        taps_grad,
        out_grad,
        gating_grad,
        down_grad,
    )


def solution(mesh):
    in_specs = (
        P("grp", ("seq", "wt"), None),
        P("grp", None),
        P("grp", None),
        P(),
        P(),
        P(("seq", "grp"), None, "wt"),
        P(None, "wt"),
        P("wt", ("seq", "grp")),
        P(("seq", "grp"), None, "wt"),
        P("wt", ("seq", "grp")),
        P("grp", ("seq", "wt"), None),
    )
    out_specs = (
        P("grp", ("seq", "wt"), None),
        P("grp", ("seq", "wt"), None),
        P(),
        P(),
        P(("seq", "grp"), None, "wt"),
        P(None, "wt"),
        P("wt", ("seq", "grp")),
        P(("seq", "grp"), None, "wt"),
        P("wt", ("seq", "grp")),
    )
    return jax.shard_map(shards, mesh=mesh, in_specs=in_specs, out_specs=out_specs, check_vma=False)
```

time: 1040 us -> 891 us (0.86)
  waiting for transfers between devices: 517 us -> 371 us
  matrix products: 266 us -> 197 us
  other arithmetic: 46.7 us -> 100 us
  local copies, waits for them, and re-layouts: 54.9 us -> 91.8 us
  starting transfers between devices: 134 us -> 102 us
    ppermute x84, waiting for transfers between devices: 431 us -> 329 us  [rotated(): lax.ppermute(array, axis, [(i, (i + by) % count) for i in range(count)])]
    dot_general x106 -> x34, matrix products: 260 us -> 184 us  [matmul(): return lax.dot_general(left, right, dims, preferred_element_type=f32)]
    ppermute x28 -> x0, waiting for transfers between devices: 46.4 us -> none  [crossed_both(): lax.ppermute(array, ('seq', 'wt'), [(i, i ^ by) for i in range(peers)])]
    convert_element_type x7 -> x28, other arithmetic: 6.68 us -> 44.3 us  [the longest x15 27.5 us: grp(): got = by_grp.send(self.total.astype(bf16), 1)]
    ppermute x84, starting transfers between devices: 95.6 us -> 63.8 us  [rotated(): lax.ppermute(array, axis, [(i, (i + by) % count) for i in range(count)])]
    ppermute x28 -> x0, starting transfers between devices: 20.3 us -> none  [crossed_both(): lax.ppermute(array, ('seq', 'wt'), [(i, i ^ by) for i in range(peers)])]
    all_to_all x0 -> x4, starting transfers between devices: none -> 19 us  [exchange(): lax.all_to_all(rows, ('seq', 'wt'), split_axis=0, concat_axis=0, tiled=True)]
    add x2 -> x11, other arithmetic: 0.31 us -> 17.2 us  [the longest x5 10.1 us: grp(): self.total = self.sums[b] + got.astype(f32)]
  transfers between devices with their start and end apart: 146 -> 114, of which waited for: 67 -> 53; matrix products, arithmetic and copies ran while one was open for 26% -> 42% of each run, Pallas kernels for 0% -> 0%
where the time goes in v2:
time: 891 us; the launch traced here: 877 us
  waiting for transfers between devices  371 us (42%)
  matrix products  197 us (22%)
  starting transfers between devices  102 us (11%)
  other arithmetic  100 us (11%)
  local copies, waits for them, and re-layouts  91.8 us (10%)
  between operations  15 us (2%)
    ppermute x84, waiting for transfers between devices, rotated(): lax.ppermute(array, axis, [(i, (i + by) % count) for i in range(count)])  329 us
    dot_general x34, matrix products, matmul(): return lax.dot_general(left, right, dims, preferred_element_type=f32)  184 us
    ppermute x84, starting transfers between devices, rotated(): lax.ppermute(array, axis, [(i, (i + by) % count) for i in range(count)])  63.8 us
    unnamed x309, local copies, waits for them, and re-layouts  58.9 us
    ppermute x24, waiting for transfers between devices, crossed(): return lax.ppermute(array, axis, [(i, i ^ by) for i in range(count)])  30.7 us
    convert_element_type x15, other arithmetic, grp(): got = by_grp.send(self.total.astype(bf16), 1)  27.5 us
    all_to_all x4, starting transfers between devices, exchange(): lax.all_to_all(rows, ('seq', 'wt'), split_axis=0, concat_axis=0, tiled=True)  19 us
  transfers between devices with their start and end apart: 114, of which 53 were waited for; matrix products, arithmetic and copies ran while one was open for 42% of the time, Pallas kernels for 0%

profile of v2, /device:TPU:0, one launch (start us, length us, event | category | flops | bytes accessed | tf_op | source)
XLA Modules:
  0.0 876.5 jit_solution(6747990776226310520)
XLA Ops:
  26.0 10.6 %all-to-all-done = bf16[8,32,2048]{2,1,0:T(8,128)(2,1)S(1)} async-done(((bf16[8,32,2048]{2,1,0:T(8,128)(2,1)}), bf16[8,32,2048]{2,1,0:T(8,128)(2,1)S(1)}, u32[]{:S(2)}, u32[]{:S(2)}) %all-to-all-start) | async-done | bytes 1048608 | tf_op jit(solution)/shard_map/all_to_all | solution.py:293
  73.4 9.8 %collective-permute-done.8 = bf16[256,1536]{0,1:T(8,128)(2,1)S(1)} collective-permute-done((bf16[256,1536]{0,1:T(8,128)(2,1)}, bf16[256,1536]{0,1:T(8,128)(2,1)S(1)}, u32[]{:S(2)}, u32[]{:S(2)}) %collective-permute-start.8) | collective-permute-done | bytes 786464 | tf_op jit(solution)/shard_map/ppermute | solution.py:16
  89.6 9.7 %collective-permute-done.11 = bf16[512,256]{1,0:T(8,128)(2,1)S(1)} collective-permute-done((bf16[512,256]{1,0:T(8,128)(2,1)S(1)}, bf16[512,256]{1,0:T(8,128)(2,1)S(1)}, u32[]{:S(2)}, u32[]{:S(2)}) %collective-permute-start.11) | collective-permute-done | bytes 262176 | tf_op jit(solution)/shard_map/ppermute | solution.py:16
  135.1 21.6 %collective-permute-done.21 = bf16[256,2048]{1,0:T(8,128)(2,1)} collective-permute-done((bf16[256,2048]{1,0:T(8,128)(2,1)S(1)}, bf16[256,2048]{1,0:T(8,128)(2,1)}, u32[]{:S(2)}, u32[]{:S(2)}) %collective-permute-start.21) | collective-permute-done | bytes 1048608 | tf_op jit(solution)/shard_map/ppermute | solution.py:16
  157.1 22.1 %collective-permute-done.20 = bf16[256,2048]{1,0:T(8,128)(2,1)} collective-permute-done((bf16[256,2048]{1,0:T(8,128)(2,1)S(1)}, bf16[256,2048]{1,0:T(8,128)(2,1)}, u32[]{:S(2)}, u32[]{:S(2)}) %collective-permute-start.20) | collective-permute-done | bytes 1048608 | tf_op jit(solution)/shard_map/ppermute | solution.py:16
  210.5 13.6 %collective-permute-done.27 = bf16[256,2048]{1,0:T(8,128)(2,1)} collective-permute-done((bf16[256,2048]{1,0:T(8,128)(2,1)}, bf16[256,2048]{1,0:T(8,128)(2,1)}, u32[]{:S(2)}, u32[]{:S(2)}) %collective-permute-start.27) | collective-permute-done | bytes 1048608 | tf_op jit(solution)/shard_map/ppermute | solution.py:16
  267.7 10.3 %multiply_convert_fusion.5 = (bf16[1024,1024]{0,1:T(8,128)(2,1)S(1)}, f32[1024,1024]{0,1:T(8,128)}) fusion(f32[1024,1024]{0,1:T(8,128)S(1)} %fusion.6, bf16[1024,2048]{1,0:T(8,128)(2,1)S(1)} %pad_maximum_fusion.1, bf16[2048,2048]{1,0:T(8,128)(2,1)} %constant_dynamic-update-slice_fusion.48), kind=kOutput, calls=%fused_computation.26 | convolution fusion | flops 4301258752 | bytes 18874368 | tf_op jit(solution)/shard_map/dot_general | solution.py:127
  283.9 12.6 %collective-permute-done.38 = bf16[1024,256]{1,0:T(8,128)(2,1)S(1)} collective-permute-done((bf16[1024,256]{1,0:T(8,128)(2,1)S(1)}, bf16[1024,256]{1,0:T(8,128)(2,1)S(1)}, u32[]{:S(2)}, u32[]{:S(2)}) %collective-permute-start.38) | collective-permute-done | bytes 524320 | tf_op jit(solution)/shard_map/ppermute | solution.py:16
  296.6 7.8 collective-permute-done.39
  312.9 8.3 collective-permute-done.37
  321.6 7.9 collective-permute-done.41
  332.7 9.6 %collective-permute-done.42 = bf16[1024,256]{1,0:T(8,128)(2,1)S(1)} collective-permute-done((bf16[1024,256]{1,0:T(8,128)(2,1)S(1)}, bf16[1024,256]{1,0:T(8,128)(2,1)S(1)}, u32[]{:S(2)}, u32[]{:S(2)}) %collective-permute-start.42) | collective-permute-done | bytes 524320 | tf_op jit(solution)/shard_map/ppermute | solution.py:16
  344.2 8.1 multiply_convert_fusion.4
  385.0 11.2 %collective-permute-done.45 = bf16[1024,256]{1,0:T(8,128)(2,1)} collective-permute-done((bf16[1024,256]{1,0:T(8,128)(2,1)}, bf16[1024,256]{1,0:T(8,128)(2,1)}, u32[]{:S(2)}, u32[]{:S(2)}) %collective-permute-start.45) | collective-permute-done | bytes 524320 | tf_op jit(solution)/shard_map/ppermute | solution.py:16
  400.4 8.3 fusion.2
  408.7 9.4 %multiply_convert_fusion.2 = (bf16[1024,1024]{0,1:T(8,128)(2,1)S(1)}, f32[1024,1024]{0,1:T(8,128)}) fusion(f32[1024,1024]{0,1:T(8,128)} %fusion.2, bf16[1024,2048]{1,0:T(8,128)(2,1)S(1)} %pad_maximum_fusion.1, bf16[2048,2048]{1,0:T(8,128)(2,1)} %constant_dynamic-update-slice_fusion.64), kind=kOutput, calls=%fused_computation.22 | convolution fusion | flops 4301258752 | bytes 18874368 | tf_op jit(solution)/shard_map/dot_general | solution.py:127
  472.8 9.7 %fusion.39 = f32[512,2048]{1,0:T(8,128)} fusion(bf16[2048,2048]{1,0:T(8,128)(2,1)} %constant_dynamic-update-slice_fusion.64, bf16[1024,2048]{0,1:T(8,128)(2,1)S(1)} %pad_maximum_fusion.4), kind=kOutput, calls=%fused_computation.116 | convolution fusion | flops 4294967296 | bytes 14680064 | tf_op jit(solution)/shard_map/dot_general | solution.py:127
  482.5 9.9 %add_convert_fusion.1 = bf16[512,2048]{1,0:T(8,128)(2,1)} fusion(f32[512,2048]{1,0:T(8,128)} %fusion.39, bf16[2048,2048]{1,0:T(8,128)(2,1)} %constant_dynamic-update-slice_fusion.48, bf16[1024,2048]{0,1:T(8,128)(2,1)S(1)} %copy-done.27), kind=kOutput, calls=%fused_computation.19 | convolution fusion | flops 4297064448 | bytes 16777216 | tf_op jit(solution)/shard_map/dot_general | solution.py:127
  492.4 10.5 %fusion.36 = f32[512,2048]{1,0:T(8,128)} fusion(bf16[2048,2048]{1,0:T(8,128)(2,1)} %constant_dynamic-update-slice_fusion.64, bf16[1024,2048]{0,1:T(8,128)(2,1)} %copy-done.29), kind=kOutput, calls=%fused_computation.113 | convolution fusion | flops 4294967296 | bytes 14680064 | tf_op jit(solution)/shard_map/dot_general | solution.py:127
  502.9 10.2 %convolution_add_fusion = f32[512,2048]{1,0:T(8,128)} fusion(f32[512,2048]{1,0:T(8,128)} %fusion.36, bf16[2048,2048]{1,0:T(8,128)(2,1)} %constant_dynamic-update-slice_fusion.48, bf16[1024,2048]{0,1:T(8,128)(2,1)S(1)} %copy-done.27), kind=kOutput, calls=%fused_computation.43 | convolution fusion | flops 4296015872 | bytes 18874368 | tf_op jit(solution)/shard_map/dot_general | solution.py:127
  521.1 9.7 %collective-permute-done.61 = bf16[1024,256]{1,0:T(8,128)(2,1)} collective-permute-done((bf16[1024,256]{1,0:T(8,128)(2,1)S(1)}, bf16[1024,256]{1,0:T(8,128)(2,1)}, u32[]{:S(2)}, u32[]{:S(2)}) %collective-permute-start.61) | collective-permute-done | bytes 524320 | tf_op jit(solution)/shard_map/ppermute | solution.py:16
  536.2 9.5 %collective-permute-done.63 = bf16[1024,256]{1,0:T(8,128)(2,1)S(1)} collective-permute-done((bf16[1024,256]{1,0:T(8,128)(2,1)S(1)}, bf16[1024,256]{1,0:T(8,128)(2,1)S(1)}, u32[]{:S(2)}, u32[]{:S(2)}) %collective-permute-start.63) | collective-permute-done | bytes 524320 | tf_op jit(solution)/shard_map/ppermute | solution.py:16
  546.1 12.6 %collective-permute-done.62 = bf16[256,2048]{1,0:T(8,128)(2,1)S(1)} collective-permute-done((bf16[256,2048]{1,0:T(8,128)(2,1)S(1)}, bf16[256,2048]{1,0:T(8,128)(2,1)S(1)}, u32[]{:S(2)}, u32[]{:S(2)}) %collective-permute-start.62) | collective-permute-done | bytes 1048608 | tf_op jit(solution)/shard_map/ppermute | solution.py:16
  560.4 8.2 collective-permute-done.64
  586.1 8.4 collective-permute-done.68
  601.2 12.1 %collective-permute-done.71 = bf16[1024,256]{1,0:T(8,128)(2,1)S(1)} collective-permute-done((bf16[1024,256]{1,0:T(8,128)(2,1)S(1)}, bf16[1024,256]{1,0:T(8,128)(2,1)S(1)}, u32[]{:S(2)}, u32[]{:S(2)}) %collective-permute-start.71) | collective-permute-done | bytes 524320 | tf_op jit(solution)/shard_map/ppermute | solution.py:16
  647.2 7.9 collective-permute-done.76
  659.8 10.0 %collective-permute-done.73 = bf16[256,2048]{1,0:T(8,128)(2,1)} collective-permute-done((bf16[256,2048]{1,0:T(8,128)(2,1)}, bf16[256,2048]{1,0:T(8,128)(2,1)}, u32[]{:S(2)}, u32[]{:S(2)}) %collective-permute-start.73) | collective-permute-done | bytes 1048608 | tf_op jit(solution)/shard_map/ppermute | solution.py:16
  732.0 12.4 %collective-permute-done.85 = bf16[256,2048]{1,0:T(8,128)(2,1)S(1)} collective-permute-done((bf16[256,2048]{1,0:T(8,128)(2,1)S(1)}, bf16[256,2048]{1,0:T(8,128)(2,1)S(1)}, u32[]{:S(2)}, u32[]{:S(2)}) %collective-permute-start.85) | collective-permute-done | bytes 1048608 | tf_op jit(solution)/shard_map/ppermute | solution.py:16
  756.0 8.8 %collective-permute-done.96 = bf16[1024,256]{1,0:T(8,128)(2,1)S(1)} collective-permute-done((bf16[1024,256]{1,0:T(8,128)(2,1)S(1)}, bf16[1024,256]{1,0:T(8,128)(2,1)S(1)}, u32[]{:S(2)}, u32[]{:S(2)}) %collective-permute-start.96) | collective-permute-done | bytes 524320 | tf_op jit(solution)/shard_map/ppermute | solution.py:16
  774.5 10.3 %collective-permute-done.90 = f32[2,2048]{1,0:T(2,128)S(1)} collective-permute-done((f32[2,2048]{1,0:T(2,128)S(1)}, f32[2,2048]{1,0:T(2,128)S(1)}, u32[]{:S(2)}, u32[]{:S(2)}) %collective-permute-start.90) | collective-permute-done | bytes 16416 | tf_op jit(solution)/shard_map/ppermute | solution.py:21
  832.6 8.9 %collective-permute-done.102 = bf16[256,1536]{1,0:T(8,128)(2,1)} collective-permute-done((bf16[256,1536]{1,0:T(8,128)(2,1)S(1)}, bf16[256,1536]{1,0:T(8,128)(2,1)}, u32[]{:S(2)}, u32[]{:S(2)}) %collective-permute-start.102) | collective-permute-done | bytes 786464 | tf_op jit(solution)/shard_map/ppermute | solution.py:16
  (718 shorter events, 521.5 us)
Async XLA Ops:
  6.1 56.3 %collective-permute-start.4 = (bf16[256,1536]{0,1:T(8,128)(2,1)}, bf16[256,1536]{0,1:T(8,128)(2,1)}, u32[]{:S(2)}, u32[]{:S(2)}) collective-permute-start(bf16[256,1536]{0,1:T(8,128)(2,1)} %bitcast.6), channel_id=1, source_target_pairs={{0,16},{16,0},{1,17},{17,1},{2,18},{18,2},{3,19},{19,3},{4,20},{20... | collective-permute-start | bytes 2359304 | tf_op jit(solution)/shard_map/ppermute | solution.py:16
  67.3 36.9 %collective-permute-start.6 = (bf16[512,2048]{1,0:T(8,128)(2,1)S(1)}, bf16[512,2048]{1,0:T(8,128)(2,1)S(1)}, u32[]{:S(2)}, u32[]{:S(2)}) collective-permute-start(bf16[512,2048]{1,0:T(8,128)(2,1)S(1)} %pad_maximum_fusion.8), channel_id=1, source_target_pairs={{0,4},{4,0},{8,12},{12,8},{1,5},{5,1},{9,13},{13,9},{2,6},{6,2},{1... | collective-permute-start | bytes 6291464 | tf_op jit(solution)/shard_map/ppermute | solution.py:21
  129.0 50.2 %collective-permute-start.20 = (bf16[256,2048]{1,0:T(8,128)(2,1)S(1)}, bf16[256,2048]{1,0:T(8,128)(2,1)}, u32[]{:S(2)}, u32[]{:S(2)}) collective-permute-start(bf16[256,2048]{1,0:T(8,128)(2,1)S(1)} %collective-permute-done.15), channel_id=1, source_target_pairs={{0,1},{1,2},{2,3},{3,0},{4,5},{5,6},{6,7},{7,4},{8,9},{9,10},{10,1... | collective-permute-start | bytes 3145736 | tf_op jit(solution)/shard_map/ppermute | solution.py:16
  129.4 49.8 %collective-permute-start.22 = (bf16[256,2048]{1,0:T(8,128)(2,1)S(1)}, bf16[256,2048]{1,0:T(8,128)(2,1)S(1)}, u32[]{:S(2)}, u32[]{:S(2)}) collective-permute-start(bf16[256,2048]{1,0:T(8,128)(2,1)S(1)} %bitcast.141), channel_id=1, source_target_pairs={{0,16},{16,0},{1,17},{17,1},{2,18},{18,2},{3,19},{19,3},{4,20},{20... | collective-permute-start | bytes 3145736 | tf_op jit(solution)/shard_map/ppermute | solution.py:16
  134.0 45.2 %collective-permute-start.19 = (bf16[256,2048]{1,0:T(8,128)(2,1)S(1)}, bf16[256,2048]{1,0:T(8,128)(2,1)S(1)}, u32[]{:S(2)}, u32[]{:S(2)}) collective-permute-start(bf16[256,2048]{1,0:T(8,128)(2,1)S(1)} %slice.1057), channel_id=1, source_target_pairs={{0,8},{4,12},{8,0},{12,4},{1,9},{5,13},{9,1},{13,5},{2,10},{6,14},... | collective-permute-start | bytes 3145736 | tf_op jit(solution)/shard_map/ppermute | solution.py:21
  134.8 49.1 %collective-permute-start.25 = (bf16[256,2048]{1,0:T(8,128)(2,1)S(1)}, bf16[256,2048]{1,0:T(8,128)(2,1)S(1)}, u32[]{:S(2)}, u32[]{:S(2)}) collective-permute-start(bf16[256,2048]{1,0:T(8,128)(2,1)S(1)} %collective-permute-done.15), channel_id=1, source_target_pairs={{0,16},{16,0},{1,17},{17,1},{2,18},{18,2},{3,19},{19,3},{4,20},{20... | collective-permute-start | bytes 3145736 | tf_op jit(solution)/shard_map/ppermute | solution.py:16
  156.7 44.9 %collective-permute-start.24 = (bf16[256,2048]{1,0:T(8,128)(2,1)}, bf16[256,2048]{1,0:T(8,128)(2,1)}, u32[]{:S(2)}, u32[]{:S(2)}) collective-permute-start(bf16[256,2048]{1,0:T(8,128)(2,1)} %collective-permute-done.21), channel_id=1, source_target_pairs={{0,1},{1,2},{2,3},{3,0},{4,5},{5,6},{6,7},{7,4},{8,9},{9,10},{10,1... | collective-permute-start | bytes 3145736 | tf_op jit(solution)/shard_map/ppermute | solution.py:16
  182.6 41.6 %collective-permute-start.27 = (bf16[256,2048]{1,0:T(8,128)(2,1)}, bf16[256,2048]{1,0:T(8,128)(2,1)}, u32[]{:S(2)}, u32[]{:S(2)}) collective-permute-start(bf16[256,2048]{1,0:T(8,128)(2,1)} %collective-permute-done.20), channel_id=1, source_target_pairs={{0,1},{1,2},{2,3},{3,0},{4,5},{5,6},{6,7},{7,4},{8,9},{9,10},{10,1... | collective-permute-start | bytes 3145736 | tf_op jit(solution)/shard_map/ppermute | solution.py:16
  184.9 46.2 %all-to-all-start.1 = ((bf16[8,32,2048]{2,1,0:T(8,128)(2,1)}), bf16[8,32,2048]{2,1,0:T(8,128)(2,1)}, u32[]{:S(2)}, u32[]{:S(2)}) async-start(bf16[8,32,2048]{2,1,0:T(8,128)(2,1)} %bitcast.145), calls=%async_computation.1 | async-start | bytes 2097152 | tf_op jit(solution)/shard_map/all_to_all | solution.py:293
  192.6 38.5 %collective-permute-start.29 = (bf16[1024,256]{1,0:T(8,128)(2,1)S(1)}, bf16[1024,256]{1,0:T(8,128)(2,1)}, u32[]{:S(2)}, u32[]{:S(2)}) collective-permute-start(bf16[1024,256]{1,0:T(8,128)(2,1)S(1)} %copy-done.85), channel_id=1, source_target_pairs={{0,16},{16,0},{1,17},{17,1},{2,18},{18,2},{3,19},{19,3},{4,20},{20... | collective-permute-start | bytes 1572872 | tf_op jit(solution)/shard_map/ppermute | solution.py:16
  201.7 44.9 %collective-permute-start.31 = (bf16[256,2048]{1,0:T(8,128)(2,1)}, bf16[256,2048]{1,0:T(8,128)(2,1)}, u32[]{:S(2)}, u32[]{:S(2)}) collective-permute-start(bf16[256,2048]{1,0:T(8,128)(2,1)} %collective-permute-done.24), channel_id=1, source_target_pairs={{0,1},{1,2},{2,3},{3,0},{4,5},{5,6},{6,7},{7,4},{8,9},{9,10},{10,1... | collective-permute-start | bytes 3145736 | tf_op jit(solution)/shard_map/ppermute | solution.py:16
  210.5 48.6 %collective-permute-start.26 = (bf16[512,2048]{1,0:T(8,128)(2,1)}, bf16[512,2048]{1,0:T(8,128)(2,1)}, u32[]{:S(2)}, u32[]{:S(2)}) collective-permute-start(bf16[512,2048]{1,0:T(8,128)(2,1)} %pad_maximum_fusion.9), channel_id=1, source_target_pairs={{0,4},{4,0},{8,12},{12,8},{1,5},{5,1},{9,13},{13,9},{2,6},{6,2},{1... | collective-permute-start | bytes 6291464 | tf_op jit(solution)/shard_map/ppermute | solution.py:21
  332.3 42.1 %collective-permute-start.47 = (bf16[256,2048]{1,0:T(8,128)(2,1)}, bf16[256,2048]{1,0:T(8,128)(2,1)S(1)}, u32[]{:S(2)}, u32[]{:S(2)}) collective-permute-start(bf16[256,2048]{1,0:T(8,128)(2,1)} %collective-permute-done.24), channel_id=1, source_target_pairs={{0,16},{16,0},{1,17},{17,1},{2,18},{18,2},{3,19},{19,3},{4,20},{20... | collective-permute-start | bytes 3145736 | tf_op jit(solution)/shard_map/ppermute | solution.py:16
  342.4 54.0 %collective-permute-start.48 = (bf16[256,2048]{1,0:T(8,128)(2,1)}, bf16[256,2048]{1,0:T(8,128)(2,1)}, u32[]{:S(2)}, u32[]{:S(2)}) collective-permute-start(bf16[256,2048]{1,0:T(8,128)(2,1)} %collective-permute-done.31), channel_id=1, source_target_pairs={{0,16},{16,0},{1,17},{17,1},{2,18},{18,2},{3,19},{19,3},{4,20},{20... | collective-permute-start | bytes 3145736 | tf_op jit(solution)/shard_map/ppermute | solution.py:16
  375.4 55.0 %collective-permute-start.53 = (bf16[256,2048]{1,0:T(8,128)(2,1)}, bf16[256,2048]{1,0:T(8,128)(2,1)S(1)}, u32[]{:S(2)}, u32[]{:S(2)}) collective-permute-start(bf16[256,2048]{1,0:T(8,128)(2,1)} %get-tuple-element.231), channel_id=1, source_target_pairs={{0,16},{16,0},{1,17},{17,1},{2,18},{18,2},{3,19},{19,3},{4,20},{20... | collective-permute-start | bytes 3145736 | tf_op jit(solution)/shard_map/ppermute | solution.py:16
  385.0 34.6 %collective-permute-start.49 = (bf16[1024,256]{1,0:T(8,128)(2,1)}, bf16[1024,256]{1,0:T(8,128)(2,1)}, u32[]{:S(2)}, u32[]{:S(2)}) collective-permute-start(bf16[1024,256]{1,0:T(8,128)(2,1)} %collective-permute-done.46), channel_id=1, source_target_pairs={{0,1},{1,2},{2,3},{3,0},{4,5},{5,6},{6,7},{7,4},{8,9},{9,10},{10,1... | collective-permute-start | bytes 1572872 | tf_op jit(solution)/shard_map/ppermute | solution.py:16
  396.4 57.0 %collective-permute-start.54 = (bf16[256,2048]{1,0:T(8,128)(2,1)}, bf16[256,2048]{1,0:T(8,128)(2,1)}, u32[]{:S(2)}, u32[]{:S(2)}) collective-permute-start(bf16[256,2048]{1,0:T(8,128)(2,1)} %get-tuple-element.234), channel_id=1, source_target_pairs={{0,16},{16,0},{1,17},{17,1},{2,18},{18,2},{3,19},{19,3},{4,20},{20... | collective-permute-start | bytes 3145736 | tf_op jit(solution)/shard_map/ppermute | solution.py:16
  429.8 39.9 %collective-permute-start.51 = (bf16[1024,256]{1,0:T(8,128)(2,1)}, bf16[1024,256]{1,0:T(8,128)(2,1)}, u32[]{:S(2)}, u32[]{:S(2)}) collective-permute-start(bf16[1024,256]{1,0:T(8,128)(2,1)} %slice.697), channel_id=1, source_target_pairs={{0,1},{1,2},{2,3},{3,0},{4,5},{5,6},{6,7},{7,4},{8,9},{9,10},{10,1... | collective-permute-start | bytes 1572872 | tf_op jit(solution)/shard_map/ppermute | solution.py:16
  430.4 84.1 %collective-permute-start.58 = (bf16[256,2048]{1,0:T(8,128)(2,1)}, bf16[256,2048]{1,0:T(8,128)(2,1)}, u32[]{:S(2)}, u32[]{:S(2)}) collective-permute-start(bf16[256,2048]{1,0:T(8,128)(2,1)} %get-tuple-element.240), channel_id=1, source_target_pairs={{0,16},{16,0},{1,17},{17,1},{2,18},{18,2},{3,19},{19,3},{4,20},{20... | collective-permute-start | bytes 3145736 | tf_op jit(solution)/shard_map/ppermute | solution.py:16
  451.5 61.7 %collective-permute-start.57 = (bf16[1024,256]{1,0:T(8,128)(2,1)}, bf16[1024,256]{1,0:T(8,128)(2,1)}, u32[]{:S(2)}, u32[]{:S(2)}) collective-permute-start(bf16[1024,256]{1,0:T(8,128)(2,1)} %add_convert_fusion.17), channel_id=1, source_target_pairs={{0,1},{1,2},{2,3},{3,0},{4,5},{5,6},{6,7},{7,4},{8,9},{9,10},{10,1... | collective-permute-start | bytes 1572872 | tf_op jit(solution)/shard_map/ppermute | solution.py:16
  453.4 67.6 %collective-permute-start.60 = (bf16[256,2048]{1,0:T(8,128)(2,1)}, bf16[256,2048]{1,0:T(8,128)(2,1)S(1)}, u32[]{:S(2)}, u32[]{:S(2)}) collective-permute-start(bf16[256,2048]{1,0:T(8,128)(2,1)} %get-tuple-element.243), channel_id=1, source_target_pairs={{0,16},{16,0},{1,17},{17,1},{2,18},{18,2},{3,19},{19,3},{4,20},{20... | collective-permute-start | bytes 3145736 | tf_op jit(solution)/shard_map/ppermute | solution.py:16
  471.7 44.8 %collective-permute-start.56 = (bf16[1024,256]{1,0:T(8,128)(2,1)}, bf16[1024,256]{1,0:T(8,128)(2,1)}, u32[]{:S(2)}, u32[]{:S(2)}) collective-permute-start(bf16[1024,256]{1,0:T(8,128)(2,1)} %add_convert_fusion.18), channel_id=1, source_target_pairs={{0,1},{1,2},{2,3},{3,0},{4,5},{5,6},{6,7},{7,4},{8,9},{9,10},{10,1... | collective-permute-start | bytes 1572872 | tf_op jit(solution)/shard_map/ppermute | solution.py:16
  531.2 37.6 %collective-permute-start.59 = (bf16[256,2048]{1,0:T(8,128)(2,1)S(1)}, bf16[256,2048]{1,0:T(8,128)(2,1)S(1)}, u32[]{:S(2)}, u32[]{:S(2)}) collective-permute-start(bf16[256,2048]{1,0:T(8,128)(2,1)S(1)} %slice.1056), channel_id=1, source_target_pairs={{0,8},{4,12},{8,0},{12,4},{1,9},{5,13},{9,1},{13,5},{2,10},{6,14},... | collective-permute-start | bytes 3145736 | tf_op jit(solution)/shard_map/ppermute | solution.py:21
  534.0 34.6 %collective-permute-start.64 = (bf16[1024,256]{1,0:T(8,128)(2,1)S(1)}, bf16[1024,256]{1,0:T(8,128)(2,1)S(1)}, u32[]{:S(2)}, u32[]{:S(2)}) collective-permute-start(bf16[1024,256]{1,0:T(8,128)(2,1)S(1)} %add_convert_fusion.16), channel_id=1, source_target_pairs={{0,1},{1,2},{2,3},{3,0},{4,5},{5,6},{6,7},{7,4},{8,9},{9,10},{10,1... | collective-permute-start | bytes 1572872 | tf_op jit(solution)/shard_map/ppermute | solution.py:16
  535.0 33.8 %collective-permute-start.65 = (bf16[1024,256]{1,0:T(8,128)(2,1)S(1)}, bf16[1024,256]{1,0:T(8,128)(2,1)S(1)}, u32[]{:S(2)}, u32[]{:S(2)}) collective-permute-start(bf16[1024,256]{1,0:T(8,128)(2,1)S(1)} %copy-done.89), channel_id=1, source_target_pairs={{0,16},{16,0},{1,17},{17,1},{2,18},{18,2},{3,19},{19,3},{4,20},{20... | collective-permute-start | bytes 1572872 | tf_op jit(solution)/shard_map/ppermute | solution.py:16
  545.8 40.3 %collective-permute-start.69 = (bf16[1024,256]{1,0:T(8,128)(2,1)S(1)}, bf16[1024,256]{1,0:T(8,128)(2,1)S(1)}, u32[]{:S(2)}, u32[]{:S(2)}) collective-permute-start(bf16[1024,256]{1,0:T(8,128)(2,1)S(1)} %copy-done.88), channel_id=1, source_target_pairs={{0,16},{16,0},{1,17},{17,1},{2,18},{18,2},{3,19},{19,3},{4,20},{20... | collective-permute-start | bytes 1572872 | tf_op jit(solution)/shard_map/ppermute | solution.py:16
  621.3 48.5 %collective-permute-start.73 = (bf16[256,2048]{1,0:T(8,128)(2,1)}, bf16[256,2048]{1,0:T(8,128)(2,1)}, u32[]{:S(2)}, u32[]{:S(2)}) collective-permute-start(bf16[256,2048]{1,0:T(8,128)(2,1)} %get-tuple-element.273), channel_id=1, source_target_pairs={{0,16},{16,0},{1,17},{17,1},{2,18},{18,2},{3,19},{19,3},{4,20},{20... | collective-permute-start | bytes 3145736 | tf_op jit(solution)/shard_map/ppermute | solution.py:16
  657.1 35.0 %collective-permute-start.81 = (bf16[256,2048]{1,0:T(8,128)(2,1)S(1)}, bf16[256,2048]{1,0:T(8,128)(2,1)S(1)}, u32[]{:S(2)}, u32[]{:S(2)}) collective-permute-start(bf16[256,2048]{1,0:T(8,128)(2,1)S(1)} %copy-done.70), channel_id=1, source_target_pairs={{0,16},{16,0},{1,17},{17,1},{2,18},{18,2},{3,19},{19,3},{4,20},{20... | collective-permute-start | bytes 3145736 | tf_op jit(solution)/shard_map/ppermute | solution.py:16
  705.0 65.2 %collective-permute-start.109 = (f32[3,512]{1,0:T(4,128)S(1)}, f32[3,512]{1,0:T(4,128)S(1)}, u32[]{:S(2)}, u32[]{:S(2)}) collective-permute-start(f32[3,512]{1,0:T(4,128)S(1)} %fusion.200), channel_id=1, source_target_pairs={{0,2},{1,3},{2,0},{3,1},{4,6},{5,7},{6,4},{7,5},{8,10},{9,11},{10,... | collective-permute-start | bytes 18440 | tf_op jit(solution)/shard_map/ppermute | solution.py:21
  710.4 35.6 %collective-permute-start.84 = (bf16[256,2048]{1,0:T(8,128)(2,1)S(1)}, bf16[256,2048]{1,0:T(8,128)(2,1)S(1)}, u32[]{:S(2)}, u32[]{:S(2)}) collective-permute-start(bf16[256,2048]{1,0:T(8,128)(2,1)S(1)} %slice.1054), channel_id=1, source_target_pairs={{0,8},{4,12},{8,0},{12,4},{1,9},{5,13},{9,1},{13,5},{2,10},{6,14},... | collective-permute-start | bytes 3145736 | tf_op jit(solution)/shard_map/ppermute | solution.py:21
  745.9 40.5 %collective-permute-start.98 = (bf16[256,2048]{1,0:T(8,128)(2,1)}, bf16[256,2048]{1,0:T(8,128)(2,1)}, u32[]{:S(2)}, u32[]{:S(2)}) collective-permute-start(bf16[256,2048]{1,0:T(8,128)(2,1)} %add_convert_fusion.2), channel_id=1, source_target_pairs={{0,1},{1,2},{2,3},{3,0},{4,5},{5,6},{6,7},{7,4},{8,9},{9,10},{10,1... | collective-permute-start | bytes 3145736 | tf_op jit(solution)/shard_map/ppermute | solution.py:16
  753.5 34.9 %collective-permute-start.95 = (bf16[256,1536]{1,0:T(8,128)(2,1)}, bf16[256,1536]{1,0:T(8,128)(2,1)}, u32[]{:S(2)}, u32[]{:S(2)}) collective-permute-start(bf16[256,1536]{1,0:T(8,128)(2,1)} %get-tuple-element.305), channel_id=1, source_target_pairs={{0,16},{16,0},{1,17},{17,1},{2,18},{18,2},{3,19},{19,3},{4,20},{20... | collective-permute-start | bytes 2359304 | tf_op jit(solution)/shard_map/ppermute | solution.py:16
  (213 other events, 4054.2 us)

commit v3 on v2

--- a/solution.py
+++ b/solution.py
@@ -42,6 +42,9 @@
         self.last = (array,)
         return array
 
+    def got(self, array):
+        return self.mark(self.tie(array))
+
     def send(self, array, move, *others):
         return move(self.mark(self.tie(array, *others)))
 
@@ -56,6 +59,9 @@
         result = self.stages.send(array, lambda v: rotated(v, self.axis, by), *behind)
         self.arrived.append(result)
         return result
+
+    def settle(self, back=1):
+        self.stages.got(self.arrived[-back])
 
 
 def go(steps, count=1):
@@ -153,26 +159,21 @@
     shard_width = in_weight.shape[0]
     channels = out_weight.shape[0]
     half = gate_up.shape[2] // 2
-
     def relative(array):
         return relative_columns(array, seq_at, grp_at, seq_count, grp_count)
-
     stages = Sequence()
     by_seq, by_grp = Chain(stages, "seq", 2), Chain(stages, "grp", 2)
     backwards = [*others, 0]
-
     def grp_steps(held, sides=(0,)):
         for b in steps:
             for a in sides:
                 held[(a, b)] = by_grp.send(held[(a, b - 1)], 1)
                 yield
-
     def seq_steps(held, at=None):
         for b in [0, *steps] if at is None else at:
             for a in others:
                 held[(a, b)] = by_seq.send(held[(0, b)], a)
             yield
-
     def gathering(values):
         step = wt_count // 2
         while step:
@@ -181,54 +182,50 @@
             values = jnp.concatenate([values, got], axis=0)
             step //= 2
         yield stages.tie(values)
-
-    def scattering(product):
-        rows, step, total = span_rows, 1, None
+    def scattering(sent, kept):
+        step = 1
         while step < wt_count:
-            half_rows = rows // 2
-            if total is None:
-                got = stages.send(
-                    product(half_rows, rows).astype(bf16), lambda v, step=step: crossed(v, "wt", step)
-                )
-                kept = stages.mark(product(0, half_rows))
-            else:
-                got = stages.send(
-                    total[half_rows:].astype(bf16), lambda v, step=step: crossed(v, "wt", step)
-                )
-                kept = total[:half_rows]
+            got = stages.send(sent.astype(bf16), lambda v, step=step: crossed(v, "wt", step))
             yield
             total = kept + stages.tie(got).astype(f32)
-            rows, step = half_rows, step * 2
+            kept, sent = (total[: total.shape[0] // 2], total[total.shape[0] // 2 :])
+            step *= 2
         yield total
-
+    def halves(array, axis=0):
+        return jnp.split(array, 2, axis=axis)
+
+    def into_width(grads):
+        return jnp.einsum("ktc,kdc->td", grads, full_in, preferred_element_type=f32)
     def side(array, a):
         return array[:, a * grp_count * shard_width : (a + 1) * grp_count * shard_width]
-
     def block(array, b, axis):
         return lax.slice_in_dim(array, b * shard_width, (b + 1) * shard_width, axis=axis)
-
     def whole(held, axis):
         return jnp.concatenate([held[p] for p in places], axis=axis)
-
     class Reduction:
         def __init__(self, axis):
-            self.axis, self.sums = axis, {}
+            self.axis, self.came = axis, {}
 
         def part(self, a, b):
             return block(self.products[a], b, self.axis)
 
         def seq(self):
             for b in ring:
-                got = [by_seq.send(self.part(a, b), -a) for a in others]
-                self.sums[b] = sum([g.astype(f32) for g in got], self.part(0, b).astype(f32))
+                for a in others:
+                    self.came[(a, b)] = by_seq.send(self.part(a, b), -a)
                 yield
 
+        def summed(self, b):
+            return sum(
+                [self.came[(a, b)].astype(f32) for a in others], self.part(0, b).astype(f32)
+            )
+
         def grp(self):
-            self.total = self.sums[ring[0]]
+            self.total = self.summed(ring[0])
             for b in ring[1:]:
                 got = by_grp.send(self.total.astype(bf16), 1)
                 yield
-                self.total = self.sums[b] + got.astype(f32)
+                self.total = self.summed(b) + got.astype(f32)
 
         def grp_first(self):
             self.totals = {a: self.part(a, ring[0]) for a in backwards}
@@ -243,20 +240,23 @@
             for a in others:
                 got = by_seq.send(self.totals[a].astype(bf16), -a)
                 self.total = self.total + got.astype(f32)
-
-    def products(left, right, axis):
-        result = {}
+    def producing(reduction, left, right):
+        reduction.products = {}
         for a in backwards:
-            pair = (side(left, a), right) if axis == 0 else (left, side(right, a))
-            result[a] = stages.mark(
-                matmul(stages.tie(pair[0]), pair[1], contract_rows).astype(bf16)
-            )
-        return result
-
+            if right.ndim == 3:
+                product = jnp.einsum(
+                    "td,ktc->kdc", stages.tie(side(left, a)), right, preferred_element_type=f32
+                )
+            elif reduction.axis == 0:
+                product = matmul(stages.tie(side(left, a)), right, contract_rows)
+            else:
+                product = matmul(stages.tie(left), side(right, a), contract_rows)
+            reduction.products[a] = stages.mark(product.astype(bf16))
+            if a in (backwards[-2], backwards[-1]):
+                yield
     def hidden_part(array, h):
         return array[..., h * half : (h + 1) * half]
-
-    in_held = {(0, 0): in_weight.reshape(shard_width, 3 * channels)}
+    in_held = {(0, 0): in_weight.transpose(1, 0, 2)}
     out_held = {(0, 0): out_weight}
     gate_held = [
         {(0, 0): hidden_part(gate_up, h).reshape(shard_width, 2 * half)} for h in range(2)
@@ -268,10 +268,8 @@
     in_seq, out_seq = seq_steps(in_held), seq_steps(out_held)
     gate_seq = [seq_steps(held) for held in gate_held]
     down_seq = [seq_steps(held, [0]) for held in down_held]
-
     go(in_grp)
     go(in_seq)
-
     order_row = order[0]
     slot_blocks = order_row.reshape(peers, local_rows)
     here_positions = lax.dynamic_index_in_dim(slot_blocks, block_index, 0, keepdims=False)
@@ -288,68 +286,60 @@
     home_place = order_row - block_index * local_rows
     home_hot = (home_place[:, None] == slots[None, :]).astype(bf16)
     arrival_hot = (arrival[:, None] == slots[None, :]).astype(bf16)
-
     def exchange(rows):
         return lax.all_to_all(rows, ("seq", "wt"), split_axis=0, concat_axis=0, tiled=True)
-
     tokens_got = stages.send(select_rows(send_matrix, tokens[0], plain), exchange)
     home_matrix = stages.mark(matmul(stages.tie(home_hot), arrival_hot, contract_rows).astype(bf16))
+    by_grp.depth = 2
+    by_seq.depth = 2
     cot_sent = stages.mark(select_rows(send_matrix, stages.tie(cotangent[0]), plain))
-
     def home_of(got):
         return relative(select_rows(home_matrix, stages.tie(got), plain))
-
     def to_arrival(rows):
         return stages.send(select_rows(home_matrix, relative(rows), contract_rows), exchange)
-
     def arrived(got):
         return select_rows(send_matrix, got, contract_rows)
-
+    mixer_row = relative(mixer_gain[None])
+    feed_row = relative(feed_gain[None])
+    token_rows = home_of(tokens_got).astype(f32)
+    scale_mix = rms_scale(token_rows)
     go(in_grp)
     go(in_seq)
-    token_rows = home_of(tokens_got).astype(f32)
-    mixer_row = relative(mixer_gain[None])
-    feed_row = relative(feed_gain[None])
-    scale_mix = rms_scale(token_rows)
+    go(in_seq)
     normed = gathering((token_rows * scale_mix * mixer_row).astype(bf16))
     next(normed)
-    rest(in_grp)
+    go(in_grp)
+    go(out_seq)
+    by_grp.depth = 2
+    go(out_grp)
     go(in_seq)
     go(out_grp)
-    go(in_seq)
     next(normed)
-    go(out_grp)
-    go(out_seq)
     normed_all = next(normed)
     span_rows = normed_all.shape[0]
-    rest(out_grp)
+    go(out_grp)
+    full_in = whole(in_held, 1)
+    go(gate_grp[1])
+    go(out_seq)
     go(gate_grp[0])
+    in_source = stages.tie(normed_all)
     go(out_seq)
-    go(gate_grp[1])
-
-    full_in = whole(in_held, 0)
-    projected = matmul(stages.tie(normed_all), full_in)
-    in_gate, out_gate, values = (
-        projected[:, k * channels : (k + 1) * channels] for k in range(3)
-    )
+    in_gate, out_gate, values = (matmul(in_source, full_in[k]) for k in range(3))
     gated = stages.mark((in_gate * values).astype(bf16))
-
     rel = peer_order(wt_count)
     place_of = jnp.array([rel.index(j) for j in range(wt_count)] + [wt_count], dtype=jnp.int32)
     block_at = [wt_at ^ j for j in rel]
-
     def taken(array, at):
         return lax.dynamic_index_in_dim(array, at, 0, keepdims=False)
-
     def row_of(block):
         return place_of[wt_at ^ block]
-
     tails = gated.reshape(wt_count, local_rows, channels)[:, -2:]
     carried = stages.send(
         taken(tails, row_of(wt_count - 1)), lambda v: passed_along(v, "seq", 1)
     )
-    rest(out_seq)
+    by_grp.depth = 3
     tails = jnp.concatenate([tails, stages.tie(carried)[None]], axis=0)
+    go(out_seq)
     before = jnp.stack(
         [
             taken(tails, jnp.where(at == 0, wt_count, row_of(jnp.maximum(at - 1, 0))))
@@ -364,52 +354,54 @@
     )[:, :, None]
     docs = lengths.shape[1]
     starts = [sum([lengths[0, i] for i in range(d)], jnp.int32(0)) for d in range(docs)]
-
     def mask(at, back):
         opening = jnp.zeros_like(at)
         for start in starts:
             opening = jnp.where(start <= at, jnp.maximum(opening, start), opening)
         return (at - back >= opening).astype(f32)
-
     mask_one, mask_two = mask(positions, 1), mask(positions, 2)
     taps = conv_taps.astype(f32)
     now, one_back, two_back = extended[:, 2:], extended[:, 1:-1], extended[:, :-2]
     mixed = (taps[2] * now + mask_one * taps[1] * one_back + mask_two * taps[0] * two_back).reshape(
         span_rows, channels
     )
+    go(gate_seq[0])
     mixed_out = stages.mark((out_gate * mixed).astype(bf16))
+    full_out = whole(out_held, 1)
+    by_grp.settle()
+    kept, sent = halves(stages.tie(mixed_out))
+    kept = stages.mark(matmul(kept, full_out))
+    sent = stages.mark(matmul(sent, full_out).astype(bf16))
     go(gate_grp[0])
-    go(gate_seq[0])
-    full_out = whole(out_held, 1)
-    branch = scattering(lambda i, j: matmul(stages.tie(mixed_out)[i:j], full_out))
+    branch = scattering(sent, kept)
+    next(branch)
     next(branch)
     go(gate_seq[0])
-    next(branch)
+    go(down_seq[0])
     go(gate_grp[1])
+    go(gate_seq[0])
     go(gate_grp[0])
-    go(gate_seq[0])
     hidden_state = token_rows + next(branch)
     scale_feed = rms_scale(hidden_state)
     feed = gathering((hidden_state * scale_feed * feed_row).astype(bf16))
     next(feed)
-    go(down_seq[0])
+    by_seq.settle()
     cot_got = stages.send(cot_sent, exchange)
     go(gate_grp[1])
+    go(gate_seq[0])
     next(feed)
     feed_all = next(feed)
-    go(gate_seq[0])
+    go(down_grp[0])
     go(down_seq[1])
-    go(down_grp[0])
     cot_rows = home_of(cot_got)
     cot = gathering(cot_rows)
     next(cot)
+    by_grp.depth = 3
     go(down_grp[0])
     go(gate_seq[1])
     go(down_grp[0])
-
     full_gate, gate_part, up_part, activated = ({} for _ in range(4))
     full_down, gates_grad = {}, {}
-
     def forward_half(h):
         full_gate[h] = whole(gate_held[h], 0)
         source = stages.tie(feed_all)
@@ -418,7 +410,7 @@
         activated[h] = stages.mark(
             (gate_part[h] * jax.nn.sigmoid(gate_part[h]) * up_part[h]).astype(bf16)
         )
-
+    forward_half(0)
     def backward_half(h):
         full_down[h] = whole(down_held[h], 1)
         act_grad = matmul(stages.tie(cot_all), full_down[h], contract_cols)
@@ -434,54 +426,70 @@
                 axis=1,
             )
         )
-
     gating, down = [Reduction(0), Reduction(0)], [Reduction(1), Reduction(1)]
     gating_seq, gating_grp = [g.seq() for g in gating], [g.grp() for g in gating]
     down_first, down_then = down[0].grp_first(), down[1].grp()
     down_swap = down[1].seq()
-    forward_half(0)
+    go(down_grp[0])
     go(down_grp[0])
     go(gate_seq[1])
     next(cot)
+    go(down_grp[0])
     cot_all = next(cot)
-    down[0].products = products(activated[0], cot_all, 1)
-    go(down_grp[0])
-    rest(down_grp[0])
+    go(gate_seq[1])
+    rest(producing(down[0], activated[0], cot_all))
     go(gate_seq[1])
     go(down_grp[1])
+    by_seq.settle(2)
+    go(down_grp[1])
+    rest(down_grp[0])
+    backward_half(0)
+    by_seq.settle(2)
+    gating_work = producing(gating[0], feed_all, gates_grad[0])
+    go(gating_work)
+    go(down_grp[1])
+    go(gating_seq[0])
+    go(gating_work)
+    go(down_grp[1])
+    go(down_grp[1])
+    by_grp.depth = 3
     rest(gate_seq[1])
+    go(gating_seq[0])
     go(down_grp[1])
-    backward_half(0)
-    gating[0].products = products(feed_all, gates_grad[0], 0)
-    go(down_grp[1], 2)
-    go(gating_seq[0])
-    rest(down_grp[1])
     go(gating_seq[0])
     forward_half(1)
     go(down_first)
-    down[1].products = products(activated[1], cot_all, 1)
     go(down_first)
-    go(gating_seq[0])
+    rest(producing(down[1], activated[1], cot_all))
+    go(down_first)
+    rest(down_grp[1])
     backward_half(1)
     go(down_first)
-    rest(gating_seq[0])
-    gating[1].products = products(feed_all, gates_grad[1], 0)
+    gating_work = producing(gating[1], feed_all, gates_grad[1])
+    go(down_swap)
+    go(gating_work)
+    go(gating_seq[0])
+    by_grp.depth = 3
     go(down_first)
-
-    feed_norm = scattering(
-        lambda i, j: sum(
-            matmul(stages.tie(gates_grad[h])[i:j], full_gate[h], contract_cols) for h in range(2)
-        )
-    )
+    norm_grad = stages.mark(
+        matmul(stages.tie(gates_grad[0]), full_gate[0], contract_cols)
+    )
+    go(down_swap)
+    go(gating_work)
+    norm_grad = stages.mark(
+        norm_grad + matmul(stages.tie(gates_grad[1]), full_gate[1], contract_cols)
+    )
+    kept, sent = halves(norm_grad)
+    go(down_swap)
+    feed_norm = scattering(sent, kept)
+    next(feed_norm)
     next(feed_norm)
     go(down_swap)
-    rest(down_first)
-    next(feed_norm)
-    go(down_swap)
+    go(down_first)
     go(gating_grp[0])
-    go(down_swap)
-    go(gating_grp[0])
-    go(down_swap)
+    go(gating_seq[1])
+    go(gating_seq[1])
+    by_grp.depth = 1
     feed_norm_grad = next(feed_norm)
     feed_hat = hidden_state * scale_feed
     feed_term = jnp.sum(feed_norm_grad * feed_hat, axis=0)
@@ -489,34 +497,45 @@
     hidden_grad = cot_rows.astype(f32) + scale_feed * (
         feed_scaled - feed_hat * jnp.mean(feed_scaled * feed_hat, axis=-1, keepdims=True)
     )
+    go(gating_grp[0])
     branch_back = gathering(hidden_grad.astype(bf16))
+    by_grp.depth = 2
     next(branch_back)
-    feed_out = scattering(
-        lambda i, j: sum(matmul(stages.tie(activated[h])[i:j], full_down[h]) for h in range(2))
-    )
-    next(feed_out)
-    go(gating_seq[1])
+    by_seq.settle(2)
+    fed = stages.mark(matmul(stages.tie(activated[0]), full_down[0]))
+    go(gating_grp[0])
     rest(gating_grp[0])
+    fed = stages.mark(fed + matmul(stages.tie(activated[1]), full_down[1]))
+    by_grp.settle()
+    go(down_then)
     next(branch_back)
     branch_grad = next(branch_back)
-    go(gating_seq[1])
-    go(down_then)
-
+    kept, sent = halves(fed)
+    feed_out = scattering(sent, kept)
     mixed_out_grad = matmul(stages.tie(branch_grad), full_out, contract_cols)
+    next(feed_out)
     out_gate_grad = (mixed_out_grad * mixed).astype(bf16)
     mixed_grad = stages.mark((mixed_out_grad * out_gate).astype(bf16))
     heads = mixed_grad.reshape(wt_count, local_rows, channels)[:, :2]
     incoming = stages.send(taken(heads, row_of(0)), lambda v: passed_along(v, "seq", -1))
-    out_sum, in_sum = Reduction(1), Reduction(0)
+    by_seq.settle()
+    by_seq.settle()
+    by_seq.settle(2)
+    out_sum, in_sum = Reduction(1), Reduction(1)
     out_swap, out_ring = out_sum.seq(), out_sum.grp()
     in_swap, in_ring = in_sum.seq(), in_sum.grp()
-    out_sum.products = products(mixed_out, branch_grad, 1)
+    by_grp.depth = 2
+    rest(producing(out_sum, mixed_out, branch_grad))
     next(feed_out)
     go(gating_seq[1])
     go(down_then)
-    rest(gating_seq[1], down_then)
+    go(down_then)
+    go(gating_seq[1])
+    rest(down_then)
+    by_seq.settle()
     go(gating_grp[1])
     heads = jnp.concatenate([heads, stages.tie(incoming)[None]], axis=0)
+    by_grp.depth = 2
     last = wt_count - 1
     behind = jnp.stack(
         [
@@ -542,22 +561,28 @@
     )
     gated_low = gated_grad.astype(bf16).astype(f32).reshape(span_rows, channels)
     projected_grad = stages.mark(
-        jnp.concatenate(
-            [(gated_low * values).astype(bf16), out_gate_grad, (gated_low * in_gate).astype(bf16)],
-            axis=1,
+        jnp.stack(
+            [(gated_low * values).astype(bf16), out_gate_grad, (gated_low * in_gate).astype(bf16)]
         )
     )
-    mix_norm = scattering(
-        lambda i, j: matmul(stages.tie(projected_grad)[i:j], full_in, contract_cols)
-    )
+    in_work = producing(in_sum, normed_all, projected_grad)
+    by_grp.depth = 2
+    kept, sent = halves(stages.tie(projected_grad), 1)
+    go(out_swap)
+    sent = stages.mark(into_width(sent).astype(bf16))
+    kept = stages.mark(into_width(kept))
+    by_grp.depth = 1
+    mix_norm = scattering(sent, kept)
     next(mix_norm)
+    go(gating_grp[1])
+    go(in_work)
+    next(mix_norm)
+    go(in_work)
     go(out_swap)
-    next(mix_norm)
-    in_sum.products = products(normed_all, projected_grad, 0)
+    go(out_swap)
+    go(out_swap)
     go(gating_grp[1])
-    go(out_swap)
     block_got = to_arrival((hidden_state + next(feed_out)).astype(bf16))
-    rest(out_swap)
     rest(gating_grp[1])
     mix_norm_grad = next(mix_norm)
     mix_hat = token_rows * scale_mix
@@ -568,18 +593,25 @@
     )
     grad_got = to_arrival(grad_home.astype(bf16))
     down[0].seq_last()
-    go(in_swap, 2)
+    by_seq.settle()
+    go(in_swap)
+    go(out_ring)
+    go(in_swap)
+    go(out_ring)
+    go(out_ring)
     rest(out_ring)
-    go(in_swap)
     block_out = arrived(block_got)
     gains = summed(relative(jnp.stack([mixer_term, feed_term])), ("wt", "seq", "grp"))
     taps_grad = summed(taps_term, ("seq", "grp"))
+    go(in_swap)
     go(in_ring)
-    rest(in_swap)
     tokens_grad = arrived(grad_got).astype(f32)
+    go(in_ring)
+    go(in_swap)
+    go(in_ring)
     rest(in_ring)
     out_grad = out_sum.total
-    in_grad = in_sum.total.reshape(shard_width, 3, channels)
+    in_grad = in_sum.total.transpose(1, 0, 2)
     down_grad = jnp.concatenate([d.total for d in down], axis=0)
     gating_grad = jnp.concatenate(
         [g.total.reshape(shard_width, 2, half) for g in gating], axis=2

time: 891 us -> 836 us (0.938)
  waiting for transfers between devices: 371 us -> 321 us
  local copies, waits for them, and re-layouts: 91.8 us -> 108 us
  other arithmetic: 100 us -> 85.2 us
    ppermute x84, waiting for transfers between devices: 329 us -> 303 us  [rotated(): lax.ppermute(array, axis, [(i, (i + by) % count) for i in range(count)])]
    dot_general x34 -> x28, matrix products: 184 us -> 157 us  [matmul(): return lax.dot_general(left, right, dims, preferred_element_type=f32)]
    ppermute x24, waiting for transfers between devices: 30.7 us -> 6.53 us  [crossed(): return lax.ppermute(array, axis, [(i, i ^ by) for i in range(count)])]
    dot_general x0 -> x4, matrix products: none -> 23.1 us  [the longest x2 13.1 us: into_width(): return jnp.einsum('ktc,kdc->td', grads, full_in, preferred_element_type=f32)]
    unnamed x309 -> x320, local copies, waits for them, and re-layouts: 58.9 us -> 70.6 us
  transfers between devices with their start and end apart: 114 -> 114, of which waited for: 53 -> 45; matrix products, arithmetic and copies ran while one was open for 42% -> 44% of each run, Pallas kernels for 0% -> 0%
where the time goes in v3:
time: 836 us; the launch traced here: 825 us
  waiting for transfers between devices  321 us (38%)
  matrix products  193 us (23%)
  local copies, waits for them, and re-layouts  108 us (13%)
  starting transfers between devices  103 us (12%)
  other arithmetic  85.2 us (10%)
  between operations  15.3 us (2%)
    ppermute x84, waiting for transfers between devices, rotated(): lax.ppermute(array, axis, [(i, (i + by) % count) for i in range(count)])  303 us
    dot_general x28, matrix products, matmul(): return lax.dot_general(left, right, dims, preferred_element_type=f32)  157 us
    unnamed x320, local copies, waits for them, and re-layouts  70.6 us
    ppermute x84, starting transfers between devices, rotated(): lax.ppermute(array, axis, [(i, (i + by) % count) for i in range(count)])  67.3 us
    convert_element_type x15, other arithmetic, grp(): got = by_grp.send(self.total.astype(bf16), 1)  26.7 us
  transfers between devices with their start and end apart: 114, of which 45 were waited for; matrix products, arithmetic and copies ran while one was open for 44% of the time, Pallas kernels for 0%

profile of v3, /device:TPU:0, one launch (start us, length us, event | category | flops | bytes accessed | tf_op | source)
XLA Modules:
  0.0 825.1 jit_solution(21355310847259406)
XLA Ops:
  25.2 10.5 %all-to-all-done = bf16[8,32,2048]{2,1,0:T(8,128)(2,1)S(1)} async-done(((bf16[8,32,2048]{2,1,0:T(8,128)(2,1)}), bf16[8,32,2048]{2,1,0:T(8,128)(2,1)S(1)}, u32[]{:S(2)}, u32[]{:S(2)}) %all-to-all-start) | async-done | bytes 1048608 | tf_op jit(solution)/shard_map/all_to_all | solution.py:290
  83.1 7.6 collective-permute-done.9
  99.7 7.8 collective-permute-done.14
  145.1 10.2 %collective-permute-done.22 = bf16[256,2048]{1,0:T(8,128)(2,1)} collective-permute-done((bf16[256,2048]{1,0:T(8,128)(2,1)}, bf16[256,2048]{1,0:T(8,128)(2,1)}, u32[]{:S(2)}, u32[]{:S(2)}) %collective-permute-start.22) | collective-permute-done | bytes 1048608 | tf_op jit(solution)/shard_map/ppermute | solution.py:16
  156.8 22.5 %collective-permute-done.20 = bf16[256,2048]{1,0:T(8,128)(2,1)} collective-permute-done((bf16[256,2048]{1,0:T(8,128)(2,1)}, bf16[256,2048]{1,0:T(8,128)(2,1)}, u32[]{:S(2)}, u32[]{:S(2)}) %collective-permute-start.20) | collective-permute-done | bytes 1048608 | tf_op jit(solution)/shard_map/ppermute | solution.py:16
  201.8 21.7 %collective-permute-done.27 = bf16[1024,256]{1,0:T(8,128)(2,1)S(1)} collective-permute-done((bf16[1024,256]{1,0:T(8,128)(2,1)}, bf16[1024,256]{1,0:T(8,128)(2,1)S(1)}, u32[]{:S(2)}, u32[]{:S(2)}) %collective-permute-start.27) | collective-permute-done | bytes 524320 | tf_op jit(solution)/shard_map/ppermute | solution.py:16
  240.6 8.2 collective-permute-done.31
  250.3 7.7 collective-permute-done.29
  270.6 10.7 %multiply_convert_fusion.5 = (bf16[1024,1024]{0,1:T(8,128)(2,1)}, f32[1024,1024]{0,1:T(8,128)}) fusion(f32[1024,1024]{0,1:T(8,128)S(1)} %fusion.6, bf16[1024,2048]{1,0:T(8,128)(2,1)S(1)} %pad_maximum_fusion.1, bf16[2048,2048]{1,0:T(8,128)(2,1)} %constant_dynamic-update-slice_fusion.48), kind=kOutput, calls=%fused_computation.27 | convolution fusion | flops 4301258752 | bytes 18874368 | tf_op jit(solution)/shard_map/dot_general | solution.py:133
  291.3 13.6 %collective-permute-done.36 = bf16[1024,256]{1,0:T(8,128)(2,1)S(1)} collective-permute-done((bf16[1024,256]{1,0:T(8,128)(2,1)S(1)}, bf16[1024,256]{1,0:T(8,128)(2,1)S(1)}, u32[]{:S(2)}, u32[]{:S(2)}) %collective-permute-start.36) | collective-permute-done | bytes 524320 | tf_op jit(solution)/shard_map/ppermute | solution.py:16
  305.6 10.6 %collective-permute-done.35 = bf16[1024,256]{1,0:T(8,128)(2,1)S(1)} collective-permute-done((bf16[1024,256]{1,0:T(8,128)(2,1)}, bf16[1024,256]{1,0:T(8,128)(2,1)S(1)}, u32[]{:S(2)}, u32[]{:S(2)}) %collective-permute-start.35) | collective-permute-done | bytes 524320 | tf_op jit(solution)/shard_map/ppermute | solution.py:16
  317.5 9.9 %collective-permute-done.39 = bf16[1024,256]{1,0:T(8,128)(2,1)S(1)} collective-permute-done((bf16[1024,256]{1,0:T(8,128)(2,1)S(1)}, bf16[1024,256]{1,0:T(8,128)(2,1)S(1)}, u32[]{:S(2)}, u32[]{:S(2)}) %collective-permute-start.39) | collective-permute-done | bytes 524320 | tf_op jit(solution)/shard_map/ppermute | solution.py:16
  336.3 8.1 multiply_convert_fusion.4
  372.3 9.0 %collective-permute-done.46 = bf16[1024,256]{1,0:T(8,128)(2,1)} collective-permute-done((bf16[1024,256]{1,0:T(8,128)(2,1)}, bf16[1024,256]{1,0:T(8,128)(2,1)}, u32[]{:S(2)}, u32[]{:S(2)}) %collective-permute-start.46) | collective-permute-done | bytes 524320 | tf_op jit(solution)/shard_map/ppermute | solution.py:16
  385.7 8.7 %fusion.2 = f32[1024,1024]{0,1:T(8,128)} fusion(bf16[1024,2048]{1,0:T(8,128)(2,1)S(1)} %pad_maximum_fusion.1, bf16[2048,2048]{1,0:T(8,128)(2,1)} %constant_dynamic-update-slice_fusion.64), kind=kOutput, calls=%fused_computation.6 | convolution fusion | flops 4294967296 | bytes 12582912 | tf_op jit(solution)/shard_map/dot_general | solution.py:133
  394.4 9.8 %multiply_convert_fusion.2 = (bf16[1024,1024]{0,1:T(8,128)(2,1)}, f32[1024,1024]{0,1:T(8,128)}) fusion(f32[1024,1024]{0,1:T(8,128)} %fusion.2, bf16[1024,2048]{1,0:T(8,128)(2,1)S(1)} %pad_maximum_fusion.1, bf16[2048,2048]{1,0:T(8,128)(2,1)} %constant_dynamic-update-slice_fusion.64), kind=kOutput, calls=%fused_computation.23 | convolution fusion | flops 4301258752 | bytes 18874368 | tf_op jit(solution)/shard_map/dot_general | solution.py:133
  429.8 9.6 %multiply_convert_fusion.1 = (bf16[1024,1024]{0,1:T(8,128)(2,1)S(1)}, bf16[1024,1024]{0,1:T(8,128)(2,1)S(1)}) fusion(f32[1024,1024]{0,1:T(8,128)} %fusion.2, f32[1024,1024]{0,1:T(8,128)} %get-tuple-element.480, bf16[1024,2048]{1,0:T(8,128)(2,1)S(1)} %pad_maximum_fusion.2, bf16[1024,2048]{1,0:T(8,128)(2,1)} %constant_dynamic-update-slice_fusion.72), kind=kOutput, calls=%fused_computation.22 | convolution fusion | flops 4308598784 | bytes 20971520 | tf_op jit(solution)/shard_map/dot_general | solution.py:133
  443.6 7.4 convolution_convert_fusion.1
  454.4 13.6 %fusion.145 = f32[1024,2048]{1,0:T(8,128)} fusion(bf16[1024,2048]{0,1:T(8,128)(2,1)S(1)} %pad_maximum_fusion.3, bf16[2048,2048]{1,0:T(8,128)(2,1)} %constant_dynamic-update-slice_fusion.48), kind=kOutput, calls=%fused_computation.544 | convolution fusion | flops 8589934592 | bytes 20971520 | tf_op jit(solution)/shard_map/dot_general | solution.py:133
  468.8 7.6 convolution_convert_fusion
  476.4 12.7 %convolution_add_fusion.1 = f32[1024,2048]{1,0:T(8,128)S(1)} fusion(f32[1024,2048]{1,0:T(8,128)} %fusion.145, bf16[1024,2048]{0,1:T(8,128)(2,1)S(1)} %copy-done.18, bf16[2048,2048]{1,0:T(8,128)(2,1)} %constant_dynamic-update-slice_fusion.64), kind=kOutput, calls=%fused_computation.35 | convolution fusion | flops 8592031744 | bytes 29360128 | tf_op jit(solution)/shard_map/dot_general | solution.py:133
  491.8 13.8 %collective-permute-done.56 = bf16[1024,256]{1,0:T(8,128)(2,1)S(1)} collective-permute-done((bf16[1024,256]{1,0:T(8,128)(2,1)S(1)}, bf16[1024,256]{1,0:T(8,128)(2,1)S(1)}, u32[]{:S(2)}, u32[]{:S(2)}) %collective-permute-start.56) | collective-permute-done | bytes 524320 | tf_op jit(solution)/shard_map/ppermute | solution.py:16
  525.6 10.0 %collective-permute-done.63 = bf16[1024,256]{1,0:T(8,128)(2,1)S(1)} collective-permute-done((bf16[1024,256]{1,0:T(8,128)(2,1)S(1)}, bf16[1024,256]{1,0:T(8,128)(2,1)S(1)}, u32[]{:S(2)}, u32[]{:S(2)}) %collective-permute-start.63) | collective-permute-done | bytes 524320 | tf_op jit(solution)/shard_map/ppermute | solution.py:16
  535.7 9.2 %collective-permute-done.64 = bf16[1024,256]{1,0:T(8,128)(2,1)S(1)} collective-permute-done((bf16[1024,256]{1,0:T(8,128)(2,1)S(1)}, bf16[1024,256]{1,0:T(8,128)(2,1)S(1)}, u32[]{:S(2)}, u32[]{:S(2)}) %collective-permute-start.64) | collective-permute-done | bytes 524320 | tf_op jit(solution)/shard_map/ppermute | solution.py:16
  562.3 10.6 %collective-permute-done.65 = bf16[256,2048]{1,0:T(8,128)(2,1)S(1)} collective-permute-done((bf16[256,2048]{1,0:T(8,128)(2,1)S(1)}, bf16[256,2048]{1,0:T(8,128)(2,1)S(1)}, u32[]{:S(2)}, u32[]{:S(2)}) %collective-permute-start.65) | collective-permute-done | bytes 1048608 | tf_op jit(solution)/shard_map/ppermute | solution.py:16
  574.7 10.3 %convolution_add_fusion = f32[1024,2048]{1,0:T(8,128)S(1)} fusion(f32[1024,2048]{1,0:T(8,128)} %fusion.144, bf16[1024,1024]{0,1:T(8,128)(2,1)} %get-tuple-element.248, bf16[1024,2048]{1,0:T(8,128)(2,1)} %constant_dynamic-update-slice_fusion.72), kind=kOutput, calls=%fused_computation.30 | convolution fusion | flops 4297064448 | bytes 23068672 | tf_op jit(solution)/shard_map/dot_general | solution.py:133
  612.1 8.1 collective-permute-done.76
  629.8 7.5 bitcast_convert_fusion
  673.1 9.0 %collective-permute-done.79 = bf16[256,2048]{1,0:T(8,128)(2,1)} collective-permute-done((bf16[256,2048]{1,0:T(8,128)(2,1)}, bf16[256,2048]{1,0:T(8,128)(2,1)}, u32[]{:S(2)}, u32[]{:S(2)}) %collective-permute-start.79) | collective-permute-done | bytes 1048608 | tf_op jit(solution)/shard_map/ppermute | solution.py:16
  697.8 13.4 %collective-permute-done.91 = bf16[256,2048]{1,0:T(8,128)(2,1)S(1)} collective-permute-done((bf16[256,2048]{1,0:T(8,128)(2,1)S(1)}, bf16[256,2048]{1,0:T(8,128)(2,1)S(1)}, u32[]{:S(2)}, u32[]{:S(2)}) %collective-permute-start.91) | collective-permute-done | bytes 1048608 | tf_op jit(solution)/shard_map/ppermute | solution.py:16
  762.8 13.2 %collective-permute-done.95 = bf16[3,256,512]{1,2,0:T(8,128)(2,1)} collective-permute-done((bf16[3,256,512]{1,2,0:T(8,128)(2,1)S(1)}, bf16[3,256,512]{1,2,0:T(8,128)(2,1)}, u32[]{:S(2)}, u32[]{:S(2)}) %collective-permute-start.95) | collective-permute-done | bytes 786464 | tf_op jit(solution)/shard_map/ppermute | solution.py:16
  807.0 7.8 collective-permute-done.101
  (724 shorter events, 469.3 us)
Async XLA Ops:
  3.8 33.8 %collective-permute-start.2 = (bf16[3,256,512]{2,1,0:T(8,128)(2,1)}, bf16[3,256,512]{2,1,0:T(8,128)(2,1)}, u32[]{:S(2)}, u32[]{:S(2)}) collective-permute-start(bf16[3,256,512]{2,1,0:T(8,128)(2,1)} %bitcast.181), channel_id=1, source_target_pairs={{0,16},{16,0},{1,17},{17,1},{2,18},{18,2},{3,19},{19,3},{4,20},{20... | collective-permute-start | bytes 2359304 | tf_op jit(solution)/shard_map/ppermute | solution.py:16
  73.4 34.7 %collective-permute-start.8 = (bf16[512,2048]{1,0:T(8,128)(2,1)S(1)}, bf16[512,2048]{1,0:T(8,128)(2,1)S(1)}, u32[]{:S(2)}, u32[]{:S(2)}) collective-permute-start(bf16[512,2048]{1,0:T(8,128)(2,1)S(1)} %pad_maximum_fusion.8), channel_id=1, source_target_pairs={{0,4},{4,0},{8,12},{12,8},{1,5},{5,1},{9,13},{13,9},{2,6},{6,2},{1... | collective-permute-start | bytes 6291464 | tf_op jit(solution)/shard_map/ppermute | solution.py:21
  130.4 48.9 %collective-permute-start.20 = (bf16[256,2048]{1,0:T(8,128)(2,1)}, bf16[256,2048]{1,0:T(8,128)(2,1)}, u32[]{:S(2)}, u32[]{:S(2)}) collective-permute-start(bf16[256,2048]{1,0:T(8,128)(2,1)} %collective-permute-done.17), channel_id=1, source_target_pairs={{0,1},{1,2},{2,3},{3,0},{4,5},{5,6},{6,7},{7,4},{8,9},{9,10},{10,1... | collective-permute-start | bytes 3145736 | tf_op jit(solution)/shard_map/ppermute | solution.py:16
  137.5 45.9 %collective-permute-start.23 = (bf16[256,2048]{1,0:T(8,128)(2,1)}, bf16[256,2048]{1,0:T(8,128)(2,1)}, u32[]{:S(2)}, u32[]{:S(2)}) collective-permute-start(bf16[256,2048]{1,0:T(8,128)(2,1)} %collective-permute-done.17), channel_id=1, source_target_pairs={{0,16},{16,0},{1,17},{17,1},{2,18},{18,2},{3,19},{19,3},{4,20},{20... | collective-permute-start | bytes 3145736 | tf_op jit(solution)/shard_map/ppermute | solution.py:16
  138.9 44.6 %collective-permute-start.19 = (bf16[256,2048]{1,0:T(8,128)(2,1)}, bf16[256,2048]{1,0:T(8,128)(2,1)}, u32[]{:S(2)}, u32[]{:S(2)}) collective-permute-start(bf16[256,2048]{1,0:T(8,128)(2,1)} %slice.985), channel_id=1, source_target_pairs={{0,8},{4,12},{8,0},{12,4},{1,9},{5,13},{9,1},{13,5},{2,10},{6,14},... | collective-permute-start | bytes 3145736 | tf_op jit(solution)/shard_map/ppermute | solution.py:21
  139.4 87.9 %all-to-all-start.1 = ((bf16[8,32,2048]{2,1,0:T(8,128)(2,1)}), bf16[8,32,2048]{2,1,0:T(8,128)(2,1)}, u32[]{:S(2)}, u32[]{:S(2)}) async-start(bf16[8,32,2048]{2,1,0:T(8,128)(2,1)} %bitcast.36), calls=%async_computation.1 | async-start | bytes 2097152 | tf_op jit(solution)/shard_map/all_to_all | solution.py:290
  156.8 44.9 %collective-permute-start.26 = (bf16[256,2048]{1,0:T(8,128)(2,1)}, bf16[256,2048]{1,0:T(8,128)(2,1)}, u32[]{:S(2)}, u32[]{:S(2)}) collective-permute-start(bf16[256,2048]{1,0:T(8,128)(2,1)} %collective-permute-done.21), channel_id=1, source_target_pairs={{0,1},{1,2},{2,3},{3,0},{4,5},{5,6},{6,7},{7,4},{8,9},{9,10},{10,1... | collective-permute-start | bytes 3145736 | tf_op jit(solution)/shard_map/ppermute | solution.py:16
  183.4 40.8 %collective-permute-start.25 = (bf16[256,2048]{1,0:T(8,128)(2,1)}, bf16[256,2048]{1,0:T(8,128)(2,1)}, u32[]{:S(2)}, u32[]{:S(2)}) collective-permute-start(bf16[256,2048]{1,0:T(8,128)(2,1)} %collective-permute-done.20), channel_id=1, source_target_pairs={{0,1},{1,2},{2,3},{3,0},{4,5},{5,6},{6,7},{7,4},{8,9},{9,10},{10,1... | collective-permute-start | bytes 3145736 | tf_op jit(solution)/shard_map/ppermute | solution.py:16
  186.1 39.5 %collective-permute-start.24 = (bf16[256,2048]{1,0:T(8,128)(2,1)S(1)}, bf16[256,2048]{1,0:T(8,128)(2,1)S(1)}, u32[]{:S(2)}, u32[]{:S(2)}) collective-permute-start(bf16[256,2048]{1,0:T(8,128)(2,1)S(1)} %multiply_convert_fusion.7), channel_id=1, source_target_pairs={{0,8},{4,12},{8,0},{12,4},{1,9},{5,13},{9,1},{13,5},{2,10},{6,14},... | collective-permute-start | bytes 3145736 | tf_op jit(solution)/shard_map/ppermute | solution.py:21
  188.1 39.2 %collective-permute-start.30 = (bf16[256,2048]{1,0:T(8,128)(2,1)}, bf16[256,2048]{1,0:T(8,128)(2,1)}, u32[]{:S(2)}, u32[]{:S(2)}) collective-permute-start(bf16[256,2048]{1,0:T(8,128)(2,1)} %collective-permute-done.20), channel_id=1, source_target_pairs={{0,16},{16,0},{1,17},{17,1},{2,18},{18,2},{3,19},{19,3},{4,20},{20... | collective-permute-start | bytes 3145736 | tf_op jit(solution)/shard_map/ppermute | solution.py:16
  201.8 47.1 %collective-permute-start.32 = (bf16[256,2048]{1,0:T(8,128)(2,1)}, bf16[256,2048]{1,0:T(8,128)(2,1)}, u32[]{:S(2)}, u32[]{:S(2)}) collective-permute-start(bf16[256,2048]{1,0:T(8,128)(2,1)} %collective-permute-done.26), channel_id=1, source_target_pairs={{0,1},{1,2},{2,3},{3,0},{4,5},{5,6},{6,7},{7,4},{8,9},{9,10},{10,1... | collective-permute-start | bytes 3145736 | tf_op jit(solution)/shard_map/ppermute | solution.py:16
  227.3 35.0 %collective-permute-start.28 = (bf16[512,2048]{1,0:T(8,128)(2,1)}, bf16[512,2048]{1,0:T(8,128)(2,1)}, u32[]{:S(2)}, u32[]{:S(2)}) collective-permute-start(bf16[512,2048]{1,0:T(8,128)(2,1)} %pad_maximum_fusion.9), channel_id=1, source_target_pairs={{0,4},{4,0},{8,12},{12,8},{1,5},{5,1},{9,13},{13,9},{2,6},{6,2},{1... | collective-permute-start | bytes 6291464 | tf_op jit(solution)/shard_map/ppermute | solution.py:21
  281.3 46.2 %collective-permute-start.40 = (bf16[512,2048]{1,0:T(8,128)(2,1)S(1)}, bf16[512,2048]{1,0:T(8,128)(2,1)S(1)}, u32[]{:S(2)}, u32[]{:S(2)}) collective-permute-start(bf16[512,2048]{1,0:T(8,128)(2,1)S(1)} %pad_maximum_fusion.10), channel_id=1, source_target_pairs={{0,4},{4,0},{8,12},{12,8},{1,5},{5,1},{9,13},{13,9},{2,6},{6,2},{1... | collective-permute-start | bytes 6291464 | tf_op jit(solution)/shard_map/ppermute | solution.py:21
  304.9 48.8 %collective-permute-start.45 = (bf16[256,2048]{1,0:T(8,128)(2,1)}, bf16[256,2048]{1,0:T(8,128)(2,1)S(1)}, u32[]{:S(2)}, u32[]{:S(2)}) collective-permute-start(bf16[256,2048]{1,0:T(8,128)(2,1)} %collective-permute-done.26), channel_id=1, source_target_pairs={{0,16},{16,0},{1,17},{17,1},{2,18},{18,2},{3,19},{19,3},{4,20},{20... | collective-permute-start | bytes 3145736 | tf_op jit(solution)/shard_map/ppermute | solution.py:16
  316.2 45.6 %collective-permute-start.41 = (bf16[1024,256]{1,0:T(8,128)(2,1)}, bf16[1024,256]{1,0:T(8,128)(2,1)}, u32[]{:S(2)}, u32[]{:S(2)}) collective-permute-start(bf16[1024,256]{1,0:T(8,128)(2,1)} %collective-permute-done.38), channel_id=1, source_target_pairs={{0,1},{1,2},{2,3},{3,0},{4,5},{5,6},{6,7},{7,4},{8,9},{9,10},{10,1... | collective-permute-start | bytes 1572872 | tf_op jit(solution)/shard_map/ppermute | solution.py:16
  335.4 35.9 %collective-permute-start.48 = (bf16[256,2048]{1,0:T(8,128)(2,1)}, bf16[256,2048]{1,0:T(8,128)(2,1)}, u32[]{:S(2)}, u32[]{:S(2)}) collective-permute-start(bf16[256,2048]{1,0:T(8,128)(2,1)} %collective-permute-done.32), channel_id=1, source_target_pairs={{0,16},{16,0},{1,17},{17,1},{2,18},{18,2},{3,19},{19,3},{4,20},{20... | collective-permute-start | bytes 3145736 | tf_op jit(solution)/shard_map/ppermute | solution.py:16
  370.0 34.8 %collective-permute-start.52 = (bf16[1024,256]{1,0:T(8,128)(2,1)}, bf16[1024,256]{1,0:T(8,128)(2,1)}, u32[]{:S(2)}, u32[]{:S(2)}) collective-permute-start(bf16[1024,256]{1,0:T(8,128)(2,1)} %collective-permute-done.47), channel_id=1, source_target_pairs={{0,1},{1,2},{2,3},{3,0},{4,5},{5,6},{6,7},{7,4},{8,9},{9,10},{10,1... | collective-permute-start | bytes 1572872 | tf_op jit(solution)/shard_map/ppermute | solution.py:16
  371.3 71.6 %collective-permute-start.51 = (bf16[256,2048]{1,0:T(8,128)(2,1)}, bf16[256,2048]{1,0:T(8,128)(2,1)S(1)}, u32[]{:S(2)}, u32[]{:S(2)}) collective-permute-start(bf16[256,2048]{1,0:T(8,128)(2,1)} %get-tuple-element.218), channel_id=1, source_target_pairs={{0,16},{16,0},{1,17},{17,1},{2,18},{18,2},{3,19},{19,3},{4,20},{20... | collective-permute-start | bytes 3145736 | tf_op jit(solution)/shard_map/ppermute | solution.py:16
  381.2 40.5 %collective-permute-start.55 = (bf16[1024,256]{1,0:T(8,128)(2,1)}, bf16[1024,256]{1,0:T(8,128)(2,1)}, u32[]{:S(2)}, u32[]{:S(2)}) collective-permute-start(bf16[1024,256]{1,0:T(8,128)(2,1)} %collective-permute-done.46), channel_id=1, source_target_pairs={{0,1},{1,2},{2,3},{3,0},{4,5},{5,6},{6,7},{7,4},{8,9},{9,10},{10,1... | collective-permute-start | bytes 1572872 | tf_op jit(solution)/shard_map/ppermute | solution.py:16
  404.8 34.6 %collective-permute-start.53 = (bf16[1024,256]{1,0:T(8,128)(2,1)}, bf16[1024,256]{1,0:T(8,128)(2,1)S(1)}, u32[]{:S(2)}, u32[]{:S(2)}) collective-permute-start(bf16[1024,256]{1,0:T(8,128)(2,1)} %slice.658), channel_id=1, source_target_pairs={{0,1},{1,2},{2,3},{3,0},{4,5},{5,6},{6,7},{7,4},{8,9},{9,10},{10,1... | collective-permute-start | bytes 1572872 | tf_op jit(solution)/shard_map/ppermute | solution.py:16
  407.3 43.7 %collective-permute-start.50 = (bf16[256,2048]{1,0:T(8,128)(2,1)}, bf16[256,2048]{1,0:T(8,128)(2,1)S(1)}, u32[]{:S(2)}, u32[]{:S(2)}) collective-permute-start(bf16[256,2048]{1,0:T(8,128)(2,1)} %get-tuple-element.220), channel_id=1, source_target_pairs={{0,16},{16,0},{1,17},{17,1},{2,18},{18,2},{3,19},{19,3},{4,20},{20... | collective-permute-start | bytes 3145736 | tf_op jit(solution)/shard_map/ppermute | solution.py:16
  452.0 37.4 %collective-permute-start.59 = (bf16[256,2048]{1,0:T(8,128)(2,1)}, bf16[256,2048]{1,0:T(8,128)(2,1)S(1)}, u32[]{:S(2)}, u32[]{:S(2)}) collective-permute-start(bf16[256,2048]{1,0:T(8,128)(2,1)} %get-tuple-element.231), channel_id=1, source_target_pairs={{0,16},{16,0},{1,17},{17,1},{2,18},{18,2},{3,19},{19,3},{4,20},{20... | collective-permute-start | bytes 3145736 | tf_op jit(solution)/shard_map/ppermute | solution.py:16
  510.5 34.4 %collective-permute-start.62 = (bf16[256,2048]{1,0:T(8,128)(2,1)S(1)}, bf16[256,2048]{1,0:T(8,128)(2,1)}, u32[]{:S(2)}, u32[]{:S(2)}) collective-permute-start(bf16[256,2048]{1,0:T(8,128)(2,1)S(1)} %add_convert_fusion.5), channel_id=1, source_target_pairs={{0,1},{1,2},{2,3},{3,0},{4,5},{5,6},{6,7},{7,4},{8,9},{9,10},{10,1... | collective-permute-start | bytes 3145736 | tf_op jit(solution)/shard_map/ppermute | solution.py:16
  525.6 33.3 %collective-permute-start.92 = (bf16[1024,256]{1,0:T(8,128)(2,1)S(1)}, bf16[1024,256]{1,0:T(8,128)(2,1)S(1)}, u32[]{:S(2)}, u32[]{:S(2)}) collective-permute-start(bf16[1024,256]{1,0:T(8,128)(2,1)S(1)} %copy-done.73), channel_id=1, source_target_pairs={{0,1},{1,2},{2,3},{3,0},{4,5},{5,6},{6,7},{7,4},{8,9},{9,10},{10,1... | collective-permute-start | bytes 1572872 | tf_op jit(solution)/shard_map/ppermute | solution.py:16
  560.2 43.6 %collective-permute-start.71 = (bf16[256,2048]{1,0:T(8,128)(2,1)}, bf16[256,2048]{1,0:T(8,128)(2,1)}, u32[]{:S(2)}, u32[]{:S(2)}) collective-permute-start(bf16[256,2048]{1,0:T(8,128)(2,1)} %get-tuple-element.244), channel_id=1, source_target_pairs={{0,16},{16,0},{1,17},{17,1},{2,18},{18,2},{3,19},{19,3},{4,20},{20... | collective-permute-start | bytes 3145736 | tf_op jit(solution)/shard_map/ppermute | solution.py:16
  560.9 83.1 %collective-permute-start.73 = (bf16[256,2048]{1,0:T(8,128)(2,1)}, bf16[256,2048]{1,0:T(8,128)(2,1)}, u32[]{:S(2)}, u32[]{:S(2)}) collective-permute-start(bf16[256,2048]{1,0:T(8,128)(2,1)} %get-tuple-element.245), channel_id=1, source_target_pairs={{0,16},{16,0},{1,17},{17,1},{2,18},{18,2},{3,19},{19,3},{4,20},{20... | collective-permute-start | bytes 3145736 | tf_op jit(solution)/shard_map/ppermute | solution.py:16
  574.7 33.6 %collective-permute-start.75 = (bf16[256,2048]{1,0:T(8,128)(2,1)}, bf16[256,2048]{1,0:T(8,128)(2,1)}, u32[]{:S(2)}, u32[]{:S(2)}) collective-permute-start(bf16[256,2048]{1,0:T(8,128)(2,1)} %add_convert_fusion.3), channel_id=1, source_target_pairs={{0,1},{1,2},{2,3},{3,0},{4,5},{5,6},{6,7},{7,4},{8,9},{9,10},{10,1... | collective-permute-start | bytes 3145736 | tf_op jit(solution)/shard_map/ppermute | solution.py:16
  611.5 74.7 %collective-permute-start.70 = (bf16[256,2048]{1,0:T(8,128)(2,1)}, bf16[256,2048]{1,0:T(8,128)(2,1)}, u32[]{:S(2)}, u32[]{:S(2)}) collective-permute-start(bf16[256,2048]{1,0:T(8,128)(2,1)} %slice.983), channel_id=1, source_target_pairs={{0,8},{4,12},{8,0},{12,4},{1,9},{5,13},{9,1},{13,5},{2,10},{6,14},... | collective-permute-start | bytes 3145736 | tf_op jit(solution)/shard_map/ppermute | solution.py:21
  648.9 62.3 %collective-permute-start.105 = (f32[3,512]{1,0:T(4,128)S(1)}, f32[3,512]{1,0:T(4,128)S(1)}, u32[]{:S(2)}, u32[]{:S(2)}) collective-permute-start(f32[3,512]{1,0:T(4,128)S(1)} %pad_maximum_fusion.13), channel_id=1, source_target_pairs={{0,16},{16,0},{1,17},{17,1},{2,18},{18,2},{3,19},{19,3},{4,20},{20... | collective-permute-start | bytes 18440 | tf_op jit(solution)/shard_map/ppermute | solution.py:21
  711.3 79.2 %collective-permute-start.108 = (bf16[1024,256]{1,0:T(8,128)(2,1)}, bf16[1024,256]{1,0:T(8,128)(2,1)}, u32[]{:S(2)}, u32[]{:S(2)}) collective-permute-start(bf16[1024,256]{1,0:T(8,128)(2,1)} %add_convert_fusion.14), channel_id=1, source_target_pairs={{0,1},{1,2},{2,3},{3,0},{4,5},{5,6},{6,7},{7,4},{8,9},{9,10},{10,1... | collective-permute-start | bytes 1572872 | tf_op jit(solution)/shard_map/ppermute | solution.py:16
  755.8 47.4 %all-to-all-start.3 = ((bf16[8,32,2048]{2,1,0:T(8,128)(2,1)}), bf16[8,32,2048]{2,1,0:T(8,128)(2,1)S(1)}, u32[]{:S(2)}, u32[]{:S(2)}) async-start(bf16[8,32,2048]{2,1,0:T(8,128)(2,1)} %bitcast.60), calls=%async_computation.3 | async-start | bytes 2097152 | tf_op jit(solution)/shard_map/all_to_all | solution.py:290
  760.9 37.6 %collective-permute-start.102 = (bf16[3,256,512]{1,2,0:T(8,128)(2,1)}, bf16[3,256,512]{1,2,0:T(8,128)(2,1)}, u32[]{:S(2)}, u32[]{:S(2)}) collective-permute-start(bf16[3,256,512]{1,2,0:T(8,128)(2,1)} %get-tuple-element.288), channel_id=1, source_target_pairs={{0,16},{16,0},{1,17},{17,1},{2,18},{18,2},{3,19},{19,3},{4,20},{20... | collective-permute-start | bytes 2359304 | tf_op jit(solution)/shard_map/ppermute | solution.py:16
  (219 other events, 4184.8 us)

commit v4 on v3

--- a/solution.py
+++ b/solution.py
@@ -169,6 +169,15 @@
             for a in sides:
                 held[(a, b)] = by_grp.send(held[(a, b - 1)], 1)
                 yield
+    def side_steps(held):
+        moving = None
+        for b in steps:
+            if moving is None:
+                moving = jnp.concatenate([held[(a, 0)] for a in range(seq_count)], axis=1)
+            moving = by_grp.send(moving, 1)
+            for a in range(seq_count):
+                held[(a, b)] = block(moving, a, 1)
+            yield
     def seq_steps(held, at=None):
         for b in [0, *steps] if at is None else at:
             for a in others:
@@ -193,7 +202,6 @@
         yield total
     def halves(array, axis=0):
         return jnp.split(array, 2, axis=axis)
-
     def into_width(grads):
         return jnp.einsum("ktc,kdc->td", grads, full_in, preferred_element_type=f32)
     def side(array, a):
@@ -209,10 +217,15 @@
         def part(self, a, b):
             return block(self.products[a], b, self.axis)
 
-        def seq(self):
-            for b in ring:
+        def seq(self, size=1):
+            for group in [ring[i : i + size] for i in range(0, grp_count, size)]:
                 for a in others:
-                    self.came[(a, b)] = by_seq.send(self.part(a, b), -a)
+                    sent = [self.part(a, b) for b in group]
+                    got = by_seq.send(
+                        sent[0] if len(sent) == 1 else jnp.concatenate(sent, axis=self.axis), -a
+                    )
+                    for i, b in enumerate(group):
+                        self.came[(a, b)] = block(got, i, self.axis)
                 yield
 
         def summed(self, b):
@@ -228,17 +241,19 @@
                 self.total = self.summed(b) + got.astype(f32)
 
         def grp_first(self):
-            self.totals = {a: self.part(a, ring[0]) for a in backwards}
+            def both(b):
+                return jnp.concatenate([self.part(a, b) for a in [0, *others]], axis=self.axis)
+
+            self.totals = both(ring[0])
             for b in ring[1:]:
-                for a in backwards:
-                    got = by_grp.send(self.totals[a].astype(bf16), 1).astype(f32)
-                    self.totals[a] = self.part(a, b).astype(f32) + got
-                    yield
+                got = by_grp.send(self.totals.astype(bf16), 1)
+                yield
+                self.totals = both(b).astype(f32) + got.astype(f32)
 
         def seq_last(self):
-            self.total = self.totals[0]
+            self.total = block(self.totals, 0, self.axis)
             for a in others:
-                got = by_seq.send(self.totals[a].astype(bf16), -a)
+                got = by_seq.send(block(self.totals, a, self.axis).astype(bf16), -a)
                 self.total = self.total + got.astype(f32)
     def producing(reduction, left, right):
         reduction.products = {}
@@ -264,12 +279,12 @@
     down_held = [{(0, 0): down_weight[h * half : (h + 1) * half]} for h in range(2)]
     in_grp, out_grp = grp_steps(in_held), grp_steps(out_held)
     gate_grp = [grp_steps(held) for held in gate_held]
-    down_grp = [grp_steps(held, [0, *others]) for held in down_held]
+    down_grp = [side_steps(held) for held in down_held]
     in_seq, out_seq = seq_steps(in_held), seq_steps(out_held)
     gate_seq = [seq_steps(held) for held in gate_held]
     down_seq = [seq_steps(held, [0]) for held in down_held]
+    go(in_seq)
     go(in_grp)
-    go(in_seq)
     order_row = order[0]
     slot_blocks = order_row.reshape(peers, local_rows)
     here_positions = lax.dynamic_index_in_dim(slot_blocks, block_index, 0, keepdims=False)
@@ -288,9 +303,9 @@
     arrival_hot = (arrival[:, None] == slots[None, :]).astype(bf16)
     def exchange(rows):
         return lax.all_to_all(rows, ("seq", "wt"), split_axis=0, concat_axis=0, tiled=True)
+    by_grp.depth = 2
     tokens_got = stages.send(select_rows(send_matrix, tokens[0], plain), exchange)
     home_matrix = stages.mark(matmul(stages.tie(home_hot), arrival_hot, contract_rows).astype(bf16))
-    by_grp.depth = 2
     by_seq.depth = 2
     cot_sent = stages.mark(select_rows(send_matrix, stages.tie(cotangent[0]), plain))
     def home_of(got):
@@ -301,9 +316,9 @@
         return select_rows(send_matrix, got, contract_rows)
     mixer_row = relative(mixer_gain[None])
     feed_row = relative(feed_gain[None])
+    go(in_grp)
     token_rows = home_of(tokens_got).astype(f32)
     scale_mix = rms_scale(token_rows)
-    go(in_grp)
     go(in_seq)
     go(in_seq)
     normed = gathering((token_rows * scale_mix * mixer_row).astype(bf16))
@@ -312,20 +327,20 @@
     go(out_seq)
     by_grp.depth = 2
     go(out_grp)
+    go(out_grp)
     go(in_seq)
-    go(out_grp)
     next(normed)
     normed_all = next(normed)
     span_rows = normed_all.shape[0]
+    go(out_seq)
     go(out_grp)
     full_in = whole(in_held, 1)
+    go(gate_grp[0])
     go(gate_grp[1])
-    go(out_seq)
-    go(gate_grp[0])
     in_source = stages.tie(normed_all)
-    go(out_seq)
     in_gate, out_gate, values = (matmul(in_source, full_in[k]) for k in range(3))
     gated = stages.mark((in_gate * values).astype(bf16))
+    go(out_seq)
     rel = peer_order(wt_count)
     place_of = jnp.array([rel.index(j) for j in range(wt_count)] + [wt_count], dtype=jnp.int32)
     block_at = [wt_at ^ j for j in rel]
@@ -366,40 +381,39 @@
         span_rows, channels
     )
     go(gate_seq[0])
+    by_grp.settle()
     mixed_out = stages.mark((out_gate * mixed).astype(bf16))
     full_out = whole(out_held, 1)
-    by_grp.settle()
     kept, sent = halves(stages.tie(mixed_out))
     kept = stages.mark(matmul(kept, full_out))
     sent = stages.mark(matmul(sent, full_out).astype(bf16))
+    branch = scattering(sent, kept)
     go(gate_grp[0])
-    branch = scattering(sent, kept)
+    go(gate_seq[0])
     next(branch)
     next(branch)
-    go(gate_seq[0])
     go(down_seq[0])
     go(gate_grp[1])
+    hidden_state = token_rows + next(branch)
     go(gate_seq[0])
+    scale_feed = rms_scale(hidden_state)
+    go(down_seq[1])
+    feed = gathering((hidden_state * scale_feed * feed_row).astype(bf16))
     go(gate_grp[0])
-    hidden_state = token_rows + next(branch)
-    scale_feed = rms_scale(hidden_state)
-    feed = gathering((hidden_state * scale_feed * feed_row).astype(bf16))
+    by_seq.settle()
     next(feed)
-    by_seq.settle()
     cot_got = stages.send(cot_sent, exchange)
     go(gate_grp[1])
     go(gate_seq[0])
     next(feed)
     feed_all = next(feed)
     go(down_grp[0])
-    go(down_seq[1])
     cot_rows = home_of(cot_got)
     cot = gathering(cot_rows)
+    by_grp.settle(2)
+    go(gate_seq[1])
     next(cot)
     by_grp.depth = 3
-    go(down_grp[0])
-    go(gate_seq[1])
-    go(down_grp[0])
     full_gate, gate_part, up_part, activated = ({} for _ in range(4))
     full_down, gates_grad = {}, {}
     def forward_half(h):
@@ -411,6 +425,7 @@
             (gate_part[h] * jax.nn.sigmoid(gate_part[h]) * up_part[h]).astype(bf16)
         )
     forward_half(0)
+    go(gate_seq[1])
     def backward_half(h):
         full_down[h] = whole(down_held[h], 1)
         act_grad = matmul(stages.tie(cot_all), full_down[h], contract_cols)
@@ -429,18 +444,17 @@
     gating, down = [Reduction(0), Reduction(0)], [Reduction(1), Reduction(1)]
     gating_seq, gating_grp = [g.seq() for g in gating], [g.grp() for g in gating]
     down_first, down_then = down[0].grp_first(), down[1].grp()
-    down_swap = down[1].seq()
+    down_swap = down[1].seq(2)
     go(down_grp[0])
+    next(cot)
     go(down_grp[0])
     go(gate_seq[1])
-    next(cot)
-    go(down_grp[0])
     cot_all = next(cot)
-    go(gate_seq[1])
+    by_grp.settle(2)
     rest(producing(down[0], activated[0], cot_all))
     go(gate_seq[1])
+    by_seq.settle(2)
     go(down_grp[1])
-    by_seq.settle(2)
     go(down_grp[1])
     rest(down_grp[0])
     backward_half(0)
@@ -449,48 +463,50 @@
     go(gating_work)
     go(down_grp[1])
     go(gating_seq[0])
-    go(gating_work)
-    go(down_grp[1])
-    go(down_grp[1])
+    go(gating_seq[0])
     by_grp.depth = 3
     rest(gate_seq[1])
+    go(down_first)
     go(gating_seq[0])
-    go(down_grp[1])
-    go(gating_seq[0])
+    by_grp.depth = 1
     forward_half(1)
     go(down_first)
-    go(down_first)
+    go(gating_work)
     rest(producing(down[1], activated[1], cot_all))
-    go(down_first)
+    go(down_swap)
     rest(down_grp[1])
     backward_half(1)
     go(down_first)
+    go(down_swap)
+    go(down_first)
+    go(down_first)
+    go(gating_seq[0])
     gating_work = producing(gating[1], feed_all, gates_grad[1])
-    go(down_swap)
     go(gating_work)
-    go(gating_seq[0])
-    by_grp.depth = 3
-    go(down_first)
+    by_seq.settle()
     norm_grad = stages.mark(
         matmul(stages.tie(gates_grad[0]), full_gate[0], contract_cols)
     )
-    go(down_swap)
+    by_grp.depth = 3
     go(gating_work)
     norm_grad = stages.mark(
         norm_grad + matmul(stages.tie(gates_grad[1]), full_gate[1], contract_cols)
     )
+    go(down_swap)
     kept, sent = halves(norm_grad)
-    go(down_swap)
     feed_norm = scattering(sent, kept)
     next(feed_norm)
     next(feed_norm)
     go(down_swap)
+    go(gating_seq[1])
+    by_grp.settle(2)
+    by_grp.settle(2)
+    by_grp.settle()
     go(down_first)
     go(gating_grp[0])
-    go(gating_seq[1])
-    go(gating_seq[1])
     by_grp.depth = 1
     feed_norm_grad = next(feed_norm)
+    go(gating_seq[1])
     feed_hat = hidden_state * scale_feed
     feed_term = jnp.sum(feed_norm_grad * feed_hat, axis=0)
     feed_scaled = feed_norm_grad * feed_row
@@ -498,6 +514,7 @@
         feed_scaled - feed_hat * jnp.mean(feed_scaled * feed_hat, axis=-1, keepdims=True)
     )
     go(gating_grp[0])
+    by_grp.depth = 3
     branch_back = gathering(hidden_grad.astype(bf16))
     by_grp.depth = 2
     next(branch_back)
@@ -510,25 +527,25 @@
     go(down_then)
     next(branch_back)
     branch_grad = next(branch_back)
+    mixed_out_grad = matmul(stages.tie(branch_grad), full_out, contract_cols)
     kept, sent = halves(fed)
     feed_out = scattering(sent, kept)
-    mixed_out_grad = matmul(stages.tie(branch_grad), full_out, contract_cols)
+    by_seq.settle()
     next(feed_out)
     out_gate_grad = (mixed_out_grad * mixed).astype(bf16)
     mixed_grad = stages.mark((mixed_out_grad * out_gate).astype(bf16))
     heads = mixed_grad.reshape(wt_count, local_rows, channels)[:, :2]
+    by_seq.settle()
+    by_seq.settle(2)
     incoming = stages.send(taken(heads, row_of(0)), lambda v: passed_along(v, "seq", -1))
-    by_seq.settle()
-    by_seq.settle()
-    by_seq.settle(2)
     out_sum, in_sum = Reduction(1), Reduction(1)
     out_swap, out_ring = out_sum.seq(), out_sum.grp()
     in_swap, in_ring = in_sum.seq(), in_sum.grp()
     by_grp.depth = 2
     rest(producing(out_sum, mixed_out, branch_grad))
     next(feed_out)
+    go(down_then)
     go(gating_seq[1])
-    go(down_then)
     go(down_then)
     go(gating_seq[1])
     rest(down_then)
@@ -566,25 +583,28 @@
         )
     )
     in_work = producing(in_sum, normed_all, projected_grad)
+    kept, sent = halves(stages.tie(projected_grad), 1)
+    by_seq.settle()
     by_grp.depth = 2
-    kept, sent = halves(stages.tie(projected_grad), 1)
     go(out_swap)
     sent = stages.mark(into_width(sent).astype(bf16))
     kept = stages.mark(into_width(kept))
     by_grp.depth = 1
+    by_grp.settle()
     mix_norm = scattering(sent, kept)
     next(mix_norm)
     go(gating_grp[1])
     go(in_work)
     next(mix_norm)
+    go(out_swap)
     go(in_work)
     go(out_swap)
     go(out_swap)
-    go(out_swap)
     go(gating_grp[1])
+    mix_norm_grad = next(mix_norm)
+    by_grp.settle(2)
     block_got = to_arrival((hidden_state + next(feed_out)).astype(bf16))
     rest(gating_grp[1])
-    mix_norm_grad = next(mix_norm)
     mix_hat = token_rows * scale_mix
     mixer_term = jnp.sum(mix_norm_grad * mix_hat, axis=0)
     mix_scaled = mix_norm_grad * mixer_row
@@ -596,18 +616,20 @@
     by_seq.settle()
     go(in_swap)
     go(out_ring)
+    go(out_ring)
+    by_seq.settle()
     go(in_swap)
-    go(out_ring)
     go(out_ring)
     rest(out_ring)
     block_out = arrived(block_got)
     gains = summed(relative(jnp.stack([mixer_term, feed_term])), ("wt", "seq", "grp"))
     taps_grad = summed(taps_term, ("seq", "grp"))
-    go(in_swap)
-    go(in_ring)
     tokens_grad = arrived(grad_got).astype(f32)
     go(in_ring)
+    go(in_ring)
     go(in_swap)
+    go(in_swap)
+    by_grp.settle()
     go(in_ring)
     rest(in_ring)
     out_grad = out_sum.total

time: 836 us -> 808 us (0.967)
  waiting for transfers between devices: 321 us -> 294 us
  other arithmetic: 85.2 us -> 93.6 us
    ppermute x84 -> x73, waiting for transfers between devices: 303 us -> 267 us  [rotated(): lax.ppermute(array, axis, [(i, (i + by) % count) for i in range(count)])]
    ppermute x24, waiting for transfers between devices: 6.53 us -> 18.6 us  [crossed(): return lax.ppermute(array, axis, [(i, i ^ by) for i in range(count)])]
    ppermute x84 -> x73, starting transfers between devices: 67.3 us -> 60.8 us  [rotated(): lax.ppermute(array, axis, [(i, (i + by) % count) for i in range(count)])]
    unnamed x320 -> x287, local copies, waits for them, and re-layouts: 70.6 us -> 66.5 us
  transfers between devices with their start and end apart: 114 -> 103, of which waited for: 45 -> 43; matrix products, arithmetic and copies ran while one was open for 44% -> 47% of each run, Pallas kernels for 0% -> 0%
where the time goes in v4:
time: 808 us; the launch traced here: 796 us
  waiting for transfers between devices  294 us (36%)
  matrix products  192 us (24%)
  local copies, waits for them, and re-layouts  101 us (12%)
  starting transfers between devices  99.4 us (12%)
  other arithmetic  93.6 us (12%)
  between operations  14.9 us (2%)
    ppermute x73, waiting for transfers between devices, rotated(): lax.ppermute(array, axis, [(i, (i + by) % count) for i in range(count)])  267 us
    dot_general x28, matrix products, matmul(): return lax.dot_general(left, right, dims, preferred_element_type=f32)  157 us
    unnamed x287, local copies, waits for them, and re-layouts  66.5 us
    ppermute x73, starting transfers between devices, rotated(): lax.ppermute(array, axis, [(i, (i + by) % count) for i in range(count)])  60.8 us
    convert_element_type x15, other arithmetic, grp(): got = by_grp.send(self.total.astype(bf16), 1)  26.9 us
    ppermute x24, starting transfers between devices, crossed(): return lax.ppermute(array, axis, [(i, i ^ by) for i in range(count)])  20.1 us
    ppermute x24, waiting for transfers between devices, crossed(): return lax.ppermute(array, axis, [(i, i ^ by) for i in range(count)])  18.6 us
  transfers between devices with their start and end apart: 103, of which 43 were waited for; matrix products, arithmetic and copies ran while one was open for 47% of the time, Pallas kernels for 0%

profile of v4, /device:TPU:0, one launch (start us, length us, event | category | flops | bytes accessed | tf_op | source)
XLA Modules:
  0.0 795.6 jit_solution(9833155869430851303)
XLA Ops:
  16.8 8.1 %collective-permute-done = bf16[3,256,512]{2,1,0:T(8,128)(2,1)} collective-permute-done((bf16[3,256,512]{2,1,0:T(8,128)(2,1)}, bf16[3,256,512]{2,1,0:T(8,128)(2,1)}, u32[]{:S(2)}, u32[]{:S(2)}) %collective-permute-start) | collective-permute-done | bytes 786464 | tf_op jit(solution)/shard_map/ppermute | solution.py:16
  25.4 8.1 %all-to-all-done = bf16[8,32,2048]{2,1,0:T(8,128)(2,1)S(1)} async-done(((bf16[8,32,2048]{2,1,0:T(8,128)(2,1)}), bf16[8,32,2048]{2,1,0:T(8,128)(2,1)S(1)}, u32[]{:S(2)}, u32[]{:S(2)}) %all-to-all-start) | async-done | bytes 1048608 | tf_op jit(solution)/shard_map/all_to_all | solution.py:305
  36.0 9.2 %collective-permute-done.1 = bf16[3,256,512]{2,1,0:T(8,128)(2,1)} collective-permute-done((bf16[3,256,512]{2,1,0:T(8,128)(2,1)}, bf16[3,256,512]{2,1,0:T(8,128)(2,1)}, u32[]{:S(2)}, u32[]{:S(2)}) %collective-permute-start.1) | collective-permute-done | bytes 786464 | tf_op jit(solution)/shard_map/ppermute | solution.py:16
  62.6 8.9 %collective-permute-done.6 = bf16[512,256]{1,0:T(8,128)(2,1)} collective-permute-done((bf16[512,256]{1,0:T(8,128)(2,1)S(1)}, bf16[512,256]{1,0:T(8,128)(2,1)}, u32[]{:S(2)}, u32[]{:S(2)}) %collective-permute-start.6) | collective-permute-done | bytes 262176 | tf_op jit(solution)/shard_map/ppermute | solution.py:16
  92.8 7.0 collective-permute-done.11
  136.0 16.9 %collective-permute-done.21 = bf16[256,2048]{1,0:T(8,128)(2,1)S(1)} collective-permute-done((bf16[256,2048]{1,0:T(8,128)(2,1)S(1)}, bf16[256,2048]{1,0:T(8,128)(2,1)S(1)}, u32[]{:S(2)}, u32[]{:S(2)}) %collective-permute-start.21) | collective-permute-done | bytes 1048608 | tf_op jit(solution)/shard_map/ppermute | solution.py:16
  163.8 11.7 %collective-permute-done.24 = bf16[256,2048]{1,0:T(8,128)(2,1)} collective-permute-done((bf16[256,2048]{1,0:T(8,128)(2,1)}, bf16[256,2048]{1,0:T(8,128)(2,1)}, u32[]{:S(2)}, u32[]{:S(2)}) %collective-permute-start.24) | collective-permute-done | bytes 1048608 | tf_op jit(solution)/shard_map/ppermute | solution.py:16
  179.4 7.4 collective-permute-done.25
  205.4 20.7 %collective-permute-done.30 = bf16[1024,256]{1,0:T(8,128)(2,1)} collective-permute-done((bf16[1024,256]{1,0:T(8,128)(2,1)}, bf16[1024,256]{1,0:T(8,128)(2,1)}, u32[]{:S(2)}, u32[]{:S(2)}) %collective-permute-start.30) | collective-permute-done | bytes 524320 | tf_op jit(solution)/shard_map/ppermute | solution.py:16
  242.1 11.6 %collective-permute-done.31 = bf16[256,2048]{1,0:T(8,128)(2,1)} collective-permute-done((bf16[256,2048]{1,0:T(8,128)(2,1)}, bf16[256,2048]{1,0:T(8,128)(2,1)}, u32[]{:S(2)}, u32[]{:S(2)}) %collective-permute-start.31) | collective-permute-done | bytes 1048608 | tf_op jit(solution)/shard_map/ppermute | solution.py:16
  256.3 10.4 %collective-permute-done.32 = bf16[1024,512]{1,0:T(8,128)(2,1)} collective-permute-done((bf16[1024,512]{1,0:T(8,128)(2,1)}, bf16[1024,512]{1,0:T(8,128)(2,1)}, u32[]{:S(2)}, u32[]{:S(2)}) %collective-permute-start.32) | collective-permute-done | bytes 1048608 | tf_op jit(solution)/shard_map/ppermute | solution.py:16
  275.5 10.7 %multiply_convert_fusion.5 = (bf16[1024,1024]{0,1:T(8,128)(2,1)}, f32[1024,1024]{0,1:T(8,128)}) fusion(f32[1024,1024]{0,1:T(8,128)S(1)} %fusion.6, bf16[1024,2048]{1,0:T(8,128)(2,1)S(1)} %pad_maximum_fusion.1, bf16[2048,2048]{1,0:T(8,128)(2,1)} %constant_dynamic-update-slice_fusion.48), kind=kOutput, calls=%fused_computation.27 | convolution fusion | flops 4301258752 | bytes 18874368 | tf_op jit(solution)/shard_map/dot_general | solution.py:133
  296.3 22.6 %collective-permute-done.33 = bf16[1024,512]{1,0:T(8,128)(2,1)S(1)} collective-permute-done((bf16[1024,512]{1,0:T(8,128)(2,1)}, bf16[1024,512]{1,0:T(8,128)(2,1)S(1)}, u32[]{:S(2)}, u32[]{:S(2)}) %collective-permute-start.33) | collective-permute-done | bytes 1048608 | tf_op jit(solution)/shard_map/ppermute | solution.py:16
  329.4 17.3 %collective-permute-done.36 = bf16[1024,512]{1,0:T(8,128)(2,1)S(1)} collective-permute-done((bf16[1024,512]{1,0:T(8,128)(2,1)S(1)}, bf16[1024,512]{1,0:T(8,128)(2,1)S(1)}, u32[]{:S(2)}, u32[]{:S(2)}) %collective-permute-start.36) | collective-permute-done | bytes 1048608 | tf_op jit(solution)/shard_map/ppermute | solution.py:16
  351.1 9.6 %multiply_convert_fusion.4 = (bf16[1024,1024]{0,1:T(8,128)(2,1)S(1)}, bf16[1024,1024]{0,1:T(8,128)(2,1)S(1)}) fusion(f32[1024,1024]{0,1:T(8,128)} %copy-done.117, f32[1024,1024]{0,1:T(8,128)} %get-tuple-element.458, bf16[1024,2048]{1,0:T(8,128)(2,1)S(1)} %pad_maximum_fusion.2, bf16[1024,2048]{1,0:T(8,128)(2,1)} %copy-done.88), kind=kOutput, calls=%fused_computation.26 | convolution fusion | flops 4308598784 | bytes 20971520 | tf_op jit(solution)/shard_map/dot_general | solution.py:133
  375.9 13.3 %fusion.147 = f32[1024,2048]{1,0:T(8,128)} fusion(bf16[1024,2048]{0,1:T(8,128)(2,1)S(1)} %pad_maximum_fusion.3, bf16[2048,2048]{1,0:T(8,128)(2,1)} %constant_dynamic-update-slice_fusion.48), kind=kOutput, calls=%fused_computation.548 | convolution fusion | flops 8589934592 | bytes 20971520 | tf_op jit(solution)/shard_map/dot_general | solution.py:133
  404.5 8.3 %fusion.2 = f32[1024,1024]{0,1:T(8,128)} fusion(bf16[1024,2048]{1,0:T(8,128)(2,1)S(1)} %pad_maximum_fusion.1, bf16[2048,2048]{1,0:T(8,128)(2,1)} %constant_dynamic-update-slice_fusion.58), kind=kOutput, calls=%fused_computation.6 | convolution fusion | flops 4294967296 | bytes 12582912 | tf_op jit(solution)/shard_map/dot_general | solution.py:133
  421.3 9.9 %multiply_convert_fusion.2 = (bf16[1024,1024]{0,1:T(8,128)(2,1)}, f32[1024,1024]{0,1:T(8,128)}) fusion(f32[1024,1024]{0,1:T(8,128)} %fusion.2, bf16[1024,2048]{1,0:T(8,128)(2,1)S(1)} %pad_maximum_fusion.1, bf16[2048,2048]{1,0:T(8,128)(2,1)} %constant_dynamic-update-slice_fusion.58), kind=kOutput, calls=%fused_computation.23 | convolution fusion | flops 4301258752 | bytes 18874368 | tf_op jit(solution)/shard_map/dot_general | solution.py:133
  447.2 8.1 %multiply_convert_fusion.1 = (bf16[1024,1024]{0,1:T(8,128)(2,1)S(1)}, bf16[1024,1024]{0,1:T(8,128)(2,1)S(1)}) fusion(f32[1024,1024]{0,1:T(8,128)S(1)} %copy-done.118, f32[1024,1024]{0,1:T(8,128)S(1)} %copy-done.119, bf16[1024,2048]{1,0:T(8,128)(2,1)S(1)} %pad_maximum_fusion.2, bf16[1024,2048]{1,0:T(8,128)(2,1)} %slice_dynamic-update-slice_fusion), kind=kOutput, calls=%fused_computation.22 | convolution fusion | flops 4308598784 | bytes 20971520 | tf_op jit(solution)/shard_map/dot_general | solution.py:133
  465.3 15.3 %convolution_add_fusion.1 = f32[1024,2048]{1,0:T(8,128)S(1)} fusion(f32[1024,2048]{1,0:T(8,128)} %fusion.147, bf16[1024,2048]{0,1:T(8,128)(2,1)} %pad_maximum_fusion.4, bf16[2048,2048]{1,0:T(8,128)(2,1)} %constant_dynamic-update-slice_fusion.58), kind=kOutput, calls=%fused_computation.35 | convolution fusion | flops 8592031744 | bytes 29360128 | tf_op jit(solution)/shard_map/dot_general | solution.py:133
  493.8 7.4 convolution_convert_fusion.1
  503.2 8.2 %collective-permute-done.48 = bf16[256,2048]{1,0:T(8,128)(2,1)} collective-permute-done((bf16[256,2048]{1,0:T(8,128)(2,1)}, bf16[256,2048]{1,0:T(8,128)(2,1)}, u32[]{:S(2)}, u32[]{:S(2)}) %collective-permute-start.48) | collective-permute-done | bytes 1048608 | tf_op jit(solution)/shard_map/ppermute | solution.py:16
  518.0 7.8 collective-permute-done.56
  543.6 11.6 %collective-permute-done.53 = bf16[256,2048]{1,0:T(8,128)(2,1)S(1)} collective-permute-done((bf16[256,2048]{1,0:T(8,128)(2,1)S(1)}, bf16[256,2048]{1,0:T(8,128)(2,1)S(1)}, u32[]{:S(2)}, u32[]{:S(2)}) %collective-permute-start.53) | collective-permute-done | bytes 1048608 | tf_op jit(solution)/shard_map/ppermute | solution.py:16
  561.2 8.8 %convolution_add_fusion = f32[1024,2048]{1,0:T(8,128)S(1)} fusion(f32[1024,2048]{1,0:T(8,128)} %fusion.146, bf16[1024,1024]{0,1:T(8,128)(2,1)S(1)} %copy-done.116, bf16[1024,2048]{1,0:T(8,128)(2,1)} %slice_dynamic-update-slice_fusion), kind=kOutput, calls=%fused_computation.30 | convolution fusion | flops 4297064448 | bytes 23068672 | tf_op jit(solution)/shard_map/dot_general | solution.py:133
  597.9 8.3 %collective-permute-done.65 = bf16[1024,256]{0,1:T(8,128)(2,1)S(1)} collective-permute-done((bf16[1024,256]{0,1:T(8,128)(2,1)S(1)}, bf16[1024,256]{0,1:T(8,128)(2,1)S(1)}, u32[]{:S(2)}, u32[]{:S(2)}) %collective-permute-start.65) | collective-permute-done | bytes 524320 | tf_op jit(solution)/shard_map/ppermute | solution.py:16
  611.8 7.5 bitcast_convert_fusion
  642.7 7.0 bitcast_add_fusion
  682.9 7.0 collective-permute-done.86
  733.0 10.2 %collective-permute-done.83 = bf16[3,256,512]{1,2,0:T(8,128)(2,1)} collective-permute-done((bf16[3,256,512]{1,2,0:T(8,128)(2,1)S(1)}, bf16[3,256,512]{1,2,0:T(8,128)(2,1)}, u32[]{:S(2)}, u32[]{:S(2)}) %collective-permute-start.83) | collective-permute-done | bytes 786464 | tf_op jit(solution)/shard_map/ppermute | solution.py:16
  762.8 7.3 collective-permute-done.92
  784.9 6.9 collective-permute-done.94
  (672 shorter events, 447.4 us)
Async XLA Ops:
  127.3 36.5 %collective-permute-start.20 = (bf16[256,2048]{1,0:T(8,128)(2,1)S(1)}, bf16[256,2048]{1,0:T(8,128)(2,1)}, u32[]{:S(2)}, u32[]{:S(2)}) collective-permute-start(bf16[256,2048]{1,0:T(8,128)(2,1)S(1)} %bitcast.165), channel_id=1, source_target_pairs={{0,1},{1,2},{2,3},{3,0},{4,5},{5,6},{6,7},{7,4},{8,9},{9,10},{10,1... | collective-permute-start | bytes 3145736 | tf_op jit(solution)/shard_map/ppermute | solution.py:16
  127.3 48.2 %collective-permute-start.24 = (bf16[256,2048]{1,0:T(8,128)(2,1)}, bf16[256,2048]{1,0:T(8,128)(2,1)}, u32[]{:S(2)}, u32[]{:S(2)}) collective-permute-start(bf16[256,2048]{1,0:T(8,128)(2,1)} %collective-permute-done.17), channel_id=1, source_target_pairs={{0,16},{16,0},{1,17},{17,1},{2,18},{18,2},{3,19},{19,3},{4,20},{20... | collective-permute-start | bytes 3145736 | tf_op jit(solution)/shard_map/ppermute | solution.py:16
  129.0 48.7 %collective-permute-start.23 = (bf16[256,2048]{1,0:T(8,128)(2,1)}, bf16[256,2048]{1,0:T(8,128)(2,1)}, u32[]{:S(2)}, u32[]{:S(2)}) collective-permute-start(bf16[256,2048]{1,0:T(8,128)(2,1)} %collective-permute-done.17), channel_id=1, source_target_pairs={{0,1},{1,2},{2,3},{3,0},{4,5},{5,6},{6,7},{7,4},{8,9},{9,10},{10,1... | collective-permute-start | bytes 3145736 | tf_op jit(solution)/shard_map/ppermute | solution.py:16
  133.5 53.2 %collective-permute-start.19 = (bf16[256,2048]{1,0:T(8,128)(2,1)}, bf16[256,2048]{1,0:T(8,128)(2,1)}, u32[]{:S(2)}, u32[]{:S(2)}) collective-permute-start(bf16[256,2048]{1,0:T(8,128)(2,1)} %slice.1081), channel_id=1, source_target_pairs={{0,8},{4,12},{8,0},{12,4},{1,9},{5,13},{9,1},{13,5},{2,10},{6,14},... | collective-permute-start | bytes 3145736 | tf_op jit(solution)/shard_map/ppermute | solution.py:21
  163.8 41.6 %collective-permute-start.27 = (bf16[256,2048]{1,0:T(8,128)(2,1)}, bf16[256,2048]{1,0:T(8,128)(2,1)}, u32[]{:S(2)}, u32[]{:S(2)}) collective-permute-start(bf16[256,2048]{1,0:T(8,128)(2,1)} %collective-permute-done.20), channel_id=1, source_target_pairs={{0,1},{1,2},{2,3},{3,0},{4,5},{5,6},{6,7},{7,4},{8,9},{9,10},{10,1... | collective-permute-start | bytes 3145736 | tf_op jit(solution)/shard_map/ppermute | solution.py:16
  177.7 50.7 %collective-permute-start.28 = (bf16[256,2048]{1,0:T(8,128)(2,1)}, bf16[256,2048]{1,0:T(8,128)(2,1)}, u32[]{:S(2)}, u32[]{:S(2)}) collective-permute-start(bf16[256,2048]{1,0:T(8,128)(2,1)} %collective-permute-done.23), channel_id=1, source_target_pairs={{0,16},{16,0},{1,17},{17,1},{2,18},{18,2},{3,19},{19,3},{4,20},{20... | collective-permute-start | bytes 3145736 | tf_op jit(solution)/shard_map/ppermute | solution.py:16
  186.8 41.6 %collective-permute-start.26 = (bf16[256,2048]{1,0:T(8,128)(2,1)}, bf16[256,2048]{1,0:T(8,128)(2,1)}, u32[]{:S(2)}, u32[]{:S(2)}) collective-permute-start(bf16[256,2048]{1,0:T(8,128)(2,1)} %collective-permute-done.23), channel_id=1, source_target_pairs={{0,1},{1,2},{2,3},{3,0},{4,5},{5,6},{6,7},{7,4},{8,9},{9,10},{10,1... | collective-permute-start | bytes 3145736 | tf_op jit(solution)/shard_map/ppermute | solution.py:16
  188.9 39.8 %collective-permute-start.22 = (bf16[256,2048]{1,0:T(8,128)(2,1)S(1)}, bf16[256,2048]{1,0:T(8,128)(2,1)}, u32[]{:S(2)}, u32[]{:S(2)}) collective-permute-start(bf16[256,2048]{1,0:T(8,128)(2,1)S(1)} %multiply_convert_fusion.7), channel_id=1, source_target_pairs={{0,8},{4,12},{8,0},{12,4},{1,9},{5,13},{9,1},{13,5},{2,10},{6,14},... | collective-permute-start | bytes 3145736 | tf_op jit(solution)/shard_map/ppermute | solution.py:21
  192.6 39.0 %all-to-all-start.1 = ((bf16[8,32,2048]{2,1,0:T(8,128)(2,1)}), bf16[8,32,2048]{2,1,0:T(8,128)(2,1)S(1)}, u32[]{:S(2)}, u32[]{:S(2)}) async-start(bf16[8,32,2048]{2,1,0:T(8,128)(2,1)} %bitcast.174), calls=%async_computation.1 | async-start | bytes 2097152 | tf_op jit(solution)/shard_map/all_to_all | solution.py:305
  205.4 83.1 %collective-permute-start.35 = (bf16[256,2048]{1,0:T(8,128)(2,1)}, bf16[256,2048]{1,0:T(8,128)(2,1)}, u32[]{:S(2)}, u32[]{:S(2)}) collective-permute-start(bf16[256,2048]{1,0:T(8,128)(2,1)} %collective-permute-done.27), channel_id=1, source_target_pairs={{0,1},{1,2},{2,3},{3,0},{4,5},{5,6},{6,7},{7,4},{8,9},{9,10},{10,1... | collective-permute-start | bytes 3145736 | tf_op jit(solution)/shard_map/ppermute | solution.py:16
  231.4 35.6 %collective-permute-start.29 = (bf16[512,2048]{1,0:T(8,128)(2,1)}, bf16[512,2048]{1,0:T(8,128)(2,1)}, u32[]{:S(2)}, u32[]{:S(2)}) collective-permute-start(bf16[512,2048]{1,0:T(8,128)(2,1)} %pad_maximum_fusion.9), channel_id=1, source_target_pairs={{0,4},{4,0},{8,12},{12,8},{1,5},{5,1},{9,13},{13,9},{2,6},{6,2},{1... | collective-permute-start | bytes 6291464 | tf_op jit(solution)/shard_map/ppermute | solution.py:21
  231.4 35.4 %collective-permute-start.32 = (bf16[1024,512]{1,0:T(8,128)(2,1)}, bf16[1024,512]{1,0:T(8,128)(2,1)}, u32[]{:S(2)}, u32[]{:S(2)}) collective-permute-start(bf16[1024,512]{1,0:T(8,128)(2,1)} %pad_maximum_fusion.13), channel_id=1, source_target_pairs={{0,1},{1,2},{2,3},{3,0},{4,5},{5,6},{6,7},{7,4},{8,9},{9,10},{10,1... | collective-permute-start | bytes 3145736 | tf_op jit(solution)/shard_map/ppermute | solution.py:16
  253.7 37.3 %collective-permute-start.38 = (bf16[256,2048]{1,0:T(8,128)(2,1)S(1)}, bf16[256,2048]{1,0:T(8,128)(2,1)S(1)}, u32[]{:S(2)}, u32[]{:S(2)}) collective-permute-start(bf16[256,2048]{1,0:T(8,128)(2,1)S(1)} %bitcast.167), channel_id=1, source_target_pairs={{0,16},{16,0},{1,17},{17,1},{2,18},{18,2},{3,19},{19,3},{4,20},{20... | collective-permute-start | bytes 3145736 | tf_op jit(solution)/shard_map/ppermute | solution.py:16
  286.2 36.4 %collective-permute-start.37 = (bf16[512,2048]{1,0:T(8,128)(2,1)S(1)}, bf16[512,2048]{1,0:T(8,128)(2,1)S(1)}, u32[]{:S(2)}, u32[]{:S(2)}) collective-permute-start(bf16[512,2048]{1,0:T(8,128)(2,1)S(1)} %pad_maximum_fusion.10), channel_id=1, source_target_pairs={{0,4},{4,0},{8,12},{12,8},{1,5},{5,1},{9,13},{13,9},{2,6},{6,2},{1... | collective-permute-start | bytes 6291464 | tf_op jit(solution)/shard_map/ppermute | solution.py:21
  318.9 55.2 %collective-permute-start.41 = (bf16[256,2048]{1,0:T(8,128)(2,1)}, bf16[256,2048]{1,0:T(8,128)(2,1)}, u32[]{:S(2)}, u32[]{:S(2)}) collective-permute-start(bf16[256,2048]{1,0:T(8,128)(2,1)} %collective-permute-done.27), channel_id=1, source_target_pairs={{0,16},{16,0},{1,17},{17,1},{2,18},{18,2},{3,19},{19,3},{4,20},{20... | collective-permute-start | bytes 3145736 | tf_op jit(solution)/shard_map/ppermute | solution.py:16
  320.6 47.6 %collective-permute-start.40 = (bf16[1024,512]{1,0:T(8,128)(2,1)S(1)}, bf16[1024,512]{1,0:T(8,128)(2,1)}, u32[]{:S(2)}, u32[]{:S(2)}) collective-permute-start(bf16[1024,512]{1,0:T(8,128)(2,1)S(1)} %collective-permute-done.39), channel_id=1, source_target_pairs={{0,1},{1,2},{2,3},{3,0},{4,5},{5,6},{6,7},{7,4},{8,9},{9,10},{10,1... | collective-permute-start | bytes 3145736 | tf_op jit(solution)/shard_map/ppermute | solution.py:16
  329.0 65.6 %collective-permute-start.43 = (bf16[256,2048]{1,0:T(8,128)(2,1)}, bf16[256,2048]{1,0:T(8,128)(2,1)}, u32[]{:S(2)}, u32[]{:S(2)}) collective-permute-start(bf16[256,2048]{1,0:T(8,128)(2,1)} %collective-permute-done.35), channel_id=1, source_target_pairs={{0,16},{16,0},{1,17},{17,1},{2,18},{18,2},{3,19},{19,3},{4,20},{20... | collective-permute-start | bytes 3145736 | tf_op jit(solution)/shard_map/ppermute | solution.py:16
  368.3 44.5 %collective-permute-start.50 = (bf16[1024,512]{1,0:T(8,128)(2,1)}, bf16[1024,512]{1,0:T(8,128)(2,1)}, u32[]{:S(2)}, u32[]{:S(2)}) collective-permute-start(bf16[1024,512]{1,0:T(8,128)(2,1)} %collective-permute-done.40), channel_id=1, source_target_pairs={{0,1},{1,2},{2,3},{3,0},{4,5},{5,6},{6,7},{7,4},{8,9},{9,10},{10,1... | collective-permute-start | bytes 3145736 | tf_op jit(solution)/shard_map/ppermute | solution.py:16
  394.7 52.1 %collective-permute-start.47 = (bf16[256,2048]{1,0:T(8,128)(2,1)}, bf16[256,2048]{1,0:T(8,128)(2,1)}, u32[]{:S(2)}, u32[]{:S(2)}) collective-permute-start(bf16[256,2048]{1,0:T(8,128)(2,1)} %get-tuple-element.199), channel_id=1, source_target_pairs={{0,16},{16,0},{1,17},{17,1},{2,18},{18,2},{3,19},{19,3},{4,20},{20... | collective-permute-start | bytes 3145736 | tf_op jit(solution)/shard_map/ppermute | solution.py:16
  395.0 36.2 %collective-permute-start.45 = (bf16[1024,512]{0,1:T(8,128)(2,1)S(1)}, bf16[1024,512]{0,1:T(8,128)(2,1)S(1)}, u32[]{:S(2)}, u32[]{:S(2)}) collective-permute-start(bf16[1024,512]{0,1:T(8,128)(2,1)S(1)} %pad_maximum_fusion.15), channel_id=1, source_target_pairs={{0,1},{1,2},{2,3},{3,0},{4,5},{5,6},{6,7},{7,4},{8,9},{9,10},{10,1... | collective-permute-start | bytes 3145736 | tf_op jit(solution)/shard_map/ppermute | solution.py:16
  400.5 87.1 %collective-permute-start.46 = (bf16[256,2048]{1,0:T(8,128)(2,1)}, bf16[256,2048]{1,0:T(8,128)(2,1)}, u32[]{:S(2)}, u32[]{:S(2)}) collective-permute-start(bf16[256,2048]{1,0:T(8,128)(2,1)} %get-tuple-element.201), channel_id=1, source_target_pairs={{0,16},{16,0},{1,17},{17,1},{2,18},{18,2},{3,19},{19,3},{4,20},{20... | collective-permute-start | bytes 3145736 | tf_op jit(solution)/shard_map/ppermute | solution.py:16
  432.6 52.3 %collective-permute-start.49 = (bf16[1024,512]{0,1:T(8,128)(2,1)}, bf16[1024,512]{0,1:T(8,128)(2,1)}, u32[]{:S(2)}, u32[]{:S(2)}) collective-permute-start(bf16[1024,512]{0,1:T(8,128)(2,1)} %add_convert_fusion.7), channel_id=1, source_target_pairs={{0,1},{1,2},{2,3},{3,0},{4,5},{5,6},{6,7},{7,4},{8,9},{9,10},{10,1... | collective-permute-start | bytes 3145736 | tf_op jit(solution)/shard_map/ppermute | solution.py:16
  446.8 40.8 %collective-permute-start.51 = (bf16[1024,512]{0,1:T(8,128)(2,1)}, bf16[1024,512]{0,1:T(8,128)(2,1)}, u32[]{:S(2)}, u32[]{:S(2)}) collective-permute-start(bf16[1024,512]{0,1:T(8,128)(2,1)} %concatenate.156), channel_id=1, source_target_pairs={{0,16},{16,0},{1,17},{17,1},{2,18},{18,2},{3,19},{19,3},{4,20},{20... | collective-permute-start | bytes 3145736 | tf_op jit(solution)/shard_map/ppermute | solution.py:16
  489.2 54.0 %collective-permute-start.61 = (bf16[1024,512]{0,1:T(8,128)(2,1)}, bf16[1024,512]{0,1:T(8,128)(2,1)}, u32[]{:S(2)}, u32[]{:S(2)}) collective-permute-start(bf16[1024,512]{0,1:T(8,128)(2,1)} %pad_maximum_fusion.16), channel_id=1, source_target_pairs={{0,16},{16,0},{1,17},{17,1},{2,18},{18,2},{3,19},{19,3},{4,20},{20... | collective-permute-start | bytes 3145736 | tf_op jit(solution)/shard_map/ppermute | solution.py:16
  489.6 49.7 %collective-permute-start.80 = (bf16[1024,512]{0,1:T(8,128)(2,1)}, bf16[1024,512]{0,1:T(8,128)(2,1)}, u32[]{:S(2)}, u32[]{:S(2)}) collective-permute-start(bf16[1024,512]{0,1:T(8,128)(2,1)} %add_convert_fusion.4), channel_id=1, source_target_pairs={{0,1},{1,2},{2,3},{3,0},{4,5},{5,6},{6,7},{7,4},{8,9},{9,10},{10,1... | collective-permute-start | bytes 3145736 | tf_op jit(solution)/shard_map/ppermute | solution.py:16
  515.6 39.6 %collective-permute-start.53 = (bf16[256,2048]{1,0:T(8,128)(2,1)S(1)}, bf16[256,2048]{1,0:T(8,128)(2,1)S(1)}, u32[]{:S(2)}, u32[]{:S(2)}) collective-permute-start(bf16[256,2048]{1,0:T(8,128)(2,1)S(1)} %add_convert_fusion.5), channel_id=1, source_target_pairs={{0,1},{1,2},{2,3},{3,0},{4,5},{5,6},{6,7},{7,4},{8,9},{9,10},{10,1... | collective-permute-start | bytes 3145736 | tf_op jit(solution)/shard_map/ppermute | solution.py:16
  537.6 85.7 %collective-permute-start.60 = (bf16[256,2048]{1,0:T(8,128)(2,1)}, bf16[256,2048]{1,0:T(8,128)(2,1)}, u32[]{:S(2)}, u32[]{:S(2)}) collective-permute-start(bf16[256,2048]{1,0:T(8,128)(2,1)} %get-tuple-element.214), channel_id=1, source_target_pairs={{0,16},{16,0},{1,17},{17,1},{2,18},{18,2},{3,19},{19,3},{4,20},{20... | collective-permute-start | bytes 3145736 | tf_op jit(solution)/shard_map/ppermute | solution.py:16
  543.2 49.2 %collective-permute-start.62 = (bf16[256,2048]{1,0:T(8,128)(2,1)}, bf16[256,2048]{1,0:T(8,128)(2,1)S(1)}, u32[]{:S(2)}, u32[]{:S(2)}) collective-permute-start(bf16[256,2048]{1,0:T(8,128)(2,1)} %get-tuple-element.233), channel_id=1, source_target_pairs={{0,16},{16,0},{1,17},{17,1},{2,18},{18,2},{3,19},{19,3},{4,20},{20... | collective-permute-start | bytes 3145736 | tf_op jit(solution)/shard_map/ppermute | solution.py:16
  623.3 43.0 %collective-permute-start.59 = (bf16[256,2048]{1,0:T(8,128)(2,1)S(1)}, bf16[256,2048]{1,0:T(8,128)(2,1)}, u32[]{:S(2)}, u32[]{:S(2)}) collective-permute-start(bf16[256,2048]{1,0:T(8,128)(2,1)S(1)} %slice.1079), channel_id=1, source_target_pairs={{0,8},{4,12},{8,0},{12,4},{1,9},{5,13},{9,1},{13,5},{2,10},{6,14},... | collective-permute-start | bytes 3145736 | tf_op jit(solution)/shard_map/ppermute | solution.py:21
  632.7 71.0 %collective-permute-start.97 = (f32[3,512]{1,0:T(4,128)}, f32[3,512]{1,0:T(4,128)}, u32[]{:S(2)}, u32[]{:S(2)}) collective-permute-start(f32[3,512]{1,0:T(4,128)} %fusion.195), channel_id=1, source_target_pairs={{0,2},{1,3},{2,0},{3,1},{4,6},{5,7},{6,4},{7,5},{8,10},{9,11},{10,... | collective-permute-start | bytes 18440 | tf_op jit(solution)/shard_map/ppermute | solution.py:21
  674.3 40.2 %collective-permute-start.85 = (bf16[3,256,512]{1,2,0:T(8,128)(2,1)}, bf16[3,256,512]{1,2,0:T(8,128)(2,1)}, u32[]{:S(2)}, u32[]{:S(2)}) collective-permute-start(bf16[3,256,512]{1,2,0:T(8,128)(2,1)} %get-tuple-element.258), channel_id=1, source_target_pairs={{0,16},{16,0},{1,17},{17,1},{2,18},{18,2},{3,19},{19,3},{4,20},{20... | collective-permute-start | bytes 2359304 | tf_op jit(solution)/shard_map/ppermute | solution.py:16
  727.7 51.7 %all-to-all-start.3 = ((bf16[8,32,2048]{2,1,0:T(8,128)(2,1)}), bf16[8,32,2048]{2,1,0:T(8,128)(2,1)S(1)}, u32[]{:S(2)}, u32[]{:S(2)}) async-start(bf16[8,32,2048]{2,1,0:T(8,128)(2,1)} %bitcast.60), calls=%async_computation.3 | async-start | bytes 2097152 | tf_op jit(solution)/shard_map/all_to_all | solution.py:305
  (191 other events, 3640.8 us)

commit v5 on v4

--- a/solution.py
+++ b/solution.py
@@ -324,9 +324,10 @@
     normed = gathering((token_rows * scale_mix * mixer_row).astype(bf16))
     next(normed)
     go(in_grp)
+    by_seq.depth = 2
     go(out_seq)
+    go(out_grp)
     by_grp.depth = 2
-    go(out_grp)
     go(out_grp)
     go(in_seq)
     next(normed)
@@ -388,8 +389,8 @@
     kept = stages.mark(matmul(kept, full_out))
     sent = stages.mark(matmul(sent, full_out).astype(bf16))
     branch = scattering(sent, kept)
+    go(gate_seq[0])
     go(gate_grp[0])
-    go(gate_seq[0])
     next(branch)
     next(branch)
     go(down_seq[0])
@@ -400,18 +401,19 @@
     go(down_seq[1])
     feed = gathering((hidden_state * scale_feed * feed_row).astype(bf16))
     go(gate_grp[0])
+    next(feed)
     by_seq.settle()
-    next(feed)
+    go(gate_grp[1])
     cot_got = stages.send(cot_sent, exchange)
-    go(gate_grp[1])
     go(gate_seq[0])
+    go(gate_seq[1])
     next(feed)
     feed_all = next(feed)
     go(down_grp[0])
     cot_rows = home_of(cot_got)
     cot = gathering(cot_rows)
+    go(gate_seq[1])
     by_grp.settle(2)
-    go(gate_seq[1])
     next(cot)
     by_grp.depth = 3
     full_gate, gate_part, up_part, activated = ({} for _ in range(4))
@@ -425,7 +427,6 @@
             (gate_part[h] * jax.nn.sigmoid(gate_part[h]) * up_part[h]).astype(bf16)
         )
     forward_half(0)
-    go(gate_seq[1])
     def backward_half(h):
         full_down[h] = whole(down_held[h], 1)
         act_grad = matmul(stages.tie(cot_all), full_down[h], contract_cols)
@@ -446,11 +447,11 @@
     down_first, down_then = down[0].grp_first(), down[1].grp()
     down_swap = down[1].seq(2)
     go(down_grp[0])
+    go(gate_seq[1])
     next(cot)
     go(down_grp[0])
-    go(gate_seq[1])
+    by_grp.settle(2)
     cot_all = next(cot)
-    by_grp.settle(2)
     rest(producing(down[0], activated[0], cot_all))
     go(gate_seq[1])
     by_seq.settle(2)
@@ -458,41 +459,41 @@
     go(down_grp[1])
     rest(down_grp[0])
     backward_half(0)
+    gating_work = producing(gating[0], feed_all, gates_grad[0])
     by_seq.settle(2)
-    gating_work = producing(gating[0], feed_all, gates_grad[0])
+    by_grp.depth = 3
     go(gating_work)
+    go(gating_seq[0])
     go(down_grp[1])
     go(gating_seq[0])
-    go(gating_seq[0])
-    by_grp.depth = 3
     rest(gate_seq[1])
     go(down_first)
     go(gating_seq[0])
+    forward_half(1)
     by_grp.depth = 1
-    forward_half(1)
+    rest(producing(down[1], activated[1], cot_all))
+    go(gating_work)
+    go(down_swap)
     go(down_first)
-    go(gating_work)
-    rest(producing(down[1], activated[1], cot_all))
-    go(down_swap)
     rest(down_grp[1])
     backward_half(1)
     go(down_first)
+    go(down_first)
     go(down_swap)
-    go(down_first)
     go(down_first)
     go(gating_seq[0])
     gating_work = producing(gating[1], feed_all, gates_grad[1])
     go(gating_work)
     by_seq.settle()
+    by_grp.depth = 3
     norm_grad = stages.mark(
         matmul(stages.tie(gates_grad[0]), full_gate[0], contract_cols)
     )
-    by_grp.depth = 3
     go(gating_work)
+    go(down_swap)
     norm_grad = stages.mark(
         norm_grad + matmul(stages.tie(gates_grad[1]), full_gate[1], contract_cols)
     )
-    go(down_swap)
     kept, sent = halves(norm_grad)
     feed_norm = scattering(sent, kept)
     next(feed_norm)
@@ -502,11 +503,11 @@
     by_grp.settle(2)
     by_grp.settle(2)
     by_grp.settle()
+    go(gating_grp[0])
     go(down_first)
-    go(gating_grp[0])
-    by_grp.depth = 1
     feed_norm_grad = next(feed_norm)
     go(gating_seq[1])
+    by_grp.depth = 1
     feed_hat = hidden_state * scale_feed
     feed_term = jnp.sum(feed_norm_grad * feed_hat, axis=0)
     feed_scaled = feed_norm_grad * feed_row
@@ -514,29 +515,28 @@
         feed_scaled - feed_hat * jnp.mean(feed_scaled * feed_hat, axis=-1, keepdims=True)
     )
     go(gating_grp[0])
-    by_grp.depth = 3
     branch_back = gathering(hidden_grad.astype(bf16))
     by_grp.depth = 2
     next(branch_back)
+    by_grp.depth = 3
+    go(down_then)
     by_seq.settle(2)
     fed = stages.mark(matmul(stages.tie(activated[0]), full_down[0]))
     go(gating_grp[0])
     rest(gating_grp[0])
     fed = stages.mark(fed + matmul(stages.tie(activated[1]), full_down[1]))
     by_grp.settle()
-    go(down_then)
     next(branch_back)
     branch_grad = next(branch_back)
     mixed_out_grad = matmul(stages.tie(branch_grad), full_out, contract_cols)
     kept, sent = halves(fed)
     feed_out = scattering(sent, kept)
-    by_seq.settle()
     next(feed_out)
     out_gate_grad = (mixed_out_grad * mixed).astype(bf16)
     mixed_grad = stages.mark((mixed_out_grad * out_gate).astype(bf16))
     heads = mixed_grad.reshape(wt_count, local_rows, channels)[:, :2]
+    by_seq.settle(2)
     by_seq.settle()
-    by_seq.settle(2)
     incoming = stages.send(taken(heads, row_of(0)), lambda v: passed_along(v, "seq", -1))
     out_sum, in_sum = Reduction(1), Reduction(1)
     out_swap, out_ring = out_sum.seq(), out_sum.grp()
@@ -545,14 +545,15 @@
     rest(producing(out_sum, mixed_out, branch_grad))
     next(feed_out)
     go(down_then)
+    by_seq.depth = 2
+    go(gating_seq[1])
     go(gating_seq[1])
     go(down_then)
-    go(gating_seq[1])
     rest(down_then)
     by_seq.settle()
+    by_grp.depth = 2
     go(gating_grp[1])
     heads = jnp.concatenate([heads, stages.tie(incoming)[None]], axis=0)
-    by_grp.depth = 2
     last = wt_count - 1
     behind = jnp.stack(
         [
@@ -582,15 +583,15 @@
             [(gated_low * values).astype(bf16), out_gate_grad, (gated_low * in_gate).astype(bf16)]
         )
     )
+    by_seq.settle(2)
     in_work = producing(in_sum, normed_all, projected_grad)
     kept, sent = halves(stages.tie(projected_grad), 1)
     by_seq.settle()
-    by_grp.depth = 2
     go(out_swap)
     sent = stages.mark(into_width(sent).astype(bf16))
     kept = stages.mark(into_width(kept))
+    by_grp.settle()
     by_grp.depth = 1
-    by_grp.settle()
     mix_norm = scattering(sent, kept)
     next(mix_norm)
     go(gating_grp[1])
@@ -617,19 +618,19 @@
     go(in_swap)
     go(out_ring)
     go(out_ring)
-    by_seq.settle()
     go(in_swap)
     go(out_ring)
+    by_seq.settle()
     rest(out_ring)
     block_out = arrived(block_got)
     gains = summed(relative(jnp.stack([mixer_term, feed_term])), ("wt", "seq", "grp"))
     taps_grad = summed(taps_term, ("seq", "grp"))
     tokens_grad = arrived(grad_got).astype(f32)
-    go(in_ring)
+    go(in_swap)
     go(in_ring)
     go(in_swap)
-    go(in_swap)
     by_grp.settle()
+    go(in_ring)
     go(in_ring)
     rest(in_ring)
     out_grad = out_sum.total

time: 808 us -> 794 us (0.983)
  starting transfers between devices: 99.4 us -> 89.2 us
    ppermute x73, starting transfers between devices: 60.8 us -> 51 us  [rotated(): lax.ppermute(array, axis, [(i, (i + by) % count) for i in range(count)])]
    ppermute x73, waiting for transfers between devices: 267 us -> 276 us  [rotated(): lax.ppermute(array, axis, [(i, (i + by) % count) for i in range(count)])]
    unnamed x287 -> x311, local copies, waits for them, and re-layouts: 66.5 us -> 67.4 us
  transfers between devices with their start and end apart: 103 -> 103, of which waited for: 43 -> 48; matrix products, arithmetic and copies ran while one was open for 47% -> 46% of each run, Pallas kernels for 0% -> 0%
where the time goes in v5:
time: 794 us; the launch traced here: 783 us
  waiting for transfers between devices  301 us (38%)
  matrix products  186 us (23%)
  local copies, waits for them, and re-layouts  103 us (13%)
  starting transfers between devices  89.2 us (11%)
  other arithmetic  88.2 us (11%)
  between operations  15.4 us (2%)
    ppermute x73, waiting for transfers between devices, rotated(): lax.ppermute(array, axis, [(i, (i + by) % count) for i in range(count)])  276 us
    dot_general x28, matrix products, matmul(): return lax.dot_general(left, right, dims, preferred_element_type=f32)  155 us
    unnamed x311, local copies, waits for them, and re-layouts  67.4 us
    ppermute x73, starting transfers between devices, rotated(): lax.ppermute(array, axis, [(i, (i + by) % count) for i in range(count)])  51 us
    convert_element_type x15, other arithmetic, grp(): got = by_grp.send(self.total.astype(bf16), 1)  27.4 us
    ppermute x24, starting transfers between devices, crossed(): return lax.ppermute(array, axis, [(i, i ^ by) for i in range(count)])  19.7 us
    ppermute x24, waiting for transfers between devices, crossed(): return lax.ppermute(array, axis, [(i, i ^ by) for i in range(count)])  16.8 us
  transfers between devices with their start and end apart: 103, of which 48 were waited for; matrix products, arithmetic and copies ran while one was open for 46% of the time, Pallas kernels for 0%

profile of v5, /device:TPU:0, one launch (start us, length us, event | category | flops | bytes accessed | tf_op | source)
XLA Modules:
  0.0 783.4 jit_solution(7517557348449640452)
XLA Ops:
  16.8 8.1 %collective-permute-done = bf16[3,256,512]{2,1,0:T(8,128)(2,1)} collective-permute-done((bf16[3,256,512]{2,1,0:T(8,128)(2,1)}, bf16[3,256,512]{2,1,0:T(8,128)(2,1)}, u32[]{:S(2)}, u32[]{:S(2)}) %collective-permute-start) | collective-permute-done | bytes 786464 | tf_op jit(solution)/shard_map/ppermute | solution.py:16
  25.4 8.1 %all-to-all-done = bf16[8,32,2048]{2,1,0:T(8,128)(2,1)S(1)} async-done(((bf16[8,32,2048]{2,1,0:T(8,128)(2,1)}), bf16[8,32,2048]{2,1,0:T(8,128)(2,1)S(1)}, u32[]{:S(2)}, u32[]{:S(2)}) %all-to-all-start) | async-done | bytes 1048608 | tf_op jit(solution)/shard_map/all_to_all | solution.py:305
  36.1 9.2 %collective-permute-done.1 = bf16[3,256,512]{2,1,0:T(8,128)(2,1)} collective-permute-done((bf16[3,256,512]{2,1,0:T(8,128)(2,1)}, bf16[3,256,512]{2,1,0:T(8,128)(2,1)}, u32[]{:S(2)}, u32[]{:S(2)}) %collective-permute-start.1) | collective-permute-done | bytes 786464 | tf_op jit(solution)/shard_map/ppermute | solution.py:16
  62.5 8.9 %collective-permute-done.6 = bf16[512,256]{1,0:T(8,128)(2,1)} collective-permute-done((bf16[512,256]{1,0:T(8,128)(2,1)S(1)}, bf16[512,256]{1,0:T(8,128)(2,1)}, u32[]{:S(2)}, u32[]{:S(2)}) %collective-permute-start.6) | collective-permute-done | bytes 262176 | tf_op jit(solution)/shard_map/ppermute | solution.py:16
  92.7 7.0 collective-permute-done.11
  137.1 16.0 %collective-permute-done.21 = bf16[256,2048]{1,0:T(8,128)(2,1)S(1)} collective-permute-done((bf16[256,2048]{1,0:T(8,128)(2,1)S(1)}, bf16[256,2048]{1,0:T(8,128)(2,1)S(1)}, u32[]{:S(2)}, u32[]{:S(2)}) %collective-permute-start.21) | collective-permute-done | bytes 1048608 | tf_op jit(solution)/shard_map/ppermute | solution.py:16
  164.9 12.9 %collective-permute-done.22 = bf16[256,2048]{1,0:T(8,128)(2,1)} collective-permute-done((bf16[256,2048]{1,0:T(8,128)(2,1)}, bf16[256,2048]{1,0:T(8,128)(2,1)}, u32[]{:S(2)}, u32[]{:S(2)}) %collective-permute-start.22) | collective-permute-done | bytes 1048608 | tf_op jit(solution)/shard_map/ppermute | solution.py:16
  179.5 7.3 collective-permute-done.24
  209.7 16.5 %collective-permute-done.29 = bf16[1024,256]{1,0:T(8,128)(2,1)} collective-permute-done((bf16[1024,256]{1,0:T(8,128)(2,1)}, bf16[1024,256]{1,0:T(8,128)(2,1)}, u32[]{:S(2)}, u32[]{:S(2)}) %collective-permute-start.29) | collective-permute-done | bytes 524320 | tf_op jit(solution)/shard_map/ppermute | solution.py:16
  242.3 11.6 %collective-permute-done.31 = bf16[256,2048]{1,0:T(8,128)(2,1)} collective-permute-done((bf16[256,2048]{1,0:T(8,128)(2,1)}, bf16[256,2048]{1,0:T(8,128)(2,1)}, u32[]{:S(2)}, u32[]{:S(2)}) %collective-permute-start.31) | collective-permute-done | bytes 1048608 | tf_op jit(solution)/shard_map/ppermute | solution.py:16
  256.5 10.4 %collective-permute-done.32 = bf16[1024,512]{1,0:T(8,128)(2,1)} collective-permute-done((bf16[1024,512]{1,0:T(8,128)(2,1)}, bf16[1024,512]{1,0:T(8,128)(2,1)}, u32[]{:S(2)}, u32[]{:S(2)}) %collective-permute-start.32) | collective-permute-done | bytes 1048608 | tf_op jit(solution)/shard_map/ppermute | solution.py:16
  270.9 8.3 %fusion.6 = f32[1024,1024]{0,1:T(8,128)} fusion(bf16[1024,2048]{1,0:T(8,128)(2,1)S(1)} %pad_maximum_fusion.1, bf16[2048,2048]{1,0:T(8,128)(2,1)} %constant_dynamic-update-slice_fusion.48), kind=kOutput, calls=%fused_computation.10 | convolution fusion | flops 4294967296 | bytes 12582912 | tf_op jit(solution)/shard_map/dot_general | solution.py:133
  279.2 9.4 %multiply_convert_fusion.5 = (bf16[1024,1024]{0,1:T(8,128)(2,1)S(1)}, f32[1024,1024]{0,1:T(8,128)}) fusion(f32[1024,1024]{0,1:T(8,128)} %fusion.6, bf16[1024,2048]{1,0:T(8,128)(2,1)S(1)} %pad_maximum_fusion.1, bf16[2048,2048]{1,0:T(8,128)(2,1)} %constant_dynamic-update-slice_fusion.48), kind=kOutput, calls=%fused_computation.27 | convolution fusion | flops 4301258752 | bytes 18874368 | tf_op jit(solution)/shard_map/dot_general | solution.py:133
  294.4 8.0 %collective-permute-done.42 = bf16[256,2048]{1,0:T(8,128)(2,1)S(1)} collective-permute-done((bf16[256,2048]{1,0:T(8,128)(2,1)}, bf16[256,2048]{1,0:T(8,128)(2,1)S(1)}, u32[]{:S(2)}, u32[]{:S(2)}) %collective-permute-start.42) | collective-permute-done | bytes 1048608 | tf_op jit(solution)/shard_map/ppermute | solution.py:16
  307.2 12.9 %collective-permute-done.33 = bf16[1024,512]{1,0:T(8,128)(2,1)S(1)} collective-permute-done((bf16[1024,512]{1,0:T(8,128)(2,1)}, bf16[1024,512]{1,0:T(8,128)(2,1)S(1)}, u32[]{:S(2)}, u32[]{:S(2)}) %collective-permute-start.33) | collective-permute-done | bytes 1048608 | tf_op jit(solution)/shard_map/ppermute | solution.py:16
  331.9 16.1 %collective-permute-done.37 = bf16[1024,512]{1,0:T(8,128)(2,1)S(1)} collective-permute-done((bf16[1024,512]{1,0:T(8,128)(2,1)S(1)}, bf16[1024,512]{1,0:T(8,128)(2,1)S(1)}, u32[]{:S(2)}, u32[]{:S(2)}) %collective-permute-start.37) | collective-permute-done | bytes 1048608 | tf_op jit(solution)/shard_map/ppermute | solution.py:16
  349.4 9.6 %multiply_convert_fusion.4 = (bf16[1024,1024]{0,1:T(8,128)(2,1)S(1)}, bf16[1024,1024]{0,1:T(8,128)(2,1)S(1)}) fusion(f32[1024,1024]{0,1:T(8,128)} %fusion.6, f32[1024,1024]{0,1:T(8,128)} %get-tuple-element.460, bf16[1024,2048]{1,0:T(8,128)(2,1)S(1)} %pad_maximum_fusion.2, bf16[1024,2048]{1,0:T(8,128)(2,1)S(1)} %slice_dynamic-update-slice_fusion.6), kind=kOutput, calls=%fused_computation.26 | convolution fusion | flops 4308598784 | bytes 20971520 | tf_op jit(solution)/shard_map/dot_general | solution.py:133
  361.6 7.1 convolution_convert_fusion.3
  371.2 13.7 %fusion.147 = f32[1024,2048]{1,0:T(8,128)} fusion(bf16[1024,2048]{0,1:T(8,128)(2,1)S(1)} %pad_maximum_fusion.3, bf16[2048,2048]{1,0:T(8,128)(2,1)} %constant_dynamic-update-slice_fusion.48), kind=kOutput, calls=%fused_computation.548 | convolution fusion | flops 8589934592 | bytes 20971520 | tf_op jit(solution)/shard_map/dot_general | solution.py:133
  399.8 8.3 %fusion.2 = f32[1024,1024]{0,1:T(8,128)} fusion(bf16[1024,2048]{1,0:T(8,128)(2,1)S(1)} %pad_maximum_fusion.1, bf16[2048,2048]{1,0:T(8,128)(2,1)} %constant_dynamic-update-slice_fusion.58), kind=kOutput, calls=%fused_computation.6 | convolution fusion | flops 4294967296 | bytes 12582912 | tf_op jit(solution)/shard_map/dot_general | solution.py:133
  408.0 9.4 %multiply_convert_fusion.2 = (bf16[1024,1024]{0,1:T(8,128)(2,1)S(1)}, f32[1024,1024]{0,1:T(8,128)}) fusion(f32[1024,1024]{0,1:T(8,128)} %fusion.2, bf16[1024,2048]{1,0:T(8,128)(2,1)S(1)} %pad_maximum_fusion.1, bf16[2048,2048]{1,0:T(8,128)(2,1)} %constant_dynamic-update-slice_fusion.58), kind=kOutput, calls=%fused_computation.23 | convolution fusion | flops 4301258752 | bytes 18874368 | tf_op jit(solution)/shard_map/dot_general | solution.py:133
  442.1 8.9 %multiply_convert_fusion.1 = (bf16[1024,1024]{0,1:T(8,128)(2,1)S(1)}, bf16[1024,1024]{0,1:T(8,128)(2,1)S(1)}) fusion(f32[1024,1024]{0,1:T(8,128)S(1)} %copy-done.129, f32[1024,1024]{0,1:T(8,128)} %get-tuple-element.462, bf16[1024,2048]{1,0:T(8,128)(2,1)S(1)} %pad_maximum_fusion.2, bf16[1024,2048]{1,0:T(8,128)(2,1)} %slice_dynamic-update-slice_fusion), kind=kOutput, calls=%fused_computation.22 | convolution fusion | flops 4308598784 | bytes 20971520 | tf_op jit(solution)/shard_map/dot_general | solution.py:133
  453.1 7.6 convolution_convert_fusion
  460.6 12.7 %convolution_add_fusion.1 = f32[1024,2048]{1,0:T(8,128)S(1)} fusion(f32[1024,2048]{1,0:T(8,128)} %fusion.147, bf16[1024,2048]{0,1:T(8,128)(2,1)S(1)} %pad_maximum_fusion.4, bf16[2048,2048]{1,0:T(8,128)(2,1)} %constant_dynamic-update-slice_fusion.58), kind=kOutput, calls=%fused_computation.35 | convolution fusion | flops 8592031744 | bytes 29360128 | tf_op jit(solution)/shard_map/dot_general | solution.py:133
  489.1 15.3 %collective-permute-done.48 = bf16[256,2048]{1,0:T(8,128)(2,1)} collective-permute-done((bf16[256,2048]{1,0:T(8,128)(2,1)}, bf16[256,2048]{1,0:T(8,128)(2,1)}, u32[]{:S(2)}, u32[]{:S(2)}) %collective-permute-start.48) | collective-permute-done | bytes 1048608 | tf_op jit(solution)/shard_map/ppermute | solution.py:16
  538.9 10.4 %collective-permute-done.53 = bf16[256,2048]{1,0:T(8,128)(2,1)S(1)} collective-permute-done((bf16[256,2048]{1,0:T(8,128)(2,1)S(1)}, bf16[256,2048]{1,0:T(8,128)(2,1)S(1)}, u32[]{:S(2)}, u32[]{:S(2)}) %collective-permute-start.53) | collective-permute-done | bytes 1048608 | tf_op jit(solution)/shard_map/ppermute | solution.py:16
  551.3 8.7 %convolution_add_fusion = f32[1024,2048]{1,0:T(8,128)S(1)} fusion(f32[1024,2048]{1,0:T(8,128)} %fusion.146, bf16[1024,1024]{0,1:T(8,128)(2,1)S(1)} %copy-done.128, bf16[1024,2048]{1,0:T(8,128)(2,1)} %slice_dynamic-update-slice_fusion), kind=kOutput, calls=%fused_computation.30 | convolution fusion | flops 4297064448 | bytes 23068672 | tf_op jit(solution)/shard_map/dot_general | solution.py:133
  581.5 11.8 %collective-permute-done.65 = bf16[1024,256]{0,1:T(8,128)(2,1)S(1)} collective-permute-done((bf16[1024,256]{0,1:T(8,128)(2,1)S(1)}, bf16[1024,256]{0,1:T(8,128)(2,1)S(1)}, u32[]{:S(2)}, u32[]{:S(2)}) %collective-permute-start.65) | collective-permute-done | bytes 524320 | tf_op jit(solution)/shard_map/ppermute | solution.py:16
  672.4 7.4 collective-permute-done.83
  705.1 7.5 collective-permute-done.87
  722.8 7.5 collective-permute-done.88
  771.9 7.5 collective-permute-done.93
  (697 shorter events, 443.9 us)
Async XLA Ops:
  0.7 35.4 %collective-permute-start.2 = (bf16[3,256,512]{2,1,0:T(8,128)(2,1)}, bf16[3,256,512]{2,1,0:T(8,128)(2,1)}, u32[]{:S(2)}, u32[]{:S(2)}) collective-permute-start(bf16[3,256,512]{2,1,0:T(8,128)(2,1)} %bitcast.185), channel_id=1, source_target_pairs={{0,16},{16,0},{1,17},{17,1},{2,18},{18,2},{3,19},{19,3},{4,20},{20... | collective-permute-start | bytes 2359304 | tf_op jit(solution)/shard_map/ppermute | solution.py:16
  127.4 50.4 %collective-permute-start.22 = (bf16[256,2048]{1,0:T(8,128)(2,1)}, bf16[256,2048]{1,0:T(8,128)(2,1)}, u32[]{:S(2)}, u32[]{:S(2)}) collective-permute-start(bf16[256,2048]{1,0:T(8,128)(2,1)} %collective-permute-done.17), channel_id=1, source_target_pairs={{0,1},{1,2},{2,3},{3,0},{4,5},{5,6},{6,7},{7,4},{8,9},{9,10},{10,1... | collective-permute-start | bytes 3145736 | tf_op jit(solution)/shard_map/ppermute | solution.py:16
  127.4 50.4 %collective-permute-start.23 = (bf16[256,2048]{1,0:T(8,128)(2,1)}, bf16[256,2048]{1,0:T(8,128)(2,1)}, u32[]{:S(2)}, u32[]{:S(2)}) collective-permute-start(bf16[256,2048]{1,0:T(8,128)(2,1)} %collective-permute-done.17), channel_id=1, source_target_pairs={{0,16},{16,0},{1,17},{17,1},{2,18},{18,2},{3,19},{19,3},{4,20},{20... | collective-permute-start | bytes 3145736 | tf_op jit(solution)/shard_map/ppermute | solution.py:16
  133.6 53.1 %collective-permute-start.19 = (bf16[256,2048]{1,0:T(8,128)(2,1)}, bf16[256,2048]{1,0:T(8,128)(2,1)}, u32[]{:S(2)}, u32[]{:S(2)}) collective-permute-start(bf16[256,2048]{1,0:T(8,128)(2,1)} %slice.1081), channel_id=1, source_target_pairs={{0,8},{4,12},{8,0},{12,4},{1,9},{5,13},{9,1},{13,5},{2,10},{6,14},... | collective-permute-start | bytes 3145736 | tf_op jit(solution)/shard_map/ppermute | solution.py:21
  164.9 35.4 %collective-permute-start.27 = (bf16[256,2048]{1,0:T(8,128)(2,1)}, bf16[256,2048]{1,0:T(8,128)(2,1)}, u32[]{:S(2)}, u32[]{:S(2)}) collective-permute-start(bf16[256,2048]{1,0:T(8,128)(2,1)} %collective-permute-done.20), channel_id=1, source_target_pairs={{0,1},{1,2},{2,3},{3,0},{4,5},{5,6},{6,7},{7,4},{8,9},{9,10},{10,1... | collective-permute-start | bytes 3145736 | tf_op jit(solution)/shard_map/ppermute | solution.py:16
  177.8 50.6 %collective-permute-start.28 = (bf16[256,2048]{1,0:T(8,128)(2,1)}, bf16[256,2048]{1,0:T(8,128)(2,1)}, u32[]{:S(2)}, u32[]{:S(2)}) collective-permute-start(bf16[256,2048]{1,0:T(8,128)(2,1)} %collective-permute-done.22), channel_id=1, source_target_pairs={{0,16},{16,0},{1,17},{17,1},{2,18},{18,2},{3,19},{19,3},{4,20},{20... | collective-permute-start | bytes 3145736 | tf_op jit(solution)/shard_map/ppermute | solution.py:16
  186.8 41.7 %collective-permute-start.26 = (bf16[256,2048]{1,0:T(8,128)(2,1)}, bf16[256,2048]{1,0:T(8,128)(2,1)}, u32[]{:S(2)}, u32[]{:S(2)}) collective-permute-start(bf16[256,2048]{1,0:T(8,128)(2,1)} %collective-permute-done.22), channel_id=1, source_target_pairs={{0,1},{1,2},{2,3},{3,0},{4,5},{5,6},{6,7},{7,4},{8,9},{9,10},{10,1... | collective-permute-start | bytes 3145736 | tf_op jit(solution)/shard_map/ppermute | solution.py:16
  190.4 38.1 %collective-permute-start.25 = (bf16[256,2048]{1,0:T(8,128)(2,1)S(1)}, bf16[256,2048]{1,0:T(8,128)(2,1)}, u32[]{:S(2)}, u32[]{:S(2)}) collective-permute-start(bf16[256,2048]{1,0:T(8,128)(2,1)S(1)} %multiply_convert_fusion.7), channel_id=1, source_target_pairs={{0,8},{4,12},{8,0},{12,4},{1,9},{5,13},{9,1},{13,5},{2,10},{6,14},... | collective-permute-start | bytes 3145736 | tf_op jit(solution)/shard_map/ppermute | solution.py:21
  207.3 81.3 %collective-permute-start.36 = (bf16[256,2048]{1,0:T(8,128)(2,1)}, bf16[256,2048]{1,0:T(8,128)(2,1)}, u32[]{:S(2)}, u32[]{:S(2)}) collective-permute-start(bf16[256,2048]{1,0:T(8,128)(2,1)} %collective-permute-done.27), channel_id=1, source_target_pairs={{0,1},{1,2},{2,3},{3,0},{4,5},{5,6},{6,7},{7,4},{8,9},{9,10},{10,1... | collective-permute-start | bytes 3145736 | tf_op jit(solution)/shard_map/ppermute | solution.py:16
  231.2 37.6 %collective-permute-start.30 = (bf16[512,2048]{1,0:T(8,128)(2,1)}, bf16[512,2048]{1,0:T(8,128)(2,1)}, u32[]{:S(2)}, u32[]{:S(2)}) collective-permute-start(bf16[512,2048]{1,0:T(8,128)(2,1)} %pad_maximum_fusion.9), channel_id=1, source_target_pairs={{0,4},{4,0},{8,12},{12,8},{1,5},{5,1},{9,13},{13,9},{2,6},{6,2},{1... | collective-permute-start | bytes 6291464 | tf_op jit(solution)/shard_map/ppermute | solution.py:21
  231.2 35.7 %collective-permute-start.32 = (bf16[1024,512]{1,0:T(8,128)(2,1)}, bf16[1024,512]{1,0:T(8,128)(2,1)}, u32[]{:S(2)}, u32[]{:S(2)}) collective-permute-start(bf16[1024,512]{1,0:T(8,128)(2,1)} %pad_maximum_fusion.13), channel_id=1, source_target_pairs={{0,1},{1,2},{2,3},{3,0},{4,5},{5,6},{6,7},{7,4},{8,9},{9,10},{10,1... | collective-permute-start | bytes 3145736 | tf_op jit(solution)/shard_map/ppermute | solution.py:16
  233.0 35.6 %collective-permute-start.34 = (bf16[256,2048]{1,0:T(8,128)(2,1)S(1)}, bf16[256,2048]{1,0:T(8,128)(2,1)S(1)}, u32[]{:S(2)}, u32[]{:S(2)}) collective-permute-start(bf16[256,2048]{1,0:T(8,128)(2,1)S(1)} %constant_dynamic-update-slice_fusion.40), channel_id=1, source_target_pairs={{0,8},{4,12},{8,0},{12,4},{1,9},{5,13},{9,1},{13,5},{2,10},{6,14},... | collective-permute-start | bytes 3145736 | tf_op jit(solution)/shard_map/ppermute | solution.py:21
  266.9 35.5 %collective-permute-start.42 = (bf16[256,2048]{1,0:T(8,128)(2,1)}, bf16[256,2048]{1,0:T(8,128)(2,1)S(1)}, u32[]{:S(2)}, u32[]{:S(2)}) collective-permute-start(bf16[256,2048]{1,0:T(8,128)(2,1)} %collective-permute-done.20), channel_id=1, source_target_pairs={{0,16},{16,0},{1,17},{17,1},{2,18},{18,2},{3,19},{19,3},{4,20},{20... | collective-permute-start | bytes 3145736 | tf_op jit(solution)/shard_map/ppermute | solution.py:16
  288.6 35.4 %collective-permute-start.38 = (bf16[512,2048]{1,0:T(8,128)(2,1)S(1)}, bf16[512,2048]{1,0:T(8,128)(2,1)S(1)}, u32[]{:S(2)}, u32[]{:S(2)}) collective-permute-start(bf16[512,2048]{1,0:T(8,128)(2,1)S(1)} %pad_maximum_fusion.10), channel_id=1, source_target_pairs={{0,4},{4,0},{8,12},{12,8},{1,5},{5,1},{9,13},{13,9},{2,6},{6,2},{1... | collective-permute-start | bytes 6291464 | tf_op jit(solution)/shard_map/ppermute | solution.py:21
  320.1 64.8 %collective-permute-start.40 = (bf16[1024,512]{1,0:T(8,128)(2,1)}, bf16[1024,512]{1,0:T(8,128)(2,1)S(1)}, u32[]{:S(2)}, u32[]{:S(2)}) collective-permute-start(bf16[1024,512]{1,0:T(8,128)(2,1)} %collective-permute-done.39), channel_id=1, source_target_pairs={{0,1},{1,2},{2,3},{3,0},{4,5},{5,6},{6,7},{7,4},{8,9},{9,10},{10,1... | collective-permute-start | bytes 3145736 | tf_op jit(solution)/shard_map/ppermute | solution.py:16
  331.2 58.0 %collective-permute-start.43 = (bf16[256,2048]{1,0:T(8,128)(2,1)}, bf16[256,2048]{1,0:T(8,128)(2,1)}, u32[]{:S(2)}, u32[]{:S(2)}) collective-permute-start(bf16[256,2048]{1,0:T(8,128)(2,1)} %collective-permute-done.36), channel_id=1, source_target_pairs={{0,16},{16,0},{1,17},{17,1},{2,18},{18,2},{3,19},{19,3},{4,20},{20... | collective-permute-start | bytes 3145736 | tf_op jit(solution)/shard_map/ppermute | solution.py:16
  384.9 40.9 %collective-permute-start.50 = (bf16[1024,512]{1,0:T(8,128)(2,1)S(1)}, bf16[1024,512]{1,0:T(8,128)(2,1)S(1)}, u32[]{:S(2)}, u32[]{:S(2)}) collective-permute-start(bf16[1024,512]{1,0:T(8,128)(2,1)S(1)} %collective-permute-done.40), channel_id=1, source_target_pairs={{0,1},{1,2},{2,3},{3,0},{4,5},{5,6},{6,7},{7,4},{8,9},{9,10},{10,1... | collective-permute-start | bytes 3145736 | tf_op jit(solution)/shard_map/ppermute | solution.py:16
  389.2 49.6 %collective-permute-start.46 = (bf16[256,2048]{1,0:T(8,128)(2,1)}, bf16[256,2048]{1,0:T(8,128)(2,1)}, u32[]{:S(2)}, u32[]{:S(2)}) collective-permute-start(bf16[256,2048]{1,0:T(8,128)(2,1)} %get-tuple-element.202), channel_id=1, source_target_pairs={{0,16},{16,0},{1,17},{17,1},{2,18},{18,2},{3,19},{19,3},{4,20},{20... | collective-permute-start | bytes 3145736 | tf_op jit(solution)/shard_map/ppermute | solution.py:16
  390.8 47.9 %collective-permute-start.47 = (bf16[1024,512]{0,1:T(8,128)(2,1)}, bf16[1024,512]{0,1:T(8,128)(2,1)S(1)}, u32[]{:S(2)}, u32[]{:S(2)}) collective-permute-start(bf16[1024,512]{0,1:T(8,128)(2,1)} %pad_maximum_fusion.15), channel_id=1, source_target_pairs={{0,1},{1,2},{2,3},{3,0},{4,5},{5,6},{6,7},{7,4},{8,9},{9,10},{10,1... | collective-permute-start | bytes 3145736 | tf_op jit(solution)/shard_map/ppermute | solution.py:16
  397.1 81.4 %collective-permute-start.45 = (bf16[256,2048]{1,0:T(8,128)(2,1)}, bf16[256,2048]{1,0:T(8,128)(2,1)}, u32[]{:S(2)}, u32[]{:S(2)}) collective-permute-start(bf16[256,2048]{1,0:T(8,128)(2,1)} %get-tuple-element.204), channel_id=1, source_target_pairs={{0,16},{16,0},{1,17},{17,1},{2,18},{18,2},{3,19},{19,3},{4,20},{20... | collective-permute-start | bytes 3145736 | tf_op jit(solution)/shard_map/ppermute | solution.py:16
  440.5 35.8 %collective-permute-start.49 = (bf16[1024,512]{0,1:T(8,128)(2,1)}, bf16[1024,512]{0,1:T(8,128)(2,1)}, u32[]{:S(2)}, u32[]{:S(2)}) collective-permute-start(bf16[1024,512]{0,1:T(8,128)(2,1)} %add_convert_fusion.5), channel_id=1, source_target_pairs={{0,1},{1,2},{2,3},{3,0},{4,5},{5,6},{6,7},{7,4},{8,9},{9,10},{10,1... | collective-permute-start | bytes 3145736 | tf_op jit(solution)/shard_map/ppermute | solution.py:16
  440.5 38.0 %collective-permute-start.51 = (bf16[1024,512]{0,1:T(8,128)(2,1)}, bf16[1024,512]{0,1:T(8,128)(2,1)}, u32[]{:S(2)}, u32[]{:S(2)}) collective-permute-start(bf16[1024,512]{0,1:T(8,128)(2,1)} %concatenate.156), channel_id=1, source_target_pairs={{0,16},{16,0},{1,17},{17,1},{2,18},{18,2},{3,19},{19,3},{4,20},{20... | collective-permute-start | bytes 3145736 | tf_op jit(solution)/shard_map/ppermute | solution.py:16
  478.9 51.9 %collective-permute-start.61 = (bf16[1024,512]{0,1:T(8,128)(2,1)}, bf16[1024,512]{0,1:T(8,128)(2,1)}, u32[]{:S(2)}, u32[]{:S(2)}) collective-permute-start(bf16[1024,512]{0,1:T(8,128)(2,1)} %pad_maximum_fusion.16), channel_id=1, source_target_pairs={{0,16},{16,0},{1,17},{17,1},{2,18},{18,2},{3,19},{19,3},{4,20},{20... | collective-permute-start | bytes 3145736 | tf_op jit(solution)/shard_map/ppermute | solution.py:16
  480.5 46.4 %collective-permute-start.63 = (bf16[1024,512]{0,1:T(8,128)(2,1)S(1)}, bf16[1024,512]{0,1:T(8,128)(2,1)}, u32[]{:S(2)}, u32[]{:S(2)}) collective-permute-start(bf16[1024,512]{0,1:T(8,128)(2,1)S(1)} %add_convert_fusion.4), channel_id=1, source_target_pairs={{0,1},{1,2},{2,3},{3,0},{4,5},{5,6},{6,7},{7,4},{8,9},{9,10},{10,1... | collective-permute-start | bytes 3145736 | tf_op jit(solution)/shard_map/ppermute | solution.py:16
  508.8 40.5 %collective-permute-start.53 = (bf16[256,2048]{1,0:T(8,128)(2,1)S(1)}, bf16[256,2048]{1,0:T(8,128)(2,1)S(1)}, u32[]{:S(2)}, u32[]{:S(2)}) collective-permute-start(bf16[256,2048]{1,0:T(8,128)(2,1)S(1)} %add_convert_fusion.6), channel_id=1, source_target_pairs={{0,1},{1,2},{2,3},{3,0},{4,5},{5,6},{6,7},{7,4},{8,9},{9,10},{10,1... | collective-permute-start | bytes 3145736 | tf_op jit(solution)/shard_map/ppermute | solution.py:16
  524.8 91.2 %collective-permute-start.60 = (bf16[256,2048]{1,0:T(8,128)(2,1)}, bf16[256,2048]{1,0:T(8,128)(2,1)}, u32[]{:S(2)}, u32[]{:S(2)}) collective-permute-start(bf16[256,2048]{1,0:T(8,128)(2,1)} %get-tuple-element.217), channel_id=1, source_target_pairs={{0,16},{16,0},{1,17},{17,1},{2,18},{18,2},{3,19},{19,3},{4,20},{20... | collective-permute-start | bytes 3145736 | tf_op jit(solution)/shard_map/ppermute | solution.py:16
  530.8 42.6 %collective-permute-start.62 = (bf16[256,2048]{1,0:T(8,128)(2,1)}, bf16[256,2048]{1,0:T(8,128)(2,1)S(1)}, u32[]{:S(2)}, u32[]{:S(2)}) collective-permute-start(bf16[256,2048]{1,0:T(8,128)(2,1)} %get-tuple-element.235), channel_id=1, source_target_pairs={{0,16},{16,0},{1,17},{17,1},{2,18},{18,2},{3,19},{19,3},{4,20},{20... | collective-permute-start | bytes 3145736 | tf_op jit(solution)/shard_map/ppermute | solution.py:16
  551.0 56.2 %collective-permute-start.97 = (bf16[256,2048]{1,0:T(8,128)(2,1)S(1)}, bf16[256,2048]{1,0:T(8,128)(2,1)S(1)}, u32[]{:S(2)}, u32[]{:S(2)}) collective-permute-start(bf16[256,2048]{1,0:T(8,128)(2,1)S(1)} %add_convert_fusion.3), channel_id=1, source_target_pairs={{0,1},{1,2},{2,3},{3,0},{4,5},{5,6},{6,7},{7,4},{8,9},{9,10},{10,1... | collective-permute-start | bytes 3145736 | tf_op jit(solution)/shard_map/ppermute | solution.py:16
  616.0 39.0 %collective-permute-start.59 = (bf16[256,2048]{1,0:T(8,128)(2,1)}, bf16[256,2048]{1,0:T(8,128)(2,1)S(1)}, u32[]{:S(2)}, u32[]{:S(2)}) collective-permute-start(bf16[256,2048]{1,0:T(8,128)(2,1)} %slice.1079), channel_id=1, source_target_pairs={{0,8},{4,12},{8,0},{12,4},{1,9},{5,13},{9,1},{13,5},{2,10},{6,14},... | collective-permute-start | bytes 3145736 | tf_op jit(solution)/shard_map/ppermute | solution.py:21
  620.0 71.4 %collective-permute-start.96 = (f32[3,512]{1,0:T(4,128)S(1)}, f32[3,512]{1,0:T(4,128)S(1)}, u32[]{:S(2)}, u32[]{:S(2)}) collective-permute-start(f32[3,512]{1,0:T(4,128)S(1)} %fusion.195), channel_id=1, source_target_pairs={{0,2},{1,3},{2,0},{3,1},{4,6},{5,7},{6,4},{7,5},{8,10},{9,11},{10,... | collective-permute-start | bytes 18440 | tf_op jit(solution)/shard_map/ppermute | solution.py:21
  663.8 36.4 %collective-permute-start.81 = (bf16[3,256,512]{1,2,0:T(8,128)(2,1)}, bf16[3,256,512]{1,2,0:T(8,128)(2,1)}, u32[]{:S(2)}, u32[]{:S(2)}) collective-permute-start(bf16[3,256,512]{1,2,0:T(8,128)(2,1)} %get-tuple-element.257), channel_id=1, source_target_pairs={{0,16},{16,0},{1,17},{17,1},{2,18},{18,2},{3,19},{19,3},{4,20},{20... | collective-permute-start | bytes 2359304 | tf_op jit(solution)/shard_map/ppermute | solution.py:16
  715.8 46.3 %all-to-all-start.3 = ((bf16[8,32,2048]{2,1,0:T(8,128)(2,1)}), bf16[8,32,2048]{2,1,0:T(8,128)(2,1)S(1)}, u32[]{:S(2)}, u32[]{:S(2)}) async-start(bf16[8,32,2048]{2,1,0:T(8,128)(2,1)} %bitcast.60), calls=%async_computation.3 | async-start | bytes 2097152 | tf_op jit(solution)/shard_map/all_to_all | solution.py:305
  (203 other events, 3475.9 us)

commit v6 on v5

--- a/solution.py
+++ b/solution.py
@@ -283,8 +283,10 @@
     in_seq, out_seq = seq_steps(in_held), seq_steps(out_held)
     gate_seq = [seq_steps(held) for held in gate_held]
     down_seq = [seq_steps(held, [0]) for held in down_held]
+    go(in_grp)
+    by_seq.depth = 2
     go(in_seq)
-    go(in_grp)
+    by_grp.depth = 2
     order_row = order[0]
     slot_blocks = order_row.reshape(peers, local_rows)
     here_positions = lax.dynamic_index_in_dim(slot_blocks, block_index, 0, keepdims=False)
@@ -306,7 +308,6 @@
     by_grp.depth = 2
     tokens_got = stages.send(select_rows(send_matrix, tokens[0], plain), exchange)
     home_matrix = stages.mark(matmul(stages.tie(home_hot), arrival_hot, contract_rows).astype(bf16))
-    by_seq.depth = 2
     cot_sent = stages.mark(select_rows(send_matrix, stages.tie(cotangent[0]), plain))
     def home_of(got):
         return relative(select_rows(home_matrix, stages.tie(got), plain))
@@ -321,27 +322,27 @@
     scale_mix = rms_scale(token_rows)
     go(in_seq)
     go(in_seq)
+    go(in_grp)
     normed = gathering((token_rows * scale_mix * mixer_row).astype(bf16))
     next(normed)
-    go(in_grp)
     by_seq.depth = 2
+    by_grp.depth = 2
     go(out_seq)
     go(out_grp)
-    by_grp.depth = 2
+    go(in_seq)
     go(out_grp)
-    go(in_seq)
+    by_grp.depth = 3
     next(normed)
     normed_all = next(normed)
+    go(out_seq)
     span_rows = normed_all.shape[0]
-    go(out_seq)
     go(out_grp)
     full_in = whole(in_held, 1)
     go(gate_grp[0])
-    go(gate_grp[1])
     in_source = stages.tie(normed_all)
     in_gate, out_gate, values = (matmul(in_source, full_in[k]) for k in range(3))
+    by_seq.depth = 2
     gated = stages.mark((in_gate * values).astype(bf16))
-    go(out_seq)
     rel = peer_order(wt_count)
     place_of = jnp.array([rel.index(j) for j in range(wt_count)] + [wt_count], dtype=jnp.int32)
     block_at = [wt_at ^ j for j in rel]
@@ -350,11 +351,13 @@
     def row_of(block):
         return place_of[wt_at ^ block]
     tails = gated.reshape(wt_count, local_rows, channels)[:, -2:]
+    go(gate_grp[1])
     carried = stages.send(
         taken(tails, row_of(wt_count - 1)), lambda v: passed_along(v, "seq", 1)
     )
-    by_grp.depth = 3
     tails = jnp.concatenate([tails, stages.tie(carried)[None]], axis=0)
+    go(out_seq)
+    by_grp.depth = 3
     go(out_seq)
     before = jnp.stack(
         [
@@ -381,41 +384,43 @@
     mixed = (taps[2] * now + mask_one * taps[1] * one_back + mask_two * taps[0] * two_back).reshape(
         span_rows, channels
     )
-    go(gate_seq[0])
-    by_grp.settle()
     mixed_out = stages.mark((out_gate * mixed).astype(bf16))
     full_out = whole(out_held, 1)
     kept, sent = halves(stages.tie(mixed_out))
+    go(gate_seq[0])
+    by_grp.settle()
     kept = stages.mark(matmul(kept, full_out))
     sent = stages.mark(matmul(sent, full_out).astype(bf16))
+    go(gate_seq[0])
     branch = scattering(sent, kept)
-    go(gate_seq[0])
     go(gate_grp[0])
     next(branch)
     next(branch)
+    go(gate_grp[1])
     go(down_seq[0])
-    go(gate_grp[1])
+    go(gate_seq[0])
     hidden_state = token_rows + next(branch)
-    go(gate_seq[0])
     scale_feed = rms_scale(hidden_state)
+    by_seq.settle()
     go(down_seq[1])
     feed = gathering((hidden_state * scale_feed * feed_row).astype(bf16))
     go(gate_grp[0])
     next(feed)
-    by_seq.settle()
     go(gate_grp[1])
     cot_got = stages.send(cot_sent, exchange)
+    by_grp.depth = 3
+    by_grp.settle(2)
     go(gate_seq[0])
-    go(gate_seq[1])
     next(feed)
     feed_all = next(feed)
+    go(gate_seq[1])
     go(down_grp[0])
     cot_rows = home_of(cot_got)
     cot = gathering(cot_rows)
     go(gate_seq[1])
     by_grp.settle(2)
+    by_grp.depth = 3
     next(cot)
-    by_grp.depth = 3
     full_gate, gate_part, up_part, activated = ({} for _ in range(4))
     full_down, gates_grad = {}, {}
     def forward_half(h):
@@ -446,46 +451,50 @@
     gating_seq, gating_grp = [g.seq() for g in gating], [g.grp() for g in gating]
     down_first, down_then = down[0].grp_first(), down[1].grp()
     down_swap = down[1].seq(2)
+    next(cot)
+    cot_all = next(cot)
+    go(gate_seq[1])
     go(down_grp[0])
-    go(gate_seq[1])
-    next(cot)
     go(down_grp[0])
     by_grp.settle(2)
-    cot_all = next(cot)
     rest(producing(down[0], activated[0], cot_all))
     go(gate_seq[1])
     by_seq.settle(2)
     go(down_grp[1])
     go(down_grp[1])
+    by_seq.settle(2)
     rest(down_grp[0])
     backward_half(0)
+    go(down_grp[1])
     gating_work = producing(gating[0], feed_all, gates_grad[0])
     by_seq.settle(2)
     by_grp.depth = 3
+    by_grp.depth = 3
     go(gating_work)
     go(gating_seq[0])
-    go(down_grp[1])
     go(gating_seq[0])
     rest(gate_seq[1])
     go(down_first)
-    go(gating_seq[0])
     forward_half(1)
+    rest(producing(down[1], activated[1], cot_all))
     by_grp.depth = 1
-    rest(producing(down[1], activated[1], cot_all))
-    go(gating_work)
     go(down_swap)
     go(down_first)
+    go(gating_seq[0])
+    by_grp.depth = 1
+    go(gating_work)
     rest(down_grp[1])
     backward_half(1)
     go(down_first)
     go(down_first)
     go(down_swap)
-    go(down_first)
     go(gating_seq[0])
     gating_work = producing(gating[1], feed_all, gates_grad[1])
+    by_grp.settle()
     go(gating_work)
+    go(down_first)
+    by_grp.depth = 3
     by_seq.settle()
-    by_grp.depth = 3
     norm_grad = stages.mark(
         matmul(stages.tie(gates_grad[0]), full_gate[0], contract_cols)
     )
@@ -496,17 +505,17 @@
     )
     kept, sent = halves(norm_grad)
     feed_norm = scattering(sent, kept)
+    go(down_swap)
     next(feed_norm)
+    go(down_first)
     next(feed_norm)
-    go(down_swap)
     go(gating_seq[1])
     by_grp.settle(2)
+    go(gating_grp[0])
+    by_grp.settle()
     by_grp.settle(2)
-    by_grp.settle()
-    go(gating_grp[0])
-    go(down_first)
+    go(gating_seq[1])
     feed_norm_grad = next(feed_norm)
-    go(gating_seq[1])
     by_grp.depth = 1
     feed_hat = hidden_state * scale_feed
     feed_term = jnp.sum(feed_norm_grad * feed_hat, axis=0)
@@ -514,11 +523,11 @@
     hidden_grad = cot_rows.astype(f32) + scale_feed * (
         feed_scaled - feed_hat * jnp.mean(feed_scaled * feed_hat, axis=-1, keepdims=True)
     )
+    branch_back = gathering(hidden_grad.astype(bf16))
+    by_grp.depth = 3
     go(gating_grp[0])
-    branch_back = gathering(hidden_grad.astype(bf16))
     by_grp.depth = 2
     next(branch_back)
-    by_grp.depth = 3
     go(down_then)
     by_seq.settle(2)
     fed = stages.mark(matmul(stages.tie(activated[0]), full_down[0]))
@@ -531,27 +540,26 @@
     mixed_out_grad = matmul(stages.tie(branch_grad), full_out, contract_cols)
     kept, sent = halves(fed)
     feed_out = scattering(sent, kept)
+    by_seq.settle()
     next(feed_out)
     out_gate_grad = (mixed_out_grad * mixed).astype(bf16)
     mixed_grad = stages.mark((mixed_out_grad * out_gate).astype(bf16))
     heads = mixed_grad.reshape(wt_count, local_rows, channels)[:, :2]
     by_seq.settle(2)
-    by_seq.settle()
     incoming = stages.send(taken(heads, row_of(0)), lambda v: passed_along(v, "seq", -1))
     out_sum, in_sum = Reduction(1), Reduction(1)
     out_swap, out_ring = out_sum.seq(), out_sum.grp()
     in_swap, in_ring = in_sum.seq(), in_sum.grp()
-    by_grp.depth = 2
     rest(producing(out_sum, mixed_out, branch_grad))
     next(feed_out)
+    by_grp.depth = 2
     go(down_then)
-    by_seq.depth = 2
-    go(gating_seq[1])
+    by_grp.depth = 2
     go(gating_seq[1])
     go(down_then)
+    go(gating_seq[1])
     rest(down_then)
     by_seq.settle()
-    by_grp.depth = 2
     go(gating_grp[1])
     heads = jnp.concatenate([heads, stages.tie(incoming)[None]], axis=0)
     last = wt_count - 1
@@ -583,14 +591,15 @@
             [(gated_low * values).astype(bf16), out_gate_grad, (gated_low * in_gate).astype(bf16)]
         )
     )
-    by_seq.settle(2)
+    by_grp.depth = 2
     in_work = producing(in_sum, normed_all, projected_grad)
     kept, sent = halves(stages.tie(projected_grad), 1)
+    by_seq.settle(2)
     by_seq.settle()
+    by_grp.settle()
     go(out_swap)
+    kept = stages.mark(into_width(kept))
     sent = stages.mark(into_width(sent).astype(bf16))
-    kept = stages.mark(into_width(kept))
-    by_grp.settle()
     by_grp.depth = 1
     mix_norm = scattering(sent, kept)
     next(mix_norm)
@@ -602,8 +611,8 @@
     go(out_swap)
     go(out_swap)
     go(gating_grp[1])
+    by_grp.settle(2)
     mix_norm_grad = next(mix_norm)
-    by_grp.settle(2)
     block_got = to_arrival((hidden_state + next(feed_out)).astype(bf16))
     rest(gating_grp[1])
     mix_hat = token_rows * scale_mix
@@ -612,12 +621,13 @@
     grad_home = hidden_grad + scale_mix * (
         mix_scaled - mix_hat * jnp.mean(mix_scaled * mix_hat, axis=-1, keepdims=True)
     )
+    go(out_ring)
     grad_got = to_arrival(grad_home.astype(bf16))
     down[0].seq_last()
     by_seq.settle()
     go(in_swap)
     go(out_ring)
-    go(out_ring)
+    go(in_swap)
     go(in_swap)
     go(out_ring)
     by_seq.settle()
@@ -626,10 +636,8 @@
     gains = summed(relative(jnp.stack([mixer_term, feed_term])), ("wt", "seq", "grp"))
     taps_grad = summed(taps_term, ("seq", "grp"))
     tokens_grad = arrived(grad_got).astype(f32)
-    go(in_swap)
     go(in_ring)
     go(in_swap)
-    by_grp.settle()
     go(in_ring)
     go(in_ring)
     rest(in_ring)

time: 794 us -> 795 us (level)
  matrix products: 186 us -> 198 us
  waiting for transfers between devices: 301 us -> 289 us
  starting transfers between devices: 89.2 us -> 98.7 us
    ppermute x73, starting transfers between devices: 51 us -> 63.7 us  [rotated(): lax.ppermute(array, axis, [(i, (i + by) % count) for i in range(count)])]
    ppermute x73, waiting for transfers between devices: 276 us -> 264 us  [rotated(): lax.ppermute(array, axis, [(i, (i + by) % count) for i in range(count)])]
    unnamed x311 -> x303, local copies, waits for them, and re-layouts: 67.4 us -> 63.5 us
  transfers between devices with their start and end apart: 103 -> 103, of which waited for: 48 -> 47; matrix products, arithmetic and copies ran while one was open for 46% -> 47% of each run, Pallas kernels for 0% -> 0%
where the time goes in v6:
time: 795 us; the launch traced here: 785 us
  waiting for transfers between devices  289 us (36%)
  matrix products  198 us (25%)
  starting transfers between devices  98.7 us (12%)
  local copies, waits for them, and re-layouts  97.5 us (12%)
  other arithmetic  86.9 us (11%)
  between operations  15.1 us (2%)
    ppermute x73, waiting for transfers between devices, rotated(): lax.ppermute(array, axis, [(i, (i + by) % count) for i in range(count)])  264 us
    dot_general x28, matrix products, matmul(): return lax.dot_general(left, right, dims, preferred_element_type=f32)  162 us
    ppermute x73, starting transfers between devices, rotated(): lax.ppermute(array, axis, [(i, (i + by) % count) for i in range(count)])  63.7 us
    unnamed x303, local copies, waits for them, and re-layouts  63.5 us
    convert_element_type x15, other arithmetic, grp(): got = by_grp.send(self.total.astype(bf16), 1)  24 us
  transfers between devices with their start and end apart: 103, of which 47 were waited for; matrix products, arithmetic and copies ran while one was open for 47% of the time, Pallas kernels for 0%

profile of v6, /device:TPU:0, one launch (start us, length us, event | category | flops | bytes accessed | tf_op | source)
XLA Modules:
  0.0 784.7 jit_solution(14808329030860724786)
XLA Ops:
  16.8 6.8 collective-permute-done
  25.1 10.5 %all-to-all-done = bf16[8,32,2048]{2,1,0:T(8,128)(2,1)S(1)} async-done(((bf16[8,32,2048]{2,1,0:T(8,128)(2,1)}), bf16[8,32,2048]{2,1,0:T(8,128)(2,1)S(1)}, u32[]{:S(2)}, u32[]{:S(2)}) %all-to-all-start) | async-done | bytes 1048608 | tf_op jit(solution)/shard_map/all_to_all | solution.py:307
  91.0 9.2 %collective-permute-done.13 = bf16[512,256]{1,0:T(8,128)(2,1)S(1)} collective-permute-done((bf16[512,256]{1,0:T(8,128)(2,1)S(1)}, bf16[512,256]{1,0:T(8,128)(2,1)S(1)}, u32[]{:S(2)}, u32[]{:S(2)}) %collective-permute-start.13) | collective-permute-done | bytes 262176 | tf_op jit(solution)/shard_map/ppermute | solution.py:16
  136.3 19.1 %collective-permute-done.21 = bf16[256,2048]{1,0:T(8,128)(2,1)S(1)} collective-permute-done((bf16[256,2048]{1,0:T(8,128)(2,1)S(1)}, bf16[256,2048]{1,0:T(8,128)(2,1)S(1)}, u32[]{:S(2)}, u32[]{:S(2)}) %collective-permute-start.21) | collective-permute-done | bytes 1048608 | tf_op jit(solution)/shard_map/ppermute | solution.py:16
  167.1 10.9 %collective-permute-done.20 = bf16[256,2048]{1,0:T(8,128)(2,1)} collective-permute-done((bf16[256,2048]{1,0:T(8,128)(2,1)}, bf16[256,2048]{1,0:T(8,128)(2,1)}, u32[]{:S(2)}, u32[]{:S(2)}) %collective-permute-start.20) | collective-permute-done | bytes 1048608 | tf_op jit(solution)/shard_map/ppermute | solution.py:16
  178.3 9.1 %collective-permute-done.24 = bf16[1024,256]{1,0:T(8,128)(2,1)S(1)} collective-permute-done((bf16[1024,256]{1,0:T(8,128)(2,1)S(1)}, bf16[1024,256]{1,0:T(8,128)(2,1)S(1)}, u32[]{:S(2)}, u32[]{:S(2)}) %collective-permute-start.24) | collective-permute-done | bytes 524320 | tf_op jit(solution)/shard_map/ppermute | solution.py:16
  209.8 17.0 %collective-permute-done.30 = bf16[1024,256]{1,0:T(8,128)(2,1)} collective-permute-done((bf16[1024,256]{1,0:T(8,128)(2,1)}, bf16[1024,256]{1,0:T(8,128)(2,1)}, u32[]{:S(2)}, u32[]{:S(2)}) %collective-permute-start.30) | collective-permute-done | bytes 524320 | tf_op jit(solution)/shard_map/ppermute | solution.py:16
  243.6 10.8 %collective-permute-done.31 = bf16[256,2048]{1,0:T(8,128)(2,1)} collective-permute-done((bf16[256,2048]{1,0:T(8,128)(2,1)}, bf16[256,2048]{1,0:T(8,128)(2,1)}, u32[]{:S(2)}, u32[]{:S(2)}) %collective-permute-start.31) | collective-permute-done | bytes 1048608 | tf_op jit(solution)/shard_map/ppermute | solution.py:16
  257.0 10.4 %collective-permute-done.32 = bf16[1024,512]{1,0:T(8,128)(2,1)} collective-permute-done((bf16[1024,512]{1,0:T(8,128)(2,1)}, bf16[1024,512]{1,0:T(8,128)(2,1)}, u32[]{:S(2)}, u32[]{:S(2)}) %collective-permute-start.32) | collective-permute-done | bytes 1048608 | tf_op jit(solution)/shard_map/ppermute | solution.py:16
  270.1 8.3 %fusion.6 = f32[1024,1024]{0,1:T(8,128)} fusion(bf16[1024,2048]{1,0:T(8,128)(2,1)S(1)} %pad_maximum_fusion.1, bf16[2048,2048]{1,0:T(8,128)(2,1)} %constant_dynamic-update-slice_fusion.48), kind=kOutput, calls=%fused_computation.10 | convolution fusion | flops 4294967296 | bytes 12582912 | tf_op jit(solution)/shard_map/dot_general | solution.py:133
  278.4 9.8 %multiply_convert_fusion.5 = (bf16[1024,1024]{0,1:T(8,128)(2,1)}, f32[1024,1024]{0,1:T(8,128)}) fusion(f32[1024,1024]{0,1:T(8,128)} %fusion.6, bf16[1024,2048]{1,0:T(8,128)(2,1)S(1)} %pad_maximum_fusion.1, bf16[2048,2048]{1,0:T(8,128)(2,1)} %constant_dynamic-update-slice_fusion.48), kind=kOutput, calls=%fused_computation.27 | convolution fusion | flops 4301258752 | bytes 18874368 | tf_op jit(solution)/shard_map/dot_general | solution.py:133
  295.3 7.7 collective-permute-done.40
  307.7 12.7 %collective-permute-done.35 = bf16[1024,512]{1,0:T(8,128)(2,1)S(1)} collective-permute-done((bf16[1024,512]{1,0:T(8,128)(2,1)}, bf16[1024,512]{1,0:T(8,128)(2,1)S(1)}, u32[]{:S(2)}, u32[]{:S(2)}) %collective-permute-start.35) | collective-permute-done | bytes 1048608 | tf_op jit(solution)/shard_map/ppermute | solution.py:16
  331.5 16.7 %collective-permute-done.37 = bf16[1024,512]{1,0:T(8,128)(2,1)S(1)} collective-permute-done((bf16[1024,512]{1,0:T(8,128)(2,1)S(1)}, bf16[1024,512]{1,0:T(8,128)(2,1)S(1)}, u32[]{:S(2)}, u32[]{:S(2)}) %collective-permute-start.37) | collective-permute-done | bytes 1048608 | tf_op jit(solution)/shard_map/ppermute | solution.py:16
  349.6 9.6 %multiply_convert_fusion.4 = (bf16[1024,1024]{0,1:T(8,128)(2,1)S(1)}, bf16[1024,1024]{0,1:T(8,128)(2,1)S(1)}) fusion(f32[1024,1024]{0,1:T(8,128)} %fusion.6, f32[1024,1024]{0,1:T(8,128)} %get-tuple-element.452, bf16[1024,2048]{1,0:T(8,128)(2,1)S(1)} %pad_maximum_fusion.2, bf16[1024,2048]{1,0:T(8,128)(2,1)S(1)} %slice_dynamic-update-slice_fusion.6), kind=kOutput, calls=%fused_computation.26 | convolution fusion | flops 4308598784 | bytes 20971520 | tf_op jit(solution)/shard_map/dot_general | solution.py:133
  359.8 14.3 %fusion.147 = f32[1024,2048]{1,0:T(8,128)} fusion(bf16[1024,2048]{0,1:T(8,128)(2,1)S(1)} %pad_maximum_fusion.3, bf16[2048,2048]{1,0:T(8,128)(2,1)} %constant_dynamic-update-slice_fusion.48), kind=kOutput, calls=%fused_computation.548 | convolution fusion | flops 8589934592 | bytes 20971520 | tf_op jit(solution)/shard_map/dot_general | solution.py:133
  390.0 8.7 %fusion.2 = f32[1024,1024]{0,1:T(8,128)} fusion(bf16[1024,2048]{1,0:T(8,128)(2,1)S(1)} %pad_maximum_fusion.1, bf16[2048,2048]{1,0:T(8,128)(2,1)} %constant_dynamic-update-slice_fusion.58), kind=kOutput, calls=%fused_computation.6 | convolution fusion | flops 4294967296 | bytes 12582912 | tf_op jit(solution)/shard_map/dot_general | solution.py:133
  398.8 9.4 %multiply_convert_fusion.2 = (bf16[1024,1024]{0,1:T(8,128)(2,1)S(1)}, f32[1024,1024]{0,1:T(8,128)}) fusion(f32[1024,1024]{0,1:T(8,128)} %fusion.2, bf16[1024,2048]{1,0:T(8,128)(2,1)S(1)} %pad_maximum_fusion.1, bf16[2048,2048]{1,0:T(8,128)(2,1)} %constant_dynamic-update-slice_fusion.58), kind=kOutput, calls=%fused_computation.23 | convolution fusion | flops 4301258752 | bytes 18874368 | tf_op jit(solution)/shard_map/dot_general | solution.py:133
  439.4 10.3 %multiply_convert_fusion.1 = (bf16[1024,1024]{0,1:T(8,128)(2,1)S(1)}, bf16[1024,1024]{0,1:T(8,128)(2,1)S(1)}) fusion(f32[1024,1024]{0,1:T(8,128)S(1)} %copy-done.127, f32[1024,1024]{0,1:T(8,128)} %get-tuple-element.454, bf16[1024,2048]{1,0:T(8,128)(2,1)S(1)} %pad_maximum_fusion.2, bf16[1024,2048]{1,0:T(8,128)(2,1)} %slice_dynamic-update-slice_fusion), kind=kOutput, calls=%fused_computation.22 | convolution fusion | flops 4308598784 | bytes 20971520 | tf_op jit(solution)/shard_map/dot_general | solution.py:133
  459.2 15.3 %convolution_add_fusion.1 = f32[1024,2048]{1,0:T(8,128)S(1)} fusion(f32[1024,2048]{1,0:T(8,128)} %fusion.147, bf16[1024,2048]{0,1:T(8,128)(2,1)} %pad_maximum_fusion.4, bf16[2048,2048]{1,0:T(8,128)(2,1)} %constant_dynamic-update-slice_fusion.58), kind=kOutput, calls=%fused_computation.35 | convolution fusion | flops 8592031744 | bytes 29360128 | tf_op jit(solution)/shard_map/dot_general | solution.py:133
  477.2 7.4 convolution_convert_fusion.1
  496.2 7.9 %collective-permute-done.47 = bf16[256,2048]{1,0:T(8,128)(2,1)} collective-permute-done((bf16[256,2048]{1,0:T(8,128)(2,1)S(1)}, bf16[256,2048]{1,0:T(8,128)(2,1)}, u32[]{:S(2)}, u32[]{:S(2)}) %collective-permute-start.47) | collective-permute-done | bytes 1048608 | tf_op jit(solution)/shard_map/ppermute | solution.py:16
  519.5 8.4 %fusion.146 = f32[1024,2048]{1,0:T(8,128)} fusion(bf16[1024,1024]{0,1:T(8,128)(2,1)} %get-tuple-element.188, bf16[1024,2048]{1,0:T(8,128)(2,1)S(1)} %copy-done.101), kind=kOutput, calls=%fused_computation.547 | convolution fusion | flops 4294967296 | bytes 14680064 | tf_op jit(solution)/shard_map/dot_general | solution.py:133
  540.1 8.8 %collective-permute-done.53 = bf16[256,2048]{1,0:T(8,128)(2,1)S(1)} collective-permute-done((bf16[256,2048]{1,0:T(8,128)(2,1)S(1)}, bf16[256,2048]{1,0:T(8,128)(2,1)S(1)}, u32[]{:S(2)}, u32[]{:S(2)}) %collective-permute-start.53) | collective-permute-done | bytes 1048608 | tf_op jit(solution)/shard_map/ppermute | solution.py:16
  552.4 10.3 %convolution_add_fusion = f32[1024,2048]{1,0:T(8,128)S(1)} fusion(f32[1024,2048]{1,0:T(8,128)} %fusion.146, bf16[1024,1024]{0,1:T(8,128)(2,1)} %copy-done.126, bf16[1024,2048]{1,0:T(8,128)(2,1)} %slice_dynamic-update-slice_fusion), kind=kOutput, calls=%fused_computation.30 | convolution fusion | flops 4297064448 | bytes 23068672 | tf_op jit(solution)/shard_map/dot_general | solution.py:133
  585.2 8.2 %collective-permute-done.64 = bf16[1024,256]{0,1:T(8,128)(2,1)S(1)} collective-permute-done((bf16[1024,256]{0,1:T(8,128)(2,1)S(1)}, bf16[1024,256]{0,1:T(8,128)(2,1)S(1)}, u32[]{:S(2)}, u32[]{:S(2)}) %collective-permute-start.64) | collective-permute-done | bytes 524320 | tf_op jit(solution)/shard_map/ppermute | solution.py:16
  598.3 7.6 bitcast_convert_fusion
  630.1 7.0 bitcast_add_fusion
  637.9 7.1 collective-permute-done.71
  672.5 7.8 collective-permute-done.75
  722.0 8.8 %collective-permute-done.89 = bf16[3,256,512]{1,2,0:T(8,128)(2,1)S(1)} collective-permute-done((bf16[3,256,512]{1,2,0:T(8,128)(2,1)S(1)}, bf16[3,256,512]{1,2,0:T(8,128)(2,1)S(1)}, u32[]{:S(2)}, u32[]{:S(2)}) %collective-permute-start.89) | collective-permute-done | bytes 786464 | tf_op jit(solution)/shard_map/ppermute | solution.py:16
  767.2 11.3 %collective-permute-done.90 = bf16[3,256,512]{1,2,0:T(8,128)(2,1)} collective-permute-done((bf16[3,256,512]{1,2,0:T(8,128)(2,1)}, bf16[3,256,512]{1,2,0:T(8,128)(2,1)}, u32[]{:S(2)}, u32[]{:S(2)}) %collective-permute-start.90) | collective-permute-done | bytes 786464 | tf_op jit(solution)/shard_map/ppermute | solution.py:16
  (688 shorter events, 442.4 us)
Async XLA Ops:
  90.9 36.6 %collective-permute-start.17 = (bf16[256,2048]{1,0:T(8,128)(2,1)S(1)}, bf16[256,2048]{1,0:T(8,128)(2,1)}, u32[]{:S(2)}, u32[]{:S(2)}) collective-permute-start(bf16[256,2048]{1,0:T(8,128)(2,1)S(1)} %bitcast.168), channel_id=1, source_target_pairs={{0,1},{1,2},{2,3},{3,0},{4,5},{5,6},{6,7},{7,4},{8,9},{9,10},{10,1... | collective-permute-start | bytes 3145736 | tf_op jit(solution)/shard_map/ppermute | solution.py:16
  128.0 49.9 %collective-permute-start.20 = (bf16[256,2048]{1,0:T(8,128)(2,1)}, bf16[256,2048]{1,0:T(8,128)(2,1)}, u32[]{:S(2)}, u32[]{:S(2)}) collective-permute-start(bf16[256,2048]{1,0:T(8,128)(2,1)} %collective-permute-done.17), channel_id=1, source_target_pairs={{0,1},{1,2},{2,3},{3,0},{4,5},{5,6},{6,7},{7,4},{8,9},{9,10},{10,1... | collective-permute-start | bytes 3145736 | tf_op jit(solution)/shard_map/ppermute | solution.py:16
  128.4 49.6 %collective-permute-start.23 = (bf16[256,2048]{1,0:T(8,128)(2,1)}, bf16[256,2048]{1,0:T(8,128)(2,1)}, u32[]{:S(2)}, u32[]{:S(2)}) collective-permute-start(bf16[256,2048]{1,0:T(8,128)(2,1)} %collective-permute-done.17), channel_id=1, source_target_pairs={{0,16},{16,0},{1,17},{17,1},{2,18},{18,2},{3,19},{19,3},{4,20},{20... | collective-permute-start | bytes 3145736 | tf_op jit(solution)/shard_map/ppermute | solution.py:16
  134.2 53.6 %collective-permute-start.19 = (bf16[256,2048]{1,0:T(8,128)(2,1)}, bf16[256,2048]{1,0:T(8,128)(2,1)}, u32[]{:S(2)}, u32[]{:S(2)}) collective-permute-start(bf16[256,2048]{1,0:T(8,128)(2,1)} %slice.1081), channel_id=1, source_target_pairs={{0,8},{4,12},{8,0},{12,4},{1,9},{5,13},{9,1},{13,5},{2,10},{6,14},... | collective-permute-start | bytes 3145736 | tf_op jit(solution)/shard_map/ppermute | solution.py:21
  178.0 51.2 %collective-permute-start.27 = (bf16[256,2048]{1,0:T(8,128)(2,1)}, bf16[256,2048]{1,0:T(8,128)(2,1)}, u32[]{:S(2)}, u32[]{:S(2)}) collective-permute-start(bf16[256,2048]{1,0:T(8,128)(2,1)} %collective-permute-done.20), channel_id=1, source_target_pairs={{0,16},{16,0},{1,17},{17,1},{2,18},{18,2},{3,19},{19,3},{4,20},{20... | collective-permute-start | bytes 3145736 | tf_op jit(solution)/shard_map/ppermute | solution.py:16
  187.4 41.8 %collective-permute-start.26 = (bf16[256,2048]{1,0:T(8,128)(2,1)}, bf16[256,2048]{1,0:T(8,128)(2,1)}, u32[]{:S(2)}, u32[]{:S(2)}) collective-permute-start(bf16[256,2048]{1,0:T(8,128)(2,1)} %collective-permute-done.20), channel_id=1, source_target_pairs={{0,1},{1,2},{2,3},{3,0},{4,5},{5,6},{6,7},{7,4},{8,9},{9,10},{10,1... | collective-permute-start | bytes 3145736 | tf_op jit(solution)/shard_map/ppermute | solution.py:16
  191.3 37.8 %collective-permute-start.25 = (bf16[256,2048]{1,0:T(8,128)(2,1)S(1)}, bf16[256,2048]{1,0:T(8,128)(2,1)}, u32[]{:S(2)}, u32[]{:S(2)}) collective-permute-start(bf16[256,2048]{1,0:T(8,128)(2,1)S(1)} %multiply_convert_fusion.7), channel_id=1, source_target_pairs={{0,8},{4,12},{8,0},{12,4},{1,9},{5,13},{9,1},{13,5},{2,10},{6,14},... | collective-permute-start | bytes 3145736 | tf_op jit(solution)/shard_map/ppermute | solution.py:21
  207.5 80.7 %collective-permute-start.36 = (bf16[256,2048]{1,0:T(8,128)(2,1)}, bf16[256,2048]{1,0:T(8,128)(2,1)}, u32[]{:S(2)}, u32[]{:S(2)}) collective-permute-start(bf16[256,2048]{1,0:T(8,128)(2,1)} %collective-permute-done.29), channel_id=1, source_target_pairs={{0,1},{1,2},{2,3},{3,0},{4,5},{5,6},{6,7},{7,4},{8,9},{9,10},{10,1... | collective-permute-start | bytes 3145736 | tf_op jit(solution)/shard_map/ppermute | solution.py:16
  231.9 36.2 %collective-permute-start.28 = (bf16[512,2048]{1,0:T(8,128)(2,1)}, bf16[512,2048]{1,0:T(8,128)(2,1)}, u32[]{:S(2)}, u32[]{:S(2)}) collective-permute-start(bf16[512,2048]{1,0:T(8,128)(2,1)} %pad_maximum_fusion.9), channel_id=1, source_target_pairs={{0,4},{4,0},{8,12},{12,8},{1,5},{5,1},{9,13},{13,9},{2,6},{6,2},{1... | collective-permute-start | bytes 6291464 | tf_op jit(solution)/shard_map/ppermute | solution.py:21
  231.9 35.5 %collective-permute-start.32 = (bf16[1024,512]{1,0:T(8,128)(2,1)}, bf16[1024,512]{1,0:T(8,128)(2,1)}, u32[]{:S(2)}, u32[]{:S(2)}) collective-permute-start(bf16[1024,512]{1,0:T(8,128)(2,1)} %pad_maximum_fusion.13), channel_id=1, source_target_pairs={{0,1},{1,2},{2,3},{3,0},{4,5},{5,6},{6,7},{7,4},{8,9},{9,10},{10,1... | collective-permute-start | bytes 3145736 | tf_op jit(solution)/shard_map/ppermute | solution.py:16
  254.4 38.1 %collective-permute-start.34 = (bf16[256,2048]{1,0:T(8,128)(2,1)S(1)}, bf16[256,2048]{1,0:T(8,128)(2,1)S(1)}, u32[]{:S(2)}, u32[]{:S(2)}) collective-permute-start(bf16[256,2048]{1,0:T(8,128)(2,1)S(1)} %bitcast.167), channel_id=1, source_target_pairs={{0,16},{16,0},{1,17},{17,1},{2,18},{18,2},{3,19},{19,3},{4,20},{20... | collective-permute-start | bytes 3145736 | tf_op jit(solution)/shard_map/ppermute | solution.py:16
  267.4 35.5 %collective-permute-start.40 = (bf16[256,2048]{1,0:T(8,128)(2,1)S(1)}, bf16[256,2048]{1,0:T(8,128)(2,1)S(1)}, u32[]{:S(2)}, u32[]{:S(2)}) collective-permute-start(bf16[256,2048]{1,0:T(8,128)(2,1)S(1)} %copy-done.67), channel_id=1, source_target_pairs={{0,16},{16,0},{1,17},{17,1},{2,18},{18,2},{3,19},{19,3},{4,20},{20... | collective-permute-start | bytes 3145736 | tf_op jit(solution)/shard_map/ppermute | solution.py:16
  267.7 36.3 %collective-permute-start.42 = (bf16[1024,512]{1,0:T(8,128)(2,1)S(1)}, bf16[1024,512]{1,0:T(8,128)(2,1)}, u32[]{:S(2)}, u32[]{:S(2)}) collective-permute-start(bf16[1024,512]{1,0:T(8,128)(2,1)S(1)} %copy-done.71), channel_id=1, source_target_pairs={{0,1},{1,2},{2,3},{3,0},{4,5},{5,6},{6,7},{7,4},{8,9},{9,10},{10,1... | collective-permute-start | bytes 3145736 | tf_op jit(solution)/shard_map/ppermute | solution.py:16
  288.2 36.1 %collective-permute-start.38 = (bf16[512,2048]{1,0:T(8,128)(2,1)S(1)}, bf16[512,2048]{1,0:T(8,128)(2,1)S(1)}, u32[]{:S(2)}, u32[]{:S(2)}) collective-permute-start(bf16[512,2048]{1,0:T(8,128)(2,1)S(1)} %pad_maximum_fusion.10), channel_id=1, source_target_pairs={{0,4},{4,0},{8,12},{12,8},{1,5},{5,1},{9,13},{13,9},{2,6},{6,2},{1... | collective-permute-start | bytes 6291464 | tf_op jit(solution)/shard_map/ppermute | solution.py:21
  320.4 60.1 %collective-permute-start.48 = (bf16[1024,512]{1,0:T(8,128)(2,1)}, bf16[1024,512]{1,0:T(8,128)(2,1)S(1)}, u32[]{:S(2)}, u32[]{:S(2)}) collective-permute-start(bf16[1024,512]{1,0:T(8,128)(2,1)} %collective-permute-done.42), channel_id=1, source_target_pairs={{0,1},{1,2},{2,3},{3,0},{4,5},{5,6},{6,7},{7,4},{8,9},{9,10},{10,1... | collective-permute-start | bytes 3145736 | tf_op jit(solution)/shard_map/ppermute | solution.py:16
  330.8 56.6 %collective-permute-start.41 = (bf16[256,2048]{1,0:T(8,128)(2,1)}, bf16[256,2048]{1,0:T(8,128)(2,1)}, u32[]{:S(2)}, u32[]{:S(2)}) collective-permute-start(bf16[256,2048]{1,0:T(8,128)(2,1)} %collective-permute-done.36), channel_id=1, source_target_pairs={{0,16},{16,0},{1,17},{17,1},{2,18},{18,2},{3,19},{19,3},{4,20},{20... | collective-permute-start | bytes 3145736 | tf_op jit(solution)/shard_map/ppermute | solution.py:16
  380.4 36.8 %collective-permute-start.49 = (bf16[1024,512]{1,0:T(8,128)(2,1)S(1)}, bf16[1024,512]{1,0:T(8,128)(2,1)S(1)}, u32[]{:S(2)}, u32[]{:S(2)}) collective-permute-start(bf16[1024,512]{1,0:T(8,128)(2,1)S(1)} %collective-permute-done.48), channel_id=1, source_target_pairs={{0,1},{1,2},{2,3},{3,0},{4,5},{5,6},{6,7},{7,4},{8,9},{9,10},{10,1... | collective-permute-start | bytes 3145736 | tf_op jit(solution)/shard_map/ppermute | solution.py:16
  387.4 40.4 %collective-permute-start.43 = (bf16[1024,512]{0,1:T(8,128)(2,1)S(1)}, bf16[1024,512]{0,1:T(8,128)(2,1)S(1)}, u32[]{:S(2)}, u32[]{:S(2)}) collective-permute-start(bf16[1024,512]{0,1:T(8,128)(2,1)S(1)} %pad_maximum_fusion.14), channel_id=1, source_target_pairs={{0,1},{1,2},{2,3},{3,0},{4,5},{5,6},{6,7},{7,4},{8,9},{9,10},{10,1... | collective-permute-start | bytes 3145736 | tf_op jit(solution)/shard_map/ppermute | solution.py:16
  387.4 43.7 %collective-permute-start.45 = (bf16[256,2048]{1,0:T(8,128)(2,1)}, bf16[256,2048]{1,0:T(8,128)(2,1)}, u32[]{:S(2)}, u32[]{:S(2)}) collective-permute-start(bf16[256,2048]{1,0:T(8,128)(2,1)} %get-tuple-element.192), channel_id=1, source_target_pairs={{0,16},{16,0},{1,17},{17,1},{2,18},{18,2},{3,19},{19,3},{4,20},{20... | collective-permute-start | bytes 3145736 | tf_op jit(solution)/shard_map/ppermute | solution.py:16
  415.4 71.0 %collective-permute-start.51 = (bf16[1024,512]{0,1:T(8,128)(2,1)}, bf16[1024,512]{0,1:T(8,128)(2,1)}, u32[]{:S(2)}, u32[]{:S(2)}) collective-permute-start(bf16[1024,512]{0,1:T(8,128)(2,1)} %concatenate.156), channel_id=1, source_target_pairs={{0,16},{16,0},{1,17},{17,1},{2,18},{18,2},{3,19},{19,3},{4,20},{20... | collective-permute-start | bytes 3145736 | tf_op jit(solution)/shard_map/ppermute | solution.py:16
  431.1 55.4 %collective-permute-start.46 = (bf16[256,2048]{1,0:T(8,128)(2,1)}, bf16[256,2048]{1,0:T(8,128)(2,1)}, u32[]{:S(2)}, u32[]{:S(2)}) collective-permute-start(bf16[256,2048]{1,0:T(8,128)(2,1)} %get-tuple-element.200), channel_id=1, source_target_pairs={{0,16},{16,0},{1,17},{17,1},{2,18},{18,2},{3,19},{19,3},{4,20},{20... | collective-permute-start | bytes 3145736 | tf_op jit(solution)/shard_map/ppermute | solution.py:16
  432.8 51.9 %collective-permute-start.50 = (bf16[1024,512]{0,1:T(8,128)(2,1)}, bf16[1024,512]{0,1:T(8,128)(2,1)}, u32[]{:S(2)}, u32[]{:S(2)}) collective-permute-start(bf16[1024,512]{0,1:T(8,128)(2,1)} %add_convert_fusion.7), channel_id=1, source_target_pairs={{0,1},{1,2},{2,3},{3,0},{4,5},{5,6},{6,7},{7,4},{8,9},{9,10},{10,1... | collective-permute-start | bytes 3145736 | tf_op jit(solution)/shard_map/ppermute | solution.py:16
  490.5 44.6 %collective-permute-start.61 = (bf16[1024,512]{0,1:T(8,128)(2,1)S(1)}, bf16[1024,512]{0,1:T(8,128)(2,1)S(1)}, u32[]{:S(2)}, u32[]{:S(2)}) collective-permute-start(bf16[1024,512]{0,1:T(8,128)(2,1)S(1)} %copy-done.70), channel_id=1, source_target_pairs={{0,16},{16,0},{1,17},{17,1},{2,18},{18,2},{3,19},{19,3},{4,20},{20... | collective-permute-start | bytes 3145736 | tf_op jit(solution)/shard_map/ppermute | solution.py:16
  492.2 37.3 %collective-permute-start.86 = (bf16[1024,512]{0,1:T(8,128)(2,1)S(1)}, bf16[1024,512]{0,1:T(8,128)(2,1)S(1)}, u32[]{:S(2)}, u32[]{:S(2)}) collective-permute-start(bf16[1024,512]{0,1:T(8,128)(2,1)S(1)} %add_convert_fusion.4), channel_id=1, source_target_pairs={{0,1},{1,2},{2,3},{3,0},{4,5},{5,6},{6,7},{7,4},{8,9},{9,10},{10,1... | collective-permute-start | bytes 3145736 | tf_op jit(solution)/shard_map/ppermute | solution.py:16
  512.6 36.3 %collective-permute-start.53 = (bf16[256,2048]{1,0:T(8,128)(2,1)S(1)}, bf16[256,2048]{1,0:T(8,128)(2,1)S(1)}, u32[]{:S(2)}, u32[]{:S(2)}) collective-permute-start(bf16[256,2048]{1,0:T(8,128)(2,1)S(1)} %add_convert_fusion.5), channel_id=1, source_target_pairs={{0,1},{1,2},{2,3},{3,0},{4,5},{5,6},{6,7},{7,4},{8,9},{9,10},{10,1... | collective-permute-start | bytes 3145736 | tf_op jit(solution)/shard_map/ppermute | solution.py:16
  529.2 84.2 %collective-permute-start.60 = (bf16[256,2048]{1,0:T(8,128)(2,1)}, bf16[256,2048]{1,0:T(8,128)(2,1)}, u32[]{:S(2)}, u32[]{:S(2)}) collective-permute-start(bf16[256,2048]{1,0:T(8,128)(2,1)} %get-tuple-element.209), channel_id=1, source_target_pairs={{0,16},{16,0},{1,17},{17,1},{2,18},{18,2},{3,19},{19,3},{4,20},{20... | collective-permute-start | bytes 3145736 | tf_op jit(solution)/shard_map/ppermute | solution.py:16
  535.1 44.6 %collective-permute-start.62 = (bf16[256,2048]{1,0:T(8,128)(2,1)}, bf16[256,2048]{1,0:T(8,128)(2,1)S(1)}, u32[]{:S(2)}, u32[]{:S(2)}) collective-permute-start(bf16[256,2048]{1,0:T(8,128)(2,1)} %get-tuple-element.226), channel_id=1, source_target_pairs={{0,16},{16,0},{1,17},{17,1},{2,18},{18,2},{3,19},{19,3},{4,20},{20... | collective-permute-start | bytes 3145736 | tf_op jit(solution)/shard_map/ppermute | solution.py:16
  551.7 57.8 %collective-permute-start.70 = (bf16[256,2048]{1,0:T(8,128)(2,1)}, bf16[256,2048]{1,0:T(8,128)(2,1)S(1)}, u32[]{:S(2)}, u32[]{:S(2)}) collective-permute-start(bf16[256,2048]{1,0:T(8,128)(2,1)} %add_convert_fusion.3), channel_id=1, source_target_pairs={{0,1},{1,2},{2,3},{3,0},{4,5},{5,6},{6,7},{7,4},{8,9},{9,10},{10,1... | collective-permute-start | bytes 3145736 | tf_op jit(solution)/shard_map/ppermute | solution.py:16
  613.4 42.3 %collective-permute-start.59 = (bf16[256,2048]{1,0:T(8,128)(2,1)}, bf16[256,2048]{1,0:T(8,128)(2,1)}, u32[]{:S(2)}, u32[]{:S(2)}) collective-permute-start(bf16[256,2048]{1,0:T(8,128)(2,1)} %slice.1079), channel_id=1, source_target_pairs={{0,8},{4,12},{8,0},{12,4},{1,9},{5,13},{9,1},{13,5},{2,10},{6,14},... | collective-permute-start | bytes 3145736 | tf_op jit(solution)/shard_map/ppermute | solution.py:21
  620.9 73.3 %collective-permute-start.97 = (f32[3,512]{1,0:T(4,128)S(1)}, f32[3,512]{1,0:T(4,128)}, u32[]{:S(2)}, u32[]{:S(2)}) collective-permute-start(f32[3,512]{1,0:T(4,128)S(1)} %fusion.195), channel_id=1, source_target_pairs={{0,2},{1,3},{2,0},{3,1},{4,6},{5,7},{6,4},{7,5},{8,10},{9,11},{10,... | collective-permute-start | bytes 18440 | tf_op jit(solution)/shard_map/ppermute | solution.py:21
  664.0 40.4 %collective-permute-start.82 = (bf16[3,256,512]{1,2,0:T(8,128)(2,1)}, bf16[3,256,512]{1,2,0:T(8,128)(2,1)}, u32[]{:S(2)}, u32[]{:S(2)}) collective-permute-start(bf16[3,256,512]{1,2,0:T(8,128)(2,1)} %get-tuple-element.251), channel_id=1, source_target_pairs={{0,16},{16,0},{1,17},{17,1},{2,18},{18,2},{3,19},{19,3},{4,20},{20... | collective-permute-start | bytes 2359304 | tf_op jit(solution)/shard_map/ppermute | solution.py:16
  720.3 36.1 %collective-permute-start.91 = (bf16[3,256,512]{1,2,0:T(8,128)(2,1)}, bf16[3,256,512]{1,2,0:T(8,128)(2,1)}, u32[]{:S(2)}, u32[]{:S(2)}) collective-permute-start(bf16[3,256,512]{1,2,0:T(8,128)(2,1)} %get-tuple-element.255), channel_id=1, source_target_pairs={{0,16},{16,0},{1,17},{17,1},{2,18},{18,2},{3,19},{19,3},{4,20},{20... | collective-permute-start | bytes 2359304 | tf_op jit(solution)/shard_map/ppermute | solution.py:16
  (199 other events, 3858.1 us)
